TPU v7x, 256 devices: a whole 4x4x8 slice. The times are simulated.
256 devices in a mesh: tm: 32 (over z_hi, y, core), chan: 8 (over x, z_lo).
Axes of the slice: x: 4, y: 4, z: 8 (z_hi: 4, z_lo: 2; z = z_hi * 2 + z_lo), core: 2. Of those that a mesh axis runs over, the one named last changes fastest.
Arguments:
- clip_input: bfloat16 [512, 64, 256], P('chan', 'tm'), may hold values from -16 to 16, as said below
- lengths: int32 [16], replicated, may hold values from 1 to 16, 64 in all
- gamma_one: float32 [512], P('chan'), may hold values from 0.25 to 1.75
- beta_one: float32 [512], P('chan'), may hold values from -1.5 to 1.5
- w_one: bfloat16 [512, 27, 512], P('chan'), may hold values from -0.0546875 to 0.0546875
- bias_one: float32 [512], P('chan'), may hold values from -1.5 to 1.5
- gamma_two: float32 [512], P('chan'), may hold values from 0.25 to 1.75
- beta_two: float32 [512], P('chan'), may hold values from -1.5 to 1.5
- w_two: bfloat16 [512, 27, 512], P('chan'), may hold values from -0.0546875 to 0.0546875
- bias_two: float32 [512], P('chan'), may hold values from -1.5 to 1.5
Outputs:
- block_output: float32 [512, 64, 256], P('chan', 'tm')
Inputs may be any that keep to these rules, and one draw needn't show every extreme that they name: `clip_input`: activations of order one. `lengths`: the 16 counts sum to 64; the longest is exactly 16.
All inputs are finite; a program needn't handle non-finite values.
Results may differ from a plain program's by a relative error of at most 0.0054.
Values may be sent and summed in bfloat16 or wider, within the bound.
No kernel may reach another device: no remote copies, remote signals or barrier semaphores. Data moves between devices by JAX's collectives and lax.ppermute only.
A program may use at most 128 MiB of HBM per device.

v0:
```python
import jax
import jax.numpy as jnp
from jax import lax
from jax.sharding import PartitionSpec as P

C = 512
GROUPS = 32
H = 16
W = 16


EPS = 1e-06


def shifted(value, axis, steps):
    count = lax.axis_size(axis)
    first, last = (max(0, -steps), min(count, count - steps))
    return lax.ppermute(value, axis, [(source, source + steps) for source in range(first, last)])


def clip_member(frames, ends, nclips):
    clips = jnp.sum((frames[:, None] >= ends[None, :]).astype(jnp.int32), axis=1)
    member = (clips[:, None] == jnp.arange(nclips, dtype=jnp.int32)[None, :]).astype(jnp.int32)
    return member


def local_sums(data, member):
    chans, frames, cells = data.shape
    group_size = C // GROUPS
    grouped = data.reshape(chans // group_size, group_size, frames, cells)
    sums = jnp.sum(grouped, axis=(1, 3))
    squares = jnp.sum(grouped * grouped, axis=(1, 3))
    weights = member.astype(jnp.float32)
    return (
        jnp.dot(sums, weights, precision=lax.Precision.HIGHEST),
        jnp.dot(squares, weights, precision=lax.Precision.HIGHEST),
    )


def apply_norm(data, mean, scale, member, gamma, beta):
    chans, frames, cells = data.shape
    group_size = C // GROUPS
    weights = member.astype(jnp.float32)
    mean_f = jnp.dot(mean, weights.T, precision=lax.Precision.HIGHEST)
    scale_f = jnp.dot(scale, weights.T, precision=lax.Precision.HIGHEST)
    grouped = data.reshape(chans // group_size, group_size, frames, cells)
    normed = (grouped - mean_f[:, None, :, None]) * scale_f[:, None, :, None]
    normed = normed.reshape(chans, frames, cells) * gamma[:, None, None] + beta[:, None, None]
    return jax.nn.silu(normed).astype(jnp.bfloat16)


def conv_taps(weight_rows, extended, keep):
    rows, span, cells = extended.shape
    count = span - 2
    padded = jnp.pad(extended.reshape(rows, span, H, W), ((0, 0), (0, 0), (1, 1), (1, 1)))
    total = None
    for kt in range(3):
        for kh in range(3):
            for kw in range(3):
                piece = (
                    padded[:, kt : kt + count, kh : kh + H, kw : kw + W]
                    * keep[kt][None, :, None, None]
                )
                term = lax.dot_general(
                    weight_rows[:, 9 * kt + 3 * kh + kw, :],
                    piece.reshape(rows, count * H * W),
                    (((0,), (0,)), ((), ())),
                    preferred_element_type=jnp.float32,
                )
                total = term if total is None else total + term
    return total


def block_layer(raw, gamma, beta, weight, bias, own_member, counts, keep):
    chans, frames, cells = raw.shape
    data = raw.astype(jnp.float32)
    sums, squares = lax.psum(local_sums(data, own_member), "tm")
    mean = sums / counts[None, :]
    var = squares / counts[None, :] - mean * mean
    scale = lax.rsqrt(var + EPS)
    hidden = apply_norm(data, mean, scale, own_member, gamma, beta)
    tail = shifted(hidden, "tm", 1)
    extended = jnp.concatenate([tail, hidden], axis=1)
    summed = lax.psum(conv_taps(weight, extended, keep), "chan")
    own = lax.dynamic_slice_in_dim(summed, lax.axis_index("chan") * chans, chans, 0)
    return own.reshape(chans, frames, cells) + bias[:, None, None]


def on_device(
    clip_input, lengths, gamma_one, beta_one, w_one, bias_one, gamma_two, beta_two, w_two, bias_two
):
    chans, frames, cells = clip_input.shape
    nclips = lengths.shape[0]
    ends = jnp.cumsum(lengths)
    starts = ends - lengths
    first_frame = lax.axis_index("tm") * frames
    own_frames = first_frame + jnp.arange(frames, dtype=jnp.int32)
    own_member = clip_member(own_frames, ends, nclips)
    clip_start = jnp.sum(own_member * starts[None, :], axis=1)
    keep = jnp.stack([own_frames - 2 + kt >= clip_start for kt in range(3)], axis=0).astype(
        jnp.bfloat16
    )
    counts = lengths.astype(jnp.float32) * float(C // GROUPS * H * W)
    y_one = block_layer(clip_input, gamma_one, beta_one, w_one, bias_one, own_member, counts, keep)
    y_one = y_one.astype(jnp.bfloat16)
    y_two = block_layer(y_one, gamma_two, beta_two, w_two, bias_two, own_member, counts, keep)
    return clip_input.astype(jnp.float32) + y_two


def solution(mesh):
    in_specs = (
        P("chan", "tm", None),
        P(),
        P("chan"),
        P("chan"),
        P("chan", None, None),
        P("chan"),
        P("chan"),
        P("chan"),
        P("chan", None, None),
        P("chan"),
    )
    out_specs = P("chan", "tm", None)
    return jax.shard_map(
        on_device, mesh=mesh, in_specs=in_specs, out_specs=out_specs, check_vma=False
    )
```

profile of v0, /device:TPU:1, one launch (start us, length us, event | category | flops | bytes accessed | tf_op | source)
XLA Modules:
  0.0 370.4 jit_solution(17842196471965252192)
XLA Ops:
  6.5 0.7 convert_multiply_fusion.2
  7.2 0.7 copy.41
  8.1 0.9 convert_reduce_fusion
  10.0 73.7 %all-reduce.3 = (f32[4,16]{1,0:T(4,128)S(1)}, f32[4,16]{1,0:T(4,128)S(1)}) all-reduce(f32[4,16]{1,0:T(4,128)S(1)} %fusion.210, f32[4,16]{1,0:T(4,128)S(1)} %fusion.214), channel_id=1, replica_groups=mesh['tm'=32,'chan'=8] {'tm'}, use_global_device_ids=true, to_apply=%region_7.8 | all-reduce | flops 128 | bytes 1024 | tf_op jit(solution)/shard_map/psum | solution.py:77
  84.3 1.1 fusion.31
  85.4 3.0 collective-permute-start
  88.3 0.7 sub.46
  89.2 4.1 %collective-permute-done = bf16[64,2,256]{2,0,1:T(8,128)(2,1)S(1)} collective-permute-done((bf16[64,2,256]{2,0,1:T(8,128)(2,1)S(1)}, bf16[64,2,256]{2,0,1:T(8,128)(2,1)S(1)}, u32[]{:S(2)}, u32[]{:S(2)}) %collective-permute-start) | collective-permute-done | bytes 65568 | tf_op jit(solution)/shard_map/ppermute | solution.py:18
  94.3 1.0 copy-done
  95.2 0.3 fusion.135
  95.5 0.3 convolution_add_fusion.31
  102.0 0.3 fusion.12
  102.3 1.3 fusion.11
  103.8 82.5 %all-reduce.7.cloned.1.call-done = f32[512,512]{0,1:T(8,128)} async-done(((f32[512,512]{0,1:T(8,128)}), f32[512,512]{0,1:T(8,128)}) %all-reduce.7.cloned.1.call-update) | async-done | bytes 1048592 | tf_op jit(solution)/shard_map/psum | solution.py:84
  186.4 1.1 constant_dynamic-slice_fusion.1
  188.3 74.3 %all-reduce.2 = (f32[4,16]{1,0:T(4,128)S(1)}, f32[4,16]{1,0:T(4,128)S(1)}) all-reduce(f32[4,16]{1,0:T(4,128)S(1)} %fusion.203, f32[4,16]{1,0:T(4,128)S(1)} %fusion.207), channel_id=1, replica_groups=mesh['tm'=32,'chan'=8] {'tm'}, use_global_device_ids=true, to_apply=%region_13.14 | all-reduce | flops 128 | bytes 1024 | tf_op jit(solution)/shard_map/psum | solution.py:77
  263.6 2.1 collective-permute-start.1
  265.7 1.1 collective-permute-done.1
  267.8 1.0 copy-done.1
  269.1 0.3 convolution_add_fusion.15
  275.9 1.3 fusion
  277.2 84.3 %all-reduce.9.cloned.1.call-done = f32[512,512]{0,1:T(8,128)} async-done(((f32[512,512]{0,1:T(8,128)}), f32[512,512]{0,1:T(8,128)}) %all-reduce.9.cloned.1.call-update) | async-done | bytes 1048592 | tf_op jit(solution)/shard_map/psum | solution.py:84
  361.5 1.1 constant_dynamic-slice_fusion
  362.8 0.8 copy.49
  (110 shorter events, 18.8 us)
Async XLA Ops:
  6.5 179.8 %all-reduce.7.cloned.1.call-start = ((), (), s32[]{:S(2)}) async-start(), calls=%async_computation | async-start | bytes 2097152 | tf_op jit(solution)/shard_map/psum | solution.py:84
  85.4 7.9 %collective-permute-start = (bf16[64,2,256]{2,0,1:T(8,128)(2,1)S(1)}, bf16[64,2,256]{2,0,1:T(8,128)(2,1)S(1)}, u32[]{:S(2)}, u32[]{:S(2)}) collective-permute-start(bf16[64,2,256]{2,0,1:T(8,128)(2,1)S(1)} %fusion.31), channel_id=1, source_target_pairs={{0,8},{8,16},{16,24},{24,32},{32,40},{40,48},{48,56},{56,64},{64,7... | collective-permute-start | bytes 196616 | tf_op jit(solution)/shard_map/ppermute | solution.py:18
  93.8 1.5 copy-start
  102.3 1.4 copy-start.3
  103.6 159.8 %copy-start.4 = (f32[64]{0:T(128)S(1)}, f32[64]{0:T(128)}, u32[]{:S(2)}) copy-start(f32[64]{0:T(128)} %param.17) | copy-start | bytes 772
  103.6 159.8 %copy-start.5 = (f32[64]{0:T(128)S(1)}, f32[64]{0:T(128)}, u32[]{:S(2)}) copy-start(f32[64]{0:T(128)} %param.16) | copy-start | bytes 772
  103.7 257.9 %all-reduce.9.cloned.1.call-start = ((), (), s32[]{:S(2)}) async-start(), calls=%async_computation.1 | async-start | bytes 2097152 | tf_op jit(solution)/shard_map/psum | solution.py:84
  263.6 3.2 collective-permute-start.1
  267.3 1.5 copy-start.1
  275.9 86.9 %copy-start.2 = (bf16[64,2,256]{2,1,0:T(2,128)(2,1)S(1)}, bf16[64,2,256]{2,1,0:T(2,128)(2,1)}, u32[]{:S(2)}) copy-start(bf16[64,2,256]{2,1,0:T(2,128)(2,1)} %param.10) | copy-start | bytes 196612
  275.9 86.9 %copy-start.6 = (f32[64]{0:T(128)S(1)}, f32[64]{0:T(128)}, u32[]{:S(2)}) copy-start(f32[64]{0:T(128)} %param.19) | copy-start | bytes 772
Sparse Core Ops, SparseCore 0:
  103.8 82.5 all-reduce.6
  277.3 84.1 all-reduce.8
where the time goes:
time: 374 us; the launch traced here: 370 us
  waiting for transfers between devices  172 us (46%)
  blocking collectives  148 us (40%)
  matrix products  18 us (5%)
  between operations  14 us (4%)
  local copies, waits for them, and re-layouts  7.26 us (2%)
  other arithmetic  6.07 us (2%)
  starting transfers between devices  5.11 us (1%)
    psum x2, waiting for transfers between devices, block_layer(): summed = lax.psum(conv_taps(weight, extended, keep), 'chan')  167 us
    psum x2, blocking collectives, block_layer(): sums, squares = lax.psum(local_sums(data, own_member), 'tm')  148 us
    dot_general x54, matrix products, conv_taps(): lax.dot_general(weight_rows[:, 9 * kt + 3 * kh + kw, :], piece.reshape(ro...  16.4 us
  transfers between devices with their start and end apart: 4, of which 4 were waited for; matrix products, arithmetic and copies ran while one was open for 0% of the time, Pallas kernels for 0%

commit v1 on v0

v1 whole, which is shorter than its diff:
```python
import jax
import jax.numpy as jnp
from jax import lax
from jax.sharding import PartitionSpec as P

C = 512
GROUPS = 32
H = 16
W = 16
EPS = 1e-06
GROUP_SIZE = C // GROUPS


def ring_shift(value, axis, steps):
    count = lax.axis_size(axis)
    return lax.ppermute(value, axis, [(source, (source + steps) % count) for source in range(count)])


def frame_sums(data):
    chans, frames, cells = data.shape
    grouped = data.reshape(chans // GROUP_SIZE, GROUP_SIZE, frames, cells)
    sums = jnp.sum(grouped, axis=(1, 3))
    squares = jnp.sum(grouped * grouped, axis=(1, 3))
    return jnp.stack([sums, squares], axis=0)


def share_over_clips(stats):
    count = lax.axis_size("tm")
    width = stats.size
    sent = jnp.broadcast_to(stats.reshape(1, width), (count, width))
    got = lax.all_to_all(sent, "tm", 0, 0, tiled=True)
    return jnp.moveaxis(got.reshape((count,) + stats.shape), 0, 2)


def conv_taps(weight_rows, extended, keep):
    rows, span, cells = extended.shape
    count = span - 2
    padded = jnp.pad(extended.reshape(rows, span, H, W), ((0, 0), (0, 0), (1, 1), (1, 1)))
    total = None
    for kt in range(3):
        for kh in range(3):
            for kw in range(3):
                piece = (
                    padded[:, kt : kt + count, kh : kh + H, kw : kw + W]
                    * keep[kt][None, :, None, None]
                )
                term = lax.dot_general(
                    weight_rows[:, 9 * kt + 3 * kh + kw, :],
                    piece.reshape(rows, count * H * W),
                    (((0,), (0,)), ((), ())),
                    preferred_element_type=jnp.float32,
                )
                total = term if total is None else total + term
    return total


def block_layer(raw, gamma, beta, weight, bias, same_clip, counts, keep):
    chans, frames, cells = raw.shape
    tail = ring_shift(raw, "tm", 1)
    stats = share_over_clips(frame_sums(raw.astype(jnp.float32)))
    stats = stats.reshape(2, chans // GROUP_SIZE, -1)
    clip = jnp.sum(stats[:, :, None, :] * same_clip[None, None], axis=3) / counts[None, None, :]
    mean = clip[0]
    scale = lax.rsqrt(clip[1] - mean * mean + EPS)
    mean = jnp.repeat(jnp.concatenate([mean[:, :1], mean[:, :1], mean], axis=1), GROUP_SIZE, axis=0)
    scale = jnp.repeat(jnp.concatenate([scale[:, :1], scale[:, :1], scale], axis=1), GROUP_SIZE, axis=0)
    data = jnp.concatenate([tail, raw], axis=1).astype(jnp.float32)
    normed = (data - mean[:, :, None]) * (scale * gamma[:, None])[:, :, None] + beta[:, None, None]
    extended = jax.nn.silu(normed).astype(jnp.bfloat16)
    partial = conv_taps(weight, extended, keep).astype(jnp.bfloat16)
    got = lax.all_to_all(partial, "chan", 0, 0, tiled=True)
    summed = jnp.sum(got.reshape(-1, chans, frames, cells).astype(jnp.float32), axis=0)
    return summed + bias[:, None, None]


def on_device(
    clip_input, lengths, gamma_one, beta_one, w_one, bias_one, gamma_two, beta_two, w_two, bias_two
):
    chans, frames, cells = clip_input.shape
    all_frames = frames * lax.axis_size("tm")
    ends = jnp.cumsum(lengths)
    starts = ends - lengths
    own = lax.axis_index("tm") * frames + jnp.arange(frames, dtype=jnp.int32)
    inside = ((own[:, None] >= starts[None, :]) & (own[:, None] < ends[None, :])).astype(jnp.int32)
    start = jnp.sum(inside * starts[None, :], axis=1)
    end = jnp.sum(inside * ends[None, :], axis=1)
    every = jnp.arange(all_frames, dtype=jnp.int32)
    same_clip = ((every[None, :] >= start[:, None]) & (every[None, :] < end[:, None])).astype(jnp.float32)
    counts = (end - start).astype(jnp.float32) * float(GROUP_SIZE * H * W)
    keep = jnp.stack([own - 2 + kt >= start for kt in range(3)], axis=0).astype(jnp.bfloat16)
    y_one = block_layer(clip_input, gamma_one, beta_one, w_one, bias_one, same_clip, counts, keep)
    y_one = y_one.astype(jnp.bfloat16)
    y_two = block_layer(y_one, gamma_two, beta_two, w_two, bias_two, same_clip, counts, keep)
    return clip_input.astype(jnp.float32) + y_two


def solution(mesh):
    in_specs = (
        P("chan", "tm", None),
        P(),
        P("chan"),
        P("chan"),
        P("chan", None, None),
        P("chan"),
        P("chan"),
        P("chan"),
        P("chan", None, None),
        P("chan"),
    )
    out_specs = P("chan", "tm", None)
    return jax.shard_map(
        on_device, mesh=mesh, in_specs=in_specs, out_specs=out_specs, check_vma=False
    )
```

time: 374 us -> 94.4 us (0.25)
  waiting for transfers between devices: 172 us -> 12.2 us
  blocking collectives: 148 us -> 25.1 us
  starting transfers between devices: 5.11 us -> 23.7 us
  between operations: 14 us -> 0.71 us
    psum x2 -> x0, waiting for transfers between devices: 167 us -> none  [block_layer(): summed = lax.psum(conv_taps(weight, extended, keep), 'chan')]
    psum x2 -> x0, blocking collectives: 148 us -> none  [block_layer(): sums, squares = lax.psum(local_sums(data, own_member), 'tm')]
    all_to_all x0 -> x2, blocking collectives: none -> 25.1 us  [block_layer(): got = lax.all_to_all(partial, 'chan', 0, 0, tiled=True)]
    all_to_all x0 -> x2, starting transfers between devices: none -> 20.1 us  [share_over_clips(): got = lax.all_to_all(sent, 'tm', 0, 0, tiled=True)]
    all_to_all x0 -> x2, waiting for transfers between devices: none -> 12.2 us  [share_over_clips(): got = lax.all_to_all(sent, 'tm', 0, 0, tiled=True)]
    ppermute x2, waiting for transfers between devices: 5.2 us -> 0.01 us  [ring_shift(): lax.ppermute(value, axis, [(source, (source + steps) % count) for source...]
  transfers between devices with their start and end apart: 4 -> 4, of which waited for: 4 -> 2; matrix products, arithmetic and copies ran while one was open for 0% -> 5% of each run, Pallas kernels for 0% -> 0%
where the time goes in v1:
time: 94.4 us; the launch traced here: 94 us
  blocking collectives  25.1 us (27%)
  starting transfers between devices  23.7 us (25%)
  matrix products  18.3 us (19%)
  waiting for transfers between devices  12.2 us (13%)
  local copies, waits for them, and re-layouts  7.03 us (7%)
  other arithmetic  7 us (7%)
    all_to_all x2, blocking collectives, block_layer(): got = lax.all_to_all(partial, 'chan', 0, 0, tiled=True)  25.1 us
    all_to_all x2, starting transfers between devices, share_over_clips(): got = lax.all_to_all(sent, 'tm', 0, 0, tiled=True)  20.1 us
    dot_general x54, matrix products, conv_taps(): lax.dot_general(weight_rows[:, 9 * kt + 3 * kh + kw, :], piece.reshape(ro...  18.3 us
    all_to_all x2, waiting for transfers between devices, share_over_clips(): got = lax.all_to_all(sent, 'tm', 0, 0, tiled=True)  12.2 us
    ppermute x2, starting transfers between devices, ring_shift(): lax.ppermute(value, axis, [(source, (source + steps) % count) for source...  3.6 us
    unnamed x17, local copies, waits for them, and re-layouts  3.1 us
  transfers between devices with their start and end apart: 4, of which 2 were waited for; matrix products, arithmetic and copies ran while one was open for 5% of the time, Pallas kernels for 0%

profile of v1, /device:TPU:1, one launch (start us, length us, event | category | flops | bytes accessed | tf_op | source)
XLA Modules:
  0.0 94.0 jit_solution(14562295817440273027)
XLA Ops:
  0.0 1.1 %convert_reduce_fusion.3 = (f32[64,2]{1,0:T(8,128)S(1)}, f32[64,2]{1,0:T(8,128)S(1)}) fusion(bf16[64,2,256]{2,1,0:T(2,128)(2,1)} %param.10), kind=kLoop, calls=%fused_computation.135 | loop fusion | flops 130816 | bytes 66560 | tf_op jit(solution)/shard_map/reduce_sum | solution.py:22
  1.5 0.6 broadcast_in_dim.17
  2.1 12.8 %all-to-all-start = ((f32[32,1,16]{2,1,0:T(1,128)}), f32[32,1,16]{2,1,0:T(1,128)S(1)}, u32[]{:S(2)}, u32[]{:S(2)}) async-start(f32[32,1,16]{2,1,0:T(1,128)} %broadcast_in_dim.17), calls=%async_computation | async-start | bytes 32768 | tf_op jit(solution)/shard_map/all_to_all | solution.py:31
  14.9 1.0 %copy.42 = bf16[64,2,256]{0,2,1:T(8,128)(2,1)S(1)} copy(bf16[64,2,256]{2,1,0:T(2,128)(2,1)} %param.10) | data formatting | bytes 131072 | tf_op args[0]
  15.8 1.7 %collective-permute-start = (bf16[64,2,256]{0,2,1:T(8,128)(2,1)S(1)}, bf16[64,2,256]{0,2,1:T(8,128)(2,1)S(1)}, u32[]{:S(2)}, u32[]{:S(2)}) collective-permute-start(bf16[64,2,256]{0,2,1:T(8,128)(2,1)S(1)} %copy.42), channel_id=1, source_target_pairs={{0,8},{8,16},{16,24},{24,32},{32,40},{40,48},{48,56},{56,64},{64,7... | collective-permute-start | bytes 196616 | tf_op jit(solution)/shard_map/ppermute | solution.py:16
  17.5 0.7 copy.50
  18.4 0.7 sub.43
  19.4 4.8 %all-to-all-done = f32[32,1,16]{2,1,0:T(1,128)S(1)} async-done(((f32[32,1,16]{2,1,0:T(1,128)}), f32[32,1,16]{2,1,0:T(1,128)S(1)}, u32[]{:S(2)}, u32[]{:S(2)}) %all-to-all-start) | async-done | bytes 2080 | tf_op jit(solution)/shard_map/all_to_all | solution.py:31
  24.8 0.7 broadcast_multiply_fusion.1
  25.7 0.9 multiply_convert_fusion.1
  27.3 1.0 %copy-done = bf16[64,27,512]{2,0,1:T(8,128)(2,1)S(1)} copy-done((bf16[64,27,512]{2,0,1:T(8,128)(2,1)S(1)}, bf16[64,27,512]{2,0,1:T(8,128)(2,1)}, u32[]{:S(2)}) %copy-start) | copy-done | bytes 1769496
  29.3 0.3 convolution_add_fusion.29
  32.4 0.3 convolution_add_fusion.20
  35.5 0.3 fusion.16
  37.6 13.5 %all_to_all.30 = bf16[8,64,512]{2,1,0:T(8,128)(2,1)S(1)} all-to-all(bf16[8,64,512]{2,1,0:T(8,128)(2,1)S(1)} %bitcast.430), channel_id=1, replica_groups=mesh['tm'=32,'chan'=8] {'chan'}, dimensions={0} | all-to-all | bytes 1048576 | tf_op jit(solution)/shard_map/all_to_all | solution.py:71
  51.9 0.6 broadcast_in_dim.21
  52.6 7.4 %all-to-all-start.2 = ((f32[32,1,16]{2,1,0:T(1,128)}), f32[32,1,16]{2,1,0:T(1,128)S(1)}, u32[]{:S(2)}, u32[]{:S(2)}) async-start(f32[32,1,16]{2,1,0:T(1,128)} %broadcast_in_dim.21), calls=%async_computation.2 | async-start | bytes 32768 | tf_op jit(solution)/shard_map/all_to_all | solution.py:31
  60.0 1.9 %collective-permute-start.1 = (bf16[64,2,256]{0,2,1:T(8,128)(2,1)S(1)}, bf16[64,2,256]{0,2,1:T(8,128)(2,1)S(1)}, u32[]{:S(2)}, u32[]{:S(2)}) collective-permute-start(bf16[64,2,256]{0,2,1:T(8,128)(2,1)S(1)} %get-tuple-element.11), channel_id=1, source_target_pairs={{0,8},{8,16},{16,24},{24,32},{32,40},{40,48},{48,56},{56,64},{64,7... | collective-permute-start | bytes 196616 | tf_op jit(solution)/shard_map/ppermute | solution.py:16
  61.9 7.4 %all-to-all-done.2 = f32[32,1,16]{2,1,0:T(1,128)S(1)} async-done(((f32[32,1,16]{2,1,0:T(1,128)}), f32[32,1,16]{2,1,0:T(1,128)S(1)}, u32[]{:S(2)}, u32[]{:S(2)}) %all-to-all-start.2) | async-done | bytes 2080 | tf_op jit(solution)/shard_map/all_to_all | solution.py:31
  71.1 1.0 %copy-done.1 = bf16[64,27,512]{2,0,1:T(8,128)(2,1)S(1)} copy-done((bf16[64,27,512]{2,0,1:T(8,128)(2,1)S(1)}, bf16[64,27,512]{2,0,1:T(8,128)(2,1)}, u32[]{:S(2)}) %copy-start.1) | copy-done | bytes 1769496
  75.2 0.3 convolution_add_fusion.7
  78.3 0.3 fusion.8
  81.4 11.6 %all_to_all.31 = bf16[8,64,512]{2,1,0:T(8,128)(2,1)S(1)} all-to-all(bf16[8,64,512]{2,1,0:T(8,128)(2,1)S(1)} %bitcast.431), channel_id=1, replica_groups=mesh['tm'=32,'chan'=8] {'chan'}, dimensions={0} | all-to-all | bytes 1048576 | tf_op jit(solution)/shard_map/all_to_all | solution.py:71
  93.2 0.8 convert_add_fusion
  (129 shorter events, 21.7 us)
Async XLA Ops:
  2.1 22.1 %all-to-all-start = ((f32[32,1,16]{2,1,0:T(1,128)}), f32[32,1,16]{2,1,0:T(1,128)S(1)}, u32[]{:S(2)}, u32[]{:S(2)}) async-start(f32[32,1,16]{2,1,0:T(1,128)} %broadcast_in_dim.17), calls=%async_computation | async-start | bytes 32768 | tf_op jit(solution)/shard_map/all_to_all | solution.py:31
  15.8 9.8 %collective-permute-start = (bf16[64,2,256]{0,2,1:T(8,128)(2,1)S(1)}, bf16[64,2,256]{0,2,1:T(8,128)(2,1)S(1)}, u32[]{:S(2)}, u32[]{:S(2)}) collective-permute-start(bf16[64,2,256]{0,2,1:T(8,128)(2,1)S(1)} %copy.42), channel_id=1, source_target_pairs={{0,8},{8,16},{16,24},{24,32},{32,40},{40,48},{48,56},{56,64},{64,7... | collective-permute-start | bytes 196616 | tf_op jit(solution)/shard_map/ppermute | solution.py:16
  26.8 1.5 %copy-start = (bf16[64,27,512]{2,0,1:T(8,128)(2,1)S(1)}, bf16[64,27,512]{2,0,1:T(8,128)(2,1)}, u32[]{:S(2)}) copy-start(bf16[64,27,512]{2,0,1:T(8,128)(2,1)} %param.14) | copy-start | bytes 5308420
  37.2 14.1 %copy-start.3 = (f32[64]{0:T(128)S(1)}, f32[64]{0:T(128)}, u32[]{:S(2)}) copy-start(f32[64]{0:T(128)} %param.15) | copy-start | bytes 772
  37.6 32.3 %copy-start.6 = (f32[64]{0:T(128)S(1)}, f32[64]{0:T(128)}, u32[]{:S(2)}) copy-start(f32[64]{0:T(128)} %param.16) | copy-start | bytes 772
  37.6 32.5 %copy-start.4 = (f32[64]{0:T(128)S(1)}, f32[64]{0:T(128)}, u32[]{:S(2)}) copy-start(f32[64]{0:T(128)} %param.17) | copy-start | bytes 772
  52.6 16.7 %all-to-all-start.2 = ((f32[32,1,16]{2,1,0:T(1,128)}), f32[32,1,16]{2,1,0:T(1,128)S(1)}, u32[]{:S(2)}, u32[]{:S(2)}) async-start(f32[32,1,16]{2,1,0:T(1,128)} %broadcast_in_dim.21), calls=%async_computation.2 | async-start | bytes 32768 | tf_op jit(solution)/shard_map/all_to_all | solution.py:31
  60.0 10.1 %collective-permute-start.1 = (bf16[64,2,256]{0,2,1:T(8,128)(2,1)S(1)}, bf16[64,2,256]{0,2,1:T(8,128)(2,1)S(1)}, u32[]{:S(2)}, u32[]{:S(2)}) collective-permute-start(bf16[64,2,256]{0,2,1:T(8,128)(2,1)S(1)} %get-tuple-element.11), channel_id=1, source_target_pairs={{0,8},{8,16},{16,24},{24,32},{32,40},{40,48},{48,56},{56,64},{64,7... | collective-permute-start | bytes 196616 | tf_op jit(solution)/shard_map/ppermute | solution.py:16
  70.6 1.5 %copy-start.1 = (bf16[64,27,512]{2,0,1:T(8,128)(2,1)S(1)}, bf16[64,27,512]{2,0,1:T(8,128)(2,1)}, u32[]{:S(2)}) copy-start(bf16[64,27,512]{2,0,1:T(8,128)(2,1)} %param.18) | copy-start | bytes 5308420
  81.0 12.1 %copy-start.2 = (bf16[64,2,256]{2,1,0:T(2,128)(2,1)S(1)}, bf16[64,2,256]{2,1,0:T(2,128)(2,1)}, u32[]{:S(2)}) copy-start(bf16[64,2,256]{2,1,0:T(2,128)(2,1)} %param.10) | copy-start | bytes 196612
  81.1 12.1 %copy-start.5 = (f32[64]{0:T(128)S(1)}, f32[64]{0:T(128)}, u32[]{:S(2)}) copy-start(f32[64]{0:T(128)} %param.19) | copy-start | bytes 772

commit v2 on v1

v2 whole, which is shorter than its diff:
```python
import jax
import jax.numpy as jnp
from jax import lax
from jax.experimental import pallas as pl
from jax.experimental.pallas import tpu as pltpu
from jax.sharding import PartitionSpec as P

C = 512
GROUPS = 32
H = 16
W = 16
EPS = 1e-06
GROUP_SIZE = C // GROUPS
CELLS = H * W
CHANS = 64
LANES = 2 * CHANS
TAPS = 27
ROWS = TAPS * CHANS
DEPTH = (TAPS + 1) * CHANS
SLOT = CELLS + 2 * W

VMEM = pl.BlockSpec(memory_space=pltpu.VMEM)
SMEM = pl.BlockSpec(memory_space=pltpu.SMEM)
ANY = pl.BlockSpec(memory_space=pl.ANY)


def ring_shift(value, axis, steps):
    count = lax.axis_size(axis)
    return lax.ppermute(value, axis, [(source, (source + steps) % count) for source in range(count)])


def left_half(shape):
    return lax.broadcasted_iota(jnp.int32, shape, len(shape) - 1) < CHANS


def write_sums(values, sums_ref):
    total = jnp.sum(values, axis=0, keepdims=True)
    squares = jnp.sum(values * values, axis=0, keepdims=True)
    row = lax.broadcasted_iota(jnp.int32, (8, LANES), 0)
    tile = jnp.where(row == 0, total, jnp.where(row == 1, squares, 0.0))
    sums_ref[...] = jnp.broadcast_to(tile[None], sums_ref.shape)


def both_halves(row):
    return jnp.concatenate([row, row], axis=1)


def pack_kernel(x_ref, packed_ref, sums_ref):
    rows = jnp.concatenate([x_ref[:, 0, :], x_ref[:, 1, :]], axis=0).astype(jnp.float32)
    values = rows.T
    packed_ref[...] = values.astype(jnp.bfloat16)
    write_sums(values, sums_ref)


def group_totals(rows):
    lane = lax.broadcasted_iota(jnp.int32, rows.shape, 1)
    rows = rows + pltpu.roll(rows, CHANS, 1)
    step = 1
    while step < GROUP_SIZE:
        other = jnp.where(
            (lane & step) == 0, pltpu.roll(rows, LANES - step, 1), pltpu.roll(rows, step, 1)
        )
        rows = rows + other
        step *= 2
    return rows


def clip_bounds(lengths_ref, frame):
    total = jnp.int32(0)
    start = jnp.int32(0)
    end = jnp.int32(0)
    for k in range(lengths_ref.shape[0]):
        after = total + lengths_ref[k]
        inside = (frame >= total) & (frame < after)
        start = jnp.where(inside, total, start)
        end = jnp.where(inside, after, end)
        total = after
    return start, end


def conv_kernel(
    lengths_ref, first_ref, sums_ref, own_ref, tail_ref, gamma_ref, beta_ref, w_hbm, out_ref,
    w_ref, slots_ref, cols_ref, sem,
):
    load = pltpu.make_async_copy(w_hbm, w_ref.at[pl.ds(0, ROWS), :], sem)
    load.start()
    w_ref[ROWS:, :] = jnp.zeros((DEPTH - ROWS, C), jnp.bfloat16)

    frame = first_ref[0]
    bounds = [clip_bounds(lengths_ref, frame), clip_bounds(lengths_ref, frame + 1)]
    count = sums_ref.shape[0]
    device = lax.broadcasted_iota(jnp.int32, (count, 1, LANES), 0)
    half = (lax.broadcasted_iota(jnp.int32, (count, 1, LANES), 2) >= CHANS).astype(jnp.int32)
    frame_of = 2 * device + half
    sums = sums_ref[...]
    stats = []
    for start, end in bounds:
        inside = (frame_of >= start) & (frame_of < end)
        per_lane = jnp.sum(jnp.where(inside, sums, 0.0), axis=0)
        totals = group_totals(per_lane)
        size = ((end - start) * (GROUP_SIZE * CELLS)).astype(jnp.float32)
        totals = totals / size
        mean = totals[0:1, :]
        var = totals[1:2, :] - mean * mean
        stats.append((mean, lax.rsqrt(var + EPS)))
    gamma = both_halves(gamma_ref[...])
    beta = both_halves(beta_ref[...])
    left_row = left_half((1, LANES))
    mean_tail, scale_tail = stats[0]
    mean_own = jnp.where(left_row, stats[0][0], stats[1][0])
    scale_own = jnp.where(left_row, stats[0][1], stats[1][1])

    def normed(ref, mean, scale):
        u = (ref[...].astype(jnp.float32) - mean) * scale * gamma + beta
        return u / (1.0 + jnp.exp(-u))

    left = left_half((CELLS, LANES))

    def split(packed):
        turned = pltpu.roll(packed, CHANS, 1)
        return jnp.where(left, packed, turned), jnp.where(left, turned, packed)

    before_two, before_one = split(normed(tail_ref, mean_tail, scale_tail))
    own_zero, own_one = split(normed(own_ref, mean_own, scale_own))
    start_zero, start_one = bounds[0][0], bounds[1][0]
    column = lax.broadcasted_iota(jnp.int32, (CELLS, LANES), 0) % W
    margin = jnp.zeros((W, LANES), jnp.bfloat16)

    def place(kw, slot, value):
        slots_ref[kw, slot, 0:W, :] = margin
        slots_ref[kw, slot, W : W + CELLS, :] = value
        slots_ref[kw, slot, W + CELLS :, :] = margin

    uses = (
        (before_two, ((0, frame - 2 >= start_zero),)),
        (before_one, ((1, frame - 1 >= start_zero), (3, frame - 1 >= start_one))),
        (own_zero, ((2, None), (4, frame >= start_one))),
        (own_one, ((5, None),)),
    )
    for value, targets in uses:
        views = (
            jnp.where(column == 0, 0.0, pltpu.roll(value, 1, 0)),
            value,
            jnp.where(column == W - 1, 0.0, pltpu.roll(value, CELLS - 1, 0)),
        )
        for kw, view in enumerate(views):
            for slot, kept in targets:
                shown = view if kept is None else jnp.where(kept, view, 0.0)
                place(kw, slot, shown.astype(jnp.bfloat16))

    def tap(own, index):
        kt, kh, kw = index // 9, (index // 3) % 3, index % 3
        return slots_ref[kw, 3 * own + kt, kh * W : kh * W + CELLS, :]

    for own in range(2):
        for pair in range(DEPTH // LANES):
            first = tap(own, 2 * pair)
            second = tap(own, 2 * pair + 1) if 2 * pair + 1 < TAPS else jnp.zeros_like(first)
            cols_ref[own * CELLS : (own + 1) * CELLS, pair * LANES : (pair + 1) * LANES] = jnp.where(
                left, first, second
            )
    load.wait()
    for block in range(2):
        width = C // 2
        partial = jnp.dot(
            cols_ref[...],
            w_ref[:, block * width : (block + 1) * width],
            preferred_element_type=jnp.float32,
        )
        for tile in range(width // LANES):
            zero = partial[:CELLS, tile * LANES : (tile + 1) * LANES]
            one = partial[CELLS:, tile * LANES : (tile + 1) * LANES]
            place_at = block * (width // CHANS) + 2 * tile
            out_ref[place_at] = jnp.where(left, zero, pltpu.roll(one, CHANS, 1)).astype(jnp.bfloat16)
            out_ref[place_at + 1] = jnp.where(left, pltpu.roll(zero, CHANS, 1), one).astype(jnp.bfloat16)


def sum_partials(parts_ref, bias_ref):
    total = parts_ref[0].astype(jnp.float32)
    for k in range(1, parts_ref.shape[0]):
        total = total + parts_ref[k].astype(jnp.float32)
    return total + both_halves(bias_ref[...])


def middle_kernel(parts_ref, bias_ref, y_ref, sums_ref):
    y = sum_partials(parts_ref, bias_ref).astype(jnp.bfloat16)
    y_ref[...] = y
    write_sums(y.astype(jnp.float32), sums_ref)


def last_kernel(parts_ref, bias_ref, packed_ref, out_ref):
    value = sum_partials(parts_ref, bias_ref) + packed_ref[...].astype(jnp.float32)
    rows = value.T
    out_ref[:, 0, :] = rows[:CHANS]
    out_ref[:, 1, :] = rows[CHANS:]


def shape_of(shape, dtype):
    return jax.ShapeDtypeStruct(shape, dtype)


def normed_conv(packed, sums, lengths, first, gamma, beta, weight):
    tail = ring_shift(packed, "tm", 1)
    sums = lax.all_to_all(sums, "tm", 0, 0, tiled=True)
    parts = C // CHANS
    partial = pl.pallas_call(
        conv_kernel,
        out_shape=shape_of((parts, CELLS, LANES), jnp.bfloat16),
        in_specs=[SMEM, SMEM, VMEM, VMEM, VMEM, VMEM, VMEM, ANY],
        out_specs=VMEM,
        scratch_shapes=[
            pltpu.VMEM((DEPTH, C), jnp.bfloat16),
            pltpu.VMEM((3, 6, SLOT, LANES), jnp.bfloat16),
            pltpu.VMEM((2 * CELLS, DEPTH), jnp.bfloat16),
            pltpu.SemaphoreType.DMA,
        ],
        compiler_params=pltpu.CompilerParams(vmem_limit_bytes=24 << 20),
        cost_estimate=pl.CostEstimate(
            flops=2 * ROWS * C * 2 * CELLS, bytes_accessed=3 << 20, transcendentals=4 * CELLS * CHANS
        ),
        name="norm_conv",
    )(lengths, first, sums, packed, tail, gamma.reshape(1, CHANS), beta.reshape(1, CHANS), weight)
    return lax.all_to_all(partial, "chan", 0, 0, tiled=True)


def on_device(
    clip_input, lengths, gamma_one, beta_one, w_one, bias_one, gamma_two, beta_two, w_two, bias_two
):
    count = lax.axis_size("tm")
    first = (lax.axis_index("tm") * 2).astype(jnp.int32).reshape(1)
    packed_shape = shape_of((CELLS, LANES), jnp.bfloat16)
    sums_shape = shape_of((count, 8, LANES), jnp.float32)
    flat_one = jnp.transpose(w_one, (1, 0, 2)).reshape(ROWS, C)
    flat_two = jnp.transpose(w_two, (1, 0, 2)).reshape(ROWS, C)
    packed, sums = pl.pallas_call(
        pack_kernel,
        out_shape=(packed_shape, sums_shape),
        in_specs=[VMEM],
        out_specs=(VMEM, VMEM),
        name="pack",
    )(clip_input)
    parts = normed_conv(packed, sums, lengths, first, gamma_one, beta_one, flat_one)
    y_one, sums = pl.pallas_call(
        middle_kernel,
        out_shape=(packed_shape, sums_shape),
        in_specs=[VMEM, VMEM],
        out_specs=(VMEM, VMEM),
        name="middle",
    )(parts, bias_one.reshape(1, CHANS))
    parts = normed_conv(y_one, sums, lengths, first, gamma_two, beta_two, flat_two)
    return pl.pallas_call(
        last_kernel,
        out_shape=shape_of(clip_input.shape, jnp.float32),
        in_specs=[VMEM, VMEM, VMEM],
        out_specs=VMEM,
        name="last",
    )(parts, bias_two.reshape(1, CHANS), packed)


def solution(mesh):
    in_specs = (
        P("chan", "tm", None),
        P(),
        P("chan"),
        P("chan"),
        P("chan", None, None),
        P("chan"),
        P("chan"),
        P("chan"),
        P("chan", None, None),
        P("chan"),
    )
    out_specs = P("chan", "tm", None)
    return jax.shard_map(
        on_device, mesh=mesh, in_specs=in_specs, out_specs=out_specs, check_vma=False
    )
```

time: 94.4 us -> 84.4 us (0.89)
  matrix products: 18.3 us -> 0 us
  Pallas kernels: 0 us -> 11.9 us
  other arithmetic: 7 us -> 0 us
  waiting for transfers between devices: 12.2 us -> 18.5 us
  local copies, waits for them, and re-layouts: 7.03 us -> 5.13 us
  starting transfers between devices: 23.7 us -> 21.8 us
  blocking collectives: 25.1 us -> 26.5 us
    dot_general x54 -> x0, matrix products: 18.3 us -> none  [conv_taps(): lax.dot_general(weight_rows[:, 9 * kt + 3 * kh + kw, :], piece.reshape(ro...]
    pallas_call x0 -> x5, Pallas kernels: none -> 11.9 us  [the longest x2 6.42 us: normed_conv(): pl.pallas_call(conv_kernel, out_shape=shape_of((parts, CELLS, LANES), jnp...]
    ppermute x2, waiting for transfers between devices: 0.01 us -> 3.47 us  [ring_shift(): lax.ppermute(value, axis, [(source, (source + steps) % count) for source...]
    all_to_all x2, waiting for transfers between devices: 12.2 us -> 15 us  [normed_conv(): sums = lax.all_to_all(sums, 'tm', 0, 0, tiled=True)]
    mul x9 -> x0, other arithmetic: 2.16 us -> none  [the longest x6 1.49 us: conv_taps(): padded[:, kt:kt + count, kh:kh + H, kw:kw + W]]
    unnamed x17 -> x20, local copies, waits for them, and re-layouts: 3.1 us -> 5.13 us
    reduce_sum x10 -> x0, other arithmetic: 1.84 us -> none  [the longest x3 1.22 us: frame_sums(): sums = jnp.sum(grouped, axis=(1, 3))]
    all_to_all x2, starting transfers between devices: 20.1 us -> 18.4 us  [normed_conv(): sums = lax.all_to_all(sums, 'tm', 0, 0, tiled=True)]
  transfers between devices with their start and end apart: 4 -> 4, of which waited for: 2 -> 4; matrix products, arithmetic and copies ran while one was open for 5% -> 0% of each run, Pallas kernels for 0% -> 0%
where the time goes in v2:
time: 84.4 us; the launch traced here: 83.9 us
  blocking collectives  26.5 us (31%)
  starting transfers between devices  21.8 us (26%)
  waiting for transfers between devices  18.5 us (22%)
  Pallas kernels  11.9 us (14%)
  local copies, waits for them, and re-layouts  5.13 us (6%)
    all_to_all x2, blocking collectives, normed_conv(): return lax.all_to_all(partial, 'chan', 0, 0, tiled=True)  26.5 us
    all_to_all x2, starting transfers between devices, normed_conv(): sums = lax.all_to_all(sums, 'tm', 0, 0, tiled=True)  18.4 us
    all_to_all x2, waiting for transfers between devices, normed_conv(): sums = lax.all_to_all(sums, 'tm', 0, 0, tiled=True)  15 us
    pallas_call x2, Pallas kernels, normed_conv(): pl.pallas_call(conv_kernel, out_shape=shape_of((parts, CELLS, LANES), jnp...  6.42 us
    unnamed x20, local copies, waits for them, and re-layouts  5.13 us
    ppermute x2, waiting for transfers between devices, ring_shift(): lax.ppermute(value, axis, [(source, (source + steps) % count) for source...  3.47 us
    ppermute x2, starting transfers between devices, ring_shift(): lax.ppermute(value, axis, [(source, (source + steps) % count) for source...  3.42 us
    pallas_call x1, Pallas kernels, on_device(): pl.pallas_call(last_kernel, out_shape=shape_of(clip_input.shape, jnp.floa...  1.9 us
  transfers between devices with their start and end apart: 4, of which 4 were waited for; matrix products, arithmetic and copies ran while one was open for 0% of the time, Pallas kernels for 0%

profile of v2, /device:TPU:1, one launch (start us, length us, event | category | flops | bytes accessed | tf_op | source)
XLA Modules:
  0.0 83.9 jit_solution(7270717472399389128)
XLA Ops:
  0.0 1.7 %pack.1 = (bf16[256,128]{1,0:T(8,128)(2,1)}, f32[32,8,128]{2,1,0:T(8,128)}) custom-call(bf16[64,2,256]{2,1,0:T(2,128)(2,1)} %x_ref.1), custom_call_target="tpu_custom_call" | custom-call | tf_op jit(solution)/shard_map/pack/pallas_call | solution.py:235
  1.7 12.8 %all-to-all-start = ((f32[32,8,128]{2,1,0:T(8,128)}), f32[32,8,128]{2,1,0:T(8,128)S(1)}, u32[]{:S(2)}, u32[]{:S(2)}) async-start(f32[32,8,128]{2,1,0:T(8,128)} %get-tuple-element.9), calls=%async_computation | async-start | bytes 262144 | tf_op jit(solution)/shard_map/all_to_all | solution.py:204
  14.5 1.7 %collective-permute-start = (bf16[256,128]{1,0:T(8,128)(2,1)}, bf16[256,128]{1,0:T(8,128)(2,1)S(1)}, u32[]{:S(2)}, u32[]{:S(2)}) collective-permute-start(bf16[256,128]{1,0:T(8,128)(2,1)} %get-tuple-element.10.own_ref.packed_ref), channel_id=1, source_target_pairs={{0,8},{8,16},{16,24},{24,32},{32,40},{40,48},{48,56},{56,64},{64,7... | collective-permute-start | bytes 196616 | tf_op jit(solution)/shard_map/ppermute | solution.py:29
  16.2 1.7 %collective-permute-done.tail_ref = bf16[256,128]{1,0:T(8,128)(2,1)S(1)} collective-permute-done((bf16[256,128]{1,0:T(8,128)(2,1)}, bf16[256,128]{1,0:T(8,128)(2,1)S(1)}, u32[]{:S(2)}, u32[]{:S(2)}) %collective-permute-start) | collective-permute-done | bytes 65568 | tf_op jit(solution)/shard_map/ppermute | solution.py:29
  18.0 7.6 %all-to-all-done.sums_ref = f32[32,8,128]{2,1,0:T(8,128)S(1)} async-done(((f32[32,8,128]{2,1,0:T(8,128)}), f32[32,8,128]{2,1,0:T(8,128)S(1)}, u32[]{:S(2)}, u32[]{:S(2)}) %all-to-all-start) | async-done | bytes 131104 | tf_op jit(solution)/shard_map/all_to_all | solution.py:204
  25.5 0.8 copy-done
  26.3 1.5 %copy-done.1 = bf16[64,27,512]{2,0,1:T(8,128)(2,1)S(1)} copy-done((bf16[64,27,512]{2,0,1:T(8,128)(2,1)S(1)}, bf16[64,27,512]{2,0,1:T(8,128)(2,1)}, u32[]{:S(2)}) %copy-start.1) | copy-done | bytes 1769496
  27.8 0.7 copy-done.4
  28.5 0.7 copy-done.5
  29.1 0.7 copy-done.6
  29.8 3.2 %norm_conv.2 = bf16[8,256,128]{2,1,0:T(8,128)(2,1)S(1)} custom-call(s32[16]{0:T(128)S(1)} %copy-done.6, s32[1]{0:T(128)} %bitcast.first_ref, f32[32,8,128]{2,1,0:T(8,128)S(1)} %all-to-all-done.sums_ref, bf16[256,128]{1,0:T(8,128)(2,1)S(1)} %copy-done, bf16[256,128]{1,0:T(8,128)(2,1)S(1)} %collective-permute-done.tail_ref, f32[1,64]{1,0:T(1,128)S(1)} %bitcast.15, ...), custom_call_target="tpu_custom_call" | custom-call | flops 905969664 | bytes 3145728 | tf_op jit(solution)/shard_map/norm_conv/pallas_call | solution.py:206
  33.0 13.5 %all_to_all.20.parts_ref = bf16[8,256,128]{2,1,0:T(8,128)(2,1)} all-to-all(bf16[8,256,128]{2,1,0:T(8,128)(2,1)S(1)} %norm_conv.2), channel_id=1, replica_groups=mesh['tm'=32,'chan'=8] {'chan'}, dimensions={0} | all-to-all | bytes 1048576 | tf_op jit(solution)/shard_map/all_to_all | solution.py:223
  46.5 1.8 %middle.1 = (bf16[256,128]{1,0:T(8,128)(2,1)}, f32[32,8,128]{2,1,0:T(8,128)}) custom-call(bf16[8,256,128]{2,1,0:T(8,128)(2,1)} %all_to_all.20.parts_ref, f32[1,64]{1,0:T(1,128)} %bitcast.19), custom_call_target="tpu_custom_call" | custom-call | tf_op jit(solution)/shard_map/middle/pallas_call | solution.py:243
  48.4 5.7 %all-to-all-start.2 = ((f32[32,8,128]{2,1,0:T(8,128)}), f32[32,8,128]{2,1,0:T(8,128)S(1)}, u32[]{:S(2)}, u32[]{:S(2)}) async-start(f32[32,8,128]{2,1,0:T(8,128)} %get-tuple-element.11), calls=%async_computation.2 | async-start | bytes 262144 | tf_op jit(solution)/shard_map/all_to_all | solution.py:204
  54.0 1.7 %collective-permute-start.1 = (bf16[256,128]{1,0:T(8,128)(2,1)}, bf16[256,128]{1,0:T(8,128)(2,1)S(1)}, u32[]{:S(2)}, u32[]{:S(2)}) collective-permute-start(bf16[256,128]{1,0:T(8,128)(2,1)} %get-tuple-element.12.own_ref), channel_id=1, source_target_pairs={{0,8},{8,16},{16,24},{24,32},{32,40},{40,48},{48,56},{56,64},{64,7... | collective-permute-start | bytes 196616 | tf_op jit(solution)/shard_map/ppermute | solution.py:29
  55.7 1.7 %collective-permute-done.1.tail_ref = bf16[256,128]{1,0:T(8,128)(2,1)S(1)} collective-permute-done((bf16[256,128]{1,0:T(8,128)(2,1)}, bf16[256,128]{1,0:T(8,128)(2,1)S(1)}, u32[]{:S(2)}, u32[]{:S(2)}) %collective-permute-start.1) | collective-permute-done | bytes 65568 | tf_op jit(solution)/shard_map/ppermute | solution.py:29
  57.5 7.4 %all-to-all-done.2.sums_ref = f32[32,8,128]{2,1,0:T(8,128)S(1)} async-done(((f32[32,8,128]{2,1,0:T(8,128)}), f32[32,8,128]{2,1,0:T(8,128)S(1)}, u32[]{:S(2)}, u32[]{:S(2)}) %all-to-all-start.2) | async-done | bytes 131104 | tf_op jit(solution)/shard_map/all_to_all | solution.py:204
  64.9 0.0 copy-done.2
  64.9 0.0 copy-done.7
  64.9 0.0 copy-done.8
  65.0 0.8 copy-done.3
  65.8 3.2 %norm_conv.3 = bf16[8,256,128]{2,1,0:T(8,128)(2,1)S(1)} custom-call(s32[16]{0:T(128)S(1)} %copy-done.7, s32[1]{0:T(128)} %bitcast.first_ref, f32[32,8,128]{2,1,0:T(8,128)S(1)} %all-to-all-done.2.sums_ref, bf16[256,128]{1,0:T(8,128)(2,1)S(1)} %copy-done.3, bf16[256,128]{1,0:T(8,128)(2,1)S(1)} %collective-permute-done.1.tail_ref, f32[1,64]{1,0:T(1,128)S(1)} %bitcast.17, ...), custom_call_target="tpu_custom_call" | custom-call | flops 905969664 | bytes 3145728 | tf_op jit(solution)/shard_map/norm_conv/pallas_call | solution.py:206
  69.0 13.0 %all_to_all.21.parts_ref = bf16[8,256,128]{2,1,0:T(8,128)(2,1)} all-to-all(bf16[8,256,128]{2,1,0:T(8,128)(2,1)S(1)} %norm_conv.3), channel_id=1, replica_groups=mesh['tm'=32,'chan'=8] {'chan'}, dimensions={0} | all-to-all | bytes 1048576 | tf_op jit(solution)/shard_map/all_to_all | solution.py:223
  82.0 1.9 %last.1 = f32[64,2,256]{2,1,0:T(2,128)} custom-call(bf16[8,256,128]{2,1,0:T(8,128)(2,1)} %all_to_all.21.parts_ref, f32[1,64]{1,0:T(1,128)} %bitcast.20, bf16[256,128]{1,0:T(8,128)(2,1)} %get-tuple-element.10.own_ref.packed_ref), custom_call_target="tpu_custom_call" | custom-call | tf_op jit(solution)/shard_map/last/pallas_call | solution.py:251
  (11 shorter events, 0.0 us)
Async XLA Ops:
  1.7 23.8 %all-to-all-start = ((f32[32,8,128]{2,1,0:T(8,128)}), f32[32,8,128]{2,1,0:T(8,128)S(1)}, u32[]{:S(2)}, u32[]{:S(2)}) async-start(f32[32,8,128]{2,1,0:T(8,128)} %get-tuple-element.9), calls=%async_computation | async-start | bytes 262144 | tf_op jit(solution)/shard_map/all_to_all | solution.py:204
  14.5 3.4 %collective-permute-start = (bf16[256,128]{1,0:T(8,128)(2,1)}, bf16[256,128]{1,0:T(8,128)(2,1)S(1)}, u32[]{:S(2)}, u32[]{:S(2)}) collective-permute-start(bf16[256,128]{1,0:T(8,128)(2,1)} %get-tuple-element.10.own_ref.packed_ref), channel_id=1, source_target_pairs={{0,8},{8,16},{16,24},{24,32},{32,40},{40,48},{48,56},{56,64},{64,7... | collective-permute-start | bytes 196616 | tf_op jit(solution)/shard_map/ppermute | solution.py:29
  25.5 0.8 %copy-start = (bf16[256,128]{1,0:T(8,128)(2,1)S(1)}, bf16[256,128]{1,0:T(8,128)(2,1)}, u32[]{:S(2)}) copy-start(bf16[256,128]{1,0:T(8,128)(2,1)} %get-tuple-element.10.own_ref.packed_ref) | copy-start | bytes 196612
  26.3 1.5 %copy-start.1 = (bf16[64,27,512]{2,0,1:T(8,128)(2,1)S(1)}, bf16[64,27,512]{2,0,1:T(8,128)(2,1)}, u32[]{:S(2)}) copy-start(bf16[64,27,512]{2,0,1:T(8,128)(2,1)} %param.14) | copy-start | bytes 5308420
  27.8 0.7 copy-start.4
  28.5 0.7 copy-start.5
  29.1 0.7 copy-start.6
  29.8 35.1 %copy-start.2 = (bf16[64,27,512]{2,0,1:T(8,128)(2,1)S(1)}, bf16[64,27,512]{2,0,1:T(8,128)(2,1)}, u32[]{:S(2)}) copy-start(bf16[64,27,512]{2,0,1:T(8,128)(2,1)} %param.18) | copy-start | bytes 5308420
  29.8 35.1 %copy-start.7 = (s32[16]{0:T(128)S(1)}, s32[16]{0:T(128)}, u32[]{:S(2)}) copy-start(s32[16]{0:T(128)} %lengths_ref.3) | copy-start | bytes 196
  29.8 35.1 %copy-start.8 = (f32[64]{0:T(128)S(1)}, f32[64]{0:T(128)}, u32[]{:S(2)}) copy-start(f32[64]{0:T(128)} %param.16) | copy-start | bytes 772
  29.8 35.1 %copy-start.9 = (f32[64]{0:T(128)S(1)}, f32[64]{0:T(128)}, u32[]{:S(2)}) copy-start(f32[64]{0:T(128)} %param.17) | copy-start | bytes 772
  48.4 16.6 %all-to-all-start.2 = ((f32[32,8,128]{2,1,0:T(8,128)}), f32[32,8,128]{2,1,0:T(8,128)S(1)}, u32[]{:S(2)}, u32[]{:S(2)}) async-start(f32[32,8,128]{2,1,0:T(8,128)} %get-tuple-element.11), calls=%async_computation.2 | async-start | bytes 262144 | tf_op jit(solution)/shard_map/all_to_all | solution.py:204
  54.0 3.4 %collective-permute-start.1 = (bf16[256,128]{1,0:T(8,128)(2,1)}, bf16[256,128]{1,0:T(8,128)(2,1)S(1)}, u32[]{:S(2)}, u32[]{:S(2)}) collective-permute-start(bf16[256,128]{1,0:T(8,128)(2,1)} %get-tuple-element.12.own_ref), channel_id=1, source_target_pairs={{0,8},{8,16},{16,24},{24,32},{32,40},{40,48},{48,56},{56,64},{64,7... | collective-permute-start | bytes 196616 | tf_op jit(solution)/shard_map/ppermute | solution.py:29
  64.9 0.8 %copy-start.3 = (bf16[256,128]{1,0:T(8,128)(2,1)S(1)}, bf16[256,128]{1,0:T(8,128)(2,1)}, u32[]{:S(2)}) copy-start(bf16[256,128]{1,0:T(8,128)(2,1)} %get-tuple-element.12.own_ref) | copy-start | bytes 196612

commit v3 on v2

--- a/solution.py
+++ b/solution.py
@@ -1,3 +1,5 @@
+import functools
+
 import jax
 import jax.numpy as jnp
 from jax import lax
@@ -21,7 +23,8 @@
 
 VMEM = pl.BlockSpec(memory_space=pltpu.VMEM)
 SMEM = pl.BlockSpec(memory_space=pltpu.SMEM)
-ANY = pl.BlockSpec(memory_space=pl.ANY)
+HBM = pl.BlockSpec(memory_space=pltpu.HBM)
+SMALL = pltpu.CompilerParams(vmem_limit_bytes=4 << 20)
 
 
 def ring_shift(value, axis, steps):
@@ -33,28 +36,8 @@
     return lax.broadcasted_iota(jnp.int32, shape, len(shape) - 1) < CHANS
 
 
-def write_sums(values, sums_ref):
-    total = jnp.sum(values, axis=0, keepdims=True)
-    squares = jnp.sum(values * values, axis=0, keepdims=True)
-    row = lax.broadcasted_iota(jnp.int32, (8, LANES), 0)
-    tile = jnp.where(row == 0, total, jnp.where(row == 1, squares, 0.0))
-    sums_ref[...] = jnp.broadcast_to(tile[None], sums_ref.shape)
-
-
-def both_halves(row):
-    return jnp.concatenate([row, row], axis=1)
-
-
-def pack_kernel(x_ref, packed_ref, sums_ref):
-    rows = jnp.concatenate([x_ref[:, 0, :], x_ref[:, 1, :]], axis=0).astype(jnp.float32)
-    values = rows.T
-    packed_ref[...] = values.astype(jnp.bfloat16)
-    write_sums(values, sums_ref)
-
-
 def group_totals(rows):
     lane = lax.broadcasted_iota(jnp.int32, rows.shape, 1)
-    rows = rows + pltpu.roll(rows, CHANS, 1)
     step = 1
     while step < GROUP_SIZE:
         other = jnp.where(
@@ -63,6 +46,32 @@
         rows = rows + other
         step *= 2
     return rows
+
+
+def holds_sum(shape):
+    lane = lax.broadcasted_iota(jnp.int32, shape, len(shape) - 1)
+    return (lane & (GROUP_SIZE // 2)) == 0
+
+
+def write_sums(values, sums_ref):
+    total = group_totals(jnp.sum(values, axis=0, keepdims=True))
+    squares = group_totals(jnp.sum(values * values, axis=0, keepdims=True))
+    row = jnp.where(holds_sum((1, LANES)), total, squares)
+    sums_ref[...] = jnp.broadcast_to(row[None], sums_ref.shape)
+
+
+def both_halves(row):
+    return jnp.concatenate([row, row], axis=1)
+
+
+def pack_kernel(x_hbm, packed_ref, sums_ref, x_ref, sem):
+    load = pltpu.make_async_copy(x_hbm, x_ref, sem)
+    load.start()
+    load.wait()
+    rows = jnp.concatenate([x_ref[:, 0, :], x_ref[:, 1, :]], axis=0).astype(jnp.float32)
+    values = rows.T
+    packed_ref[...] = values.astype(jnp.bfloat16)
+    write_sums(values, sums_ref)
 
 
 def clip_bounds(lengths_ref, frame):
@@ -78,33 +87,42 @@
     return start, end
 
 
+def prepare_kernel(
+    lengths_ref, first_ref, after_ref, weight_ref, affine_ref, params_ref, clips_ref
+):
+    del after_ref, weight_ref
+    params_ref[...] = both_halves(affine_ref[...])
+    frame = first_ref[0]
+    start_zero, end_zero = clip_bounds(lengths_ref, frame)
+    start_one, end_one = clip_bounds(lengths_ref, frame + 1)
+    for k, number in enumerate((start_zero, end_zero, start_one, end_one, frame, frame, frame, frame)):
+        clips_ref[k : k + 1, :] = jnp.full((1, LANES), number, jnp.int32)
+
+
 def conv_kernel(
-    lengths_ref, first_ref, sums_ref, own_ref, tail_ref, gamma_ref, beta_ref, w_hbm, out_ref,
-    w_ref, slots_ref, cols_ref, sem,
+    at, sums_ref, own_ref, tail_ref, params_ref, clips_ref, w_ref, out_ref, slots_ref, cols_ref
 ):
-    load = pltpu.make_async_copy(w_hbm, w_ref.at[pl.ds(0, ROWS), :], sem)
-    load.start()
-    w_ref[ROWS:, :] = jnp.zeros((DEPTH - ROWS, C), jnp.bfloat16)
-
-    frame = first_ref[0]
-    bounds = [clip_bounds(lengths_ref, frame), clip_bounds(lengths_ref, frame + 1)]
+    clips = clips_ref[...]
+    start_zero, end_zero = clips[0:1, :], clips[1:2, :]
+    start_one, end_one = clips[2:3, :], clips[3:4, :]
+    frame = clips[4:5, :]
     count = sums_ref.shape[0]
     device = lax.broadcasted_iota(jnp.int32, (count, 1, LANES), 0)
     half = (lax.broadcasted_iota(jnp.int32, (count, 1, LANES), 2) >= CHANS).astype(jnp.int32)
     frame_of = 2 * device + half
     sums = sums_ref[...]
+    is_sum = holds_sum((1, LANES))
     stats = []
-    for start, end in bounds:
-        inside = (frame_of >= start) & (frame_of < end)
-        per_lane = jnp.sum(jnp.where(inside, sums, 0.0), axis=0)
-        totals = group_totals(per_lane)
+    for start, end in ((start_zero, end_zero), (start_one, end_one)):
+        inside = (frame_of >= start[None]) & (frame_of < end[None])
+        row = jnp.sum(jnp.where(inside, sums, 0.0), axis=0)
         size = ((end - start) * (GROUP_SIZE * CELLS)).astype(jnp.float32)
-        totals = totals / size
-        mean = totals[0:1, :]
-        var = totals[1:2, :] - mean * mean
-        stats.append((mean, lax.rsqrt(var + EPS)))
-    gamma = both_halves(gamma_ref[...])
-    beta = both_halves(beta_ref[...])
+        row = (row + pltpu.roll(row, CHANS, 1)) / size
+        mean = jnp.where(is_sum, row, pltpu.roll(row, GROUP_SIZE // 2, 1))
+        second = jnp.where(is_sum, pltpu.roll(row, LANES - GROUP_SIZE // 2, 1), row)
+        stats.append((mean, lax.rsqrt(second - mean * mean + EPS)))
+    gamma = params_ref[at : at + 1, :]
+    beta = params_ref[at + 1 : at + 2, :]
     left_row = left_half((1, LANES))
     mean_tail, scale_tail = stats[0]
     mean_own = jnp.where(left_row, stats[0][0], stats[1][0])
@@ -122,7 +140,6 @@
 
     before_two, before_one = split(normed(tail_ref, mean_tail, scale_tail))
     own_zero, own_one = split(normed(own_ref, mean_own, scale_own))
-    start_zero, start_one = bounds[0][0], bounds[1][0]
     column = lax.broadcasted_iota(jnp.int32, (CELLS, LANES), 0) % W
     margin = jnp.zeros((W, LANES), jnp.bfloat16)
 
@@ -159,11 +176,10 @@
             cols_ref[own * CELLS : (own + 1) * CELLS, pair * LANES : (pair + 1) * LANES] = jnp.where(
                 left, first, second
             )
-    load.wait()
     for block in range(2):
         width = C // 2
         partial = jnp.dot(
-            cols_ref[...],
+            cols_ref[:, :ROWS],
             w_ref[:, block * width : (block + 1) * width],
             preferred_element_type=jnp.float32,
         )
@@ -175,21 +191,21 @@
             out_ref[place_at + 1] = jnp.where(left, pltpu.roll(zero, CHANS, 1), one).astype(jnp.bfloat16)
 
 
-def sum_partials(parts_ref, bias_ref):
+def sum_partials(parts_ref, bias):
     total = parts_ref[0].astype(jnp.float32)
     for k in range(1, parts_ref.shape[0]):
         total = total + parts_ref[k].astype(jnp.float32)
-    return total + both_halves(bias_ref[...])
-
-
-def middle_kernel(parts_ref, bias_ref, y_ref, sums_ref):
-    y = sum_partials(parts_ref, bias_ref).astype(jnp.bfloat16)
+    return total + bias
+
+
+def middle_kernel(parts_ref, params_ref, y_ref, sums_ref):
+    y = sum_partials(parts_ref, params_ref[2:3, :]).astype(jnp.bfloat16)
     y_ref[...] = y
     write_sums(y.astype(jnp.float32), sums_ref)
 
 
-def last_kernel(parts_ref, bias_ref, packed_ref, out_ref):
-    value = sum_partials(parts_ref, bias_ref) + packed_ref[...].astype(jnp.float32)
+def last_kernel(parts_ref, params_ref, packed_ref, out_ref):
+    value = sum_partials(parts_ref, params_ref[5:6, :]) + packed_ref[...].astype(jnp.float32)
     rows = value.T
     out_ref[:, 0, :] = rows[:CHANS]
     out_ref[:, 1, :] = rows[CHANS:]
@@ -199,27 +215,23 @@
     return jax.ShapeDtypeStruct(shape, dtype)
 
 
-def normed_conv(packed, sums, lengths, first, gamma, beta, weight):
-    tail = ring_shift(packed, "tm", 1)
-    sums = lax.all_to_all(sums, "tm", 0, 0, tiled=True)
+def normed_conv(at, tail, packed, sums, params, clips, weight):
     parts = C // CHANS
     partial = pl.pallas_call(
-        conv_kernel,
+        functools.partial(conv_kernel, at),
         out_shape=shape_of((parts, CELLS, LANES), jnp.bfloat16),
-        in_specs=[SMEM, SMEM, VMEM, VMEM, VMEM, VMEM, VMEM, ANY],
+        in_specs=[VMEM, VMEM, VMEM, VMEM, VMEM, VMEM],
         out_specs=VMEM,
         scratch_shapes=[
-            pltpu.VMEM((DEPTH, C), jnp.bfloat16),
             pltpu.VMEM((3, 6, SLOT, LANES), jnp.bfloat16),
             pltpu.VMEM((2 * CELLS, DEPTH), jnp.bfloat16),
-            pltpu.SemaphoreType.DMA,
         ],
-        compiler_params=pltpu.CompilerParams(vmem_limit_bytes=24 << 20),
+        compiler_params=pltpu.CompilerParams(vmem_limit_bytes=10 << 20),
         cost_estimate=pl.CostEstimate(
             flops=2 * ROWS * C * 2 * CELLS, bytes_accessed=3 << 20, transcendentals=4 * CELLS * CHANS
         ),
         name="norm_conv",
-    )(lengths, first, sums, packed, tail, gamma.reshape(1, CHANS), beta.reshape(1, CHANS), weight)
+    )(sums, packed, tail, params, clips, weight)
     return lax.all_to_all(partial, "chan", 0, 0, tiled=True)
 
 
@@ -229,32 +241,50 @@
     count = lax.axis_size("tm")
     first = (lax.axis_index("tm") * 2).astype(jnp.int32).reshape(1)
     packed_shape = shape_of((CELLS, LANES), jnp.bfloat16)
-    sums_shape = shape_of((count, 8, LANES), jnp.float32)
+    sums_shape = shape_of((count, 1, LANES), jnp.float32)
     flat_one = jnp.transpose(w_one, (1, 0, 2)).reshape(ROWS, C)
     flat_two = jnp.transpose(w_two, (1, 0, 2)).reshape(ROWS, C)
     packed, sums = pl.pallas_call(
         pack_kernel,
         out_shape=(packed_shape, sums_shape),
-        in_specs=[VMEM],
+        in_specs=[HBM],
         out_specs=(VMEM, VMEM),
+        scratch_shapes=[pltpu.VMEM((CHANS, 2, CELLS), jnp.bfloat16), pltpu.SemaphoreType.DMA],
+        compiler_params=SMALL,
         name="pack",
     )(clip_input)
-    parts = normed_conv(packed, sums, lengths, first, gamma_one, beta_one, flat_one)
+    everyone = lax.all_to_all(sums, "tm", 0, 0, tiled=True)
+    tail = ring_shift(packed, "tm", 1)
+    affine = (gamma_one, beta_one, bias_one, gamma_two, beta_two, bias_two, gamma_two, beta_two)
+    params, clips = pl.pallas_call(
+        prepare_kernel,
+        out_shape=(shape_of((8, LANES), jnp.float32), shape_of((8, LANES), jnp.int32)),
+        in_specs=[SMEM, SMEM, VMEM, VMEM, VMEM],
+        out_specs=(VMEM, VMEM),
+        compiler_params=SMALL,
+        cost_estimate=pl.CostEstimate(flops=10000, bytes_accessed=2 << 20, transcendentals=0),
+        name="prepare",
+    )(lengths, first, packed, flat_one, jnp.stack(affine))
+    parts = normed_conv(0, tail, packed, everyone, params, clips, flat_one)
     y_one, sums = pl.pallas_call(
         middle_kernel,
         out_shape=(packed_shape, sums_shape),
         in_specs=[VMEM, VMEM],
         out_specs=(VMEM, VMEM),
+        compiler_params=SMALL,
         name="middle",
-    )(parts, bias_one.reshape(1, CHANS))
-    parts = normed_conv(y_one, sums, lengths, first, gamma_two, beta_two, flat_two)
+    )(parts, params)
+    everyone = lax.all_to_all(sums, "tm", 0, 0, tiled=True)
+    tail = ring_shift(y_one, "tm", 1)
+    parts = normed_conv(3, tail, y_one, everyone, params, clips, flat_two)
     return pl.pallas_call(
         last_kernel,
         out_shape=shape_of(clip_input.shape, jnp.float32),
         in_specs=[VMEM, VMEM, VMEM],
         out_specs=VMEM,
+        compiler_params=SMALL,
         name="last",
-    )(parts, bias_two.reshape(1, CHANS), packed)
+    )(parts, params, packed)
 
 
 def solution(mesh):

time: 84.4 us -> 73.9 us (0.88)
  blocking collectives: 26.5 us -> 41.4 us
  waiting for transfers between devices: 18.5 us -> 5.77 us
  starting transfers between devices: 21.8 us -> 15.9 us
  Pallas kernels: 11.9 us -> 6.6 us
  local copies, waits for them, and re-layouts: 5.13 us -> 3.77 us
    all_to_all x0 -> x1, blocking collectives: none -> 16.4 us  [on_device(): everyone = lax.all_to_all(sums, 'tm', 0, 0, tiled=True)]
    all_to_all x2 -> x1, waiting for transfers between devices: 15 us -> 5.76 us  [on_device(): everyone = lax.all_to_all(sums, 'tm', 0, 0, tiled=True)]
    all_to_all x2 -> x1, starting transfers between devices: 18.4 us -> 11.1 us  [on_device(): everyone = lax.all_to_all(sums, 'tm', 0, 0, tiled=True)]
    ppermute x2, waiting for transfers between devices: 3.47 us -> 0.01 us  [ring_shift(): lax.ppermute(value, axis, [(source, (source + steps) % count) for source...]
    pallas_call x2 -> x3, Pallas kernels: 6.42 us -> 4.17 us  [the longest x2 3.56 us: normed_conv(): pl.pallas_call(functools.partial(conv_kernel, at), out_shape=shape_of((pa...]
    unnamed x20 -> x10, local copies, waits for them, and re-layouts: 5.13 us -> 2.97 us
    all_to_all x2, blocking collectives: 26.5 us -> 25.1 us  [normed_conv(): return lax.all_to_all(partial, 'chan', 0, 0, tiled=True)]
    ppermute x2, starting transfers between devices: 3.42 us -> 4.85 us  [ring_shift(): lax.ppermute(value, axis, [(source, (source + steps) % count) for source...]
  transfers between devices with their start and end apart: 4 -> 3, of which waited for: 4 -> 1; matrix products, arithmetic and copies ran while one was open for 0% -> 1% of each run, Pallas kernels for 0% -> 1%
where the time goes in v3:
time: 73.9 us; the launch traced here: 73.6 us
  blocking collectives  41.4 us (56%)
  starting transfers between devices  15.9 us (22%)
  Pallas kernels  6.6 us (9%)
  waiting for transfers between devices  5.77 us (8%)
  local copies, waits for them, and re-layouts  3.77 us (5%)
    all_to_all x2, blocking collectives, normed_conv(): return lax.all_to_all(partial, 'chan', 0, 0, tiled=True)  25.1 us
    all_to_all x1, blocking collectives, on_device(): everyone = lax.all_to_all(sums, 'tm', 0, 0, tiled=True)  16.4 us
    all_to_all x1, starting transfers between devices, on_device(): everyone = lax.all_to_all(sums, 'tm', 0, 0, tiled=True)  11.1 us
    all_to_all x1, waiting for transfers between devices, on_device(): everyone = lax.all_to_all(sums, 'tm', 0, 0, tiled=True)  5.76 us
    ppermute x2, starting transfers between devices, ring_shift(): lax.ppermute(value, axis, [(source, (source + steps) % count) for source...  4.85 us
    pallas_call x2, Pallas kernels, normed_conv(): pl.pallas_call(functools.partial(conv_kernel, at), out_shape=shape_of((pa...  3.56 us
    unnamed x10, local copies, waits for them, and re-layouts  2.97 us
  transfers between devices with their start and end apart: 3, of which 1 were waited for; matrix products, arithmetic and copies ran while one was open for 1% of the time, Pallas kernels for 1%

profile of v3, /device:TPU:1, one launch (start us, length us, event | category | flops | bytes accessed | tf_op | source)
XLA Modules:
  0.0 73.6 jit_solution(17951542839228491345)
XLA Ops:
  0.0 0.0 copy-start.2
  0.0 0.8 %copy-done.2 = bf16[64,2,256]{2,1,0:T(2,128)(2,1)S(1)} copy-done((bf16[64,2,256]{2,1,0:T(2,128)(2,1)S(1)}, bf16[64,2,256]{2,1,0:T(2,128)(2,1)}, u32[]{:S(2)}) %copy-start.2) | copy-done | bytes 65560
  0.8 1.2 %pack.1 = (bf16[256,128]{1,0:T(8,128)(2,1)S(1)}, f32[32,1,128]{2,1,0:T(1,128)}) custom-call(bf16[64,2,256]{2,1,0:T(2,128)(2,1)S(1)} %copy-done.2), custom_call_target="tpu_custom_call" | custom-call | tf_op jit(solution)/shard_map/pack/pallas_call | solution.py:247
  2.0 2.8 %collective-permute-start = (bf16[256,128]{1,0:T(8,128)(2,1)S(1)}, bf16[256,128]{1,0:T(8,128)(2,1)S(1)}, u32[]{:S(2)}, u32[]{:S(2)}) collective-permute-start(bf16[256,128]{1,0:T(8,128)(2,1)S(1)} %get-tuple-element.12.after_ref.own_ref.packed_ref), channel_id=1, source_target_pairs={{0,8},{8,16},{16,24},{24,32},{32,40},{40,48},{48,56},{56,64},{64,7... | collective-permute-start | bytes 196616 | tf_op jit(solution)/shard_map/ppermute | solution.py:32
  4.8 11.1 %all-to-all-start = ((f32[32,1,128]{2,1,0:T(1,128)}), f32[32,1,128]{2,1,0:T(1,128)S(1)}, u32[]{:S(2)}, u32[]{:S(2)}) async-start(f32[32,1,128]{2,1,0:T(1,128)} %get-tuple-element.11), calls=%async_computation | async-start | bytes 32768 | tf_op jit(solution)/shard_map/all_to_all | solution.py:256
  15.9 0.8 %stack.29.affine_ref = f32[8,64]{1,0:T(8,128)S(1)} concatenate(f32[1,64]{1,0:T(1,128)} %bitcast.20, f32[1,64]{1,0:T(1,128)} %bitcast.21, f32[1,64]{1,0:T(1,128)} %bitcast.22, f32[1,64]{1,0:T(1,128)} %bitcast.16, f32[1,64]{1,0:T(1,128)} %bitcast.18, f32[1,64]{1,0:T(1,128)} %bitcast.23, f32[1,64]{1,0:T(1,128)} %bitcast.17, f32[1,64]{1,0:T(1,128)} %bitcast.19), dimensions={0} | concatenate | bytes 4096 | tf_op jit(solution)/shard_map/stack | solution.py:267
  16.7 0.0 copy-start
  16.7 1.5 %copy-done = bf16[64,27,512]{2,0,1:T(8,128)(2,1)S(1)} copy-done((bf16[64,27,512]{2,0,1:T(8,128)(2,1)S(1)}, bf16[64,27,512]{2,0,1:T(8,128)(2,1)}, u32[]{:S(2)}) %copy-start) | copy-done | bytes 1769496
  18.2 0.0 copy-start.3
  18.2 0.7 copy-done.3
  18.8 0.6 prepare.1
  19.4 5.8 %all-to-all-done.sums_ref = f32[32,1,128]{2,1,0:T(1,128)S(1)} async-done(((f32[32,1,128]{2,1,0:T(1,128)}), f32[32,1,128]{2,1,0:T(1,128)S(1)}, u32[]{:S(2)}, u32[]{:S(2)}) %all-to-all-start) | async-done | bytes 16416 | tf_op jit(solution)/shard_map/all_to_all | solution.py:256
  25.2 0.0 collective-permute-done.tail_ref
  25.2 0.0 copy-done.1
  25.2 1.8 %norm_conv.2 = bf16[8,256,128]{2,1,0:T(8,128)(2,1)S(1)} custom-call(f32[32,1,128]{2,1,0:T(1,128)S(1)} %all-to-all-done.sums_ref, bf16[256,128]{1,0:T(8,128)(2,1)S(1)} %get-tuple-element.12.after_ref.own_ref.packed_ref, bf16[256,128]{1,0:T(8,128)(2,1)S(1)} %collective-permute-done.tail_ref, f32[8,128]{1,0:T(8,128)S(1)} %get-tuple-element.13.params_ref, ...), custom_call_target="tpu_custom_call" | custom-call | flops 905969664 | bytes 3145728 | tf_op jit(solution)/shard_map/norm_conv/pallas_call | solution.py:220
  27.0 13.5 %all_to_all.20.parts_ref = bf16[8,256,128]{2,1,0:T(8,128)(2,1)S(1)} all-to-all(bf16[8,256,128]{2,1,0:T(8,128)(2,1)S(1)} %norm_conv.2), channel_id=1, replica_groups=mesh['tm'=32,'chan'=8] {'chan'}, dimensions={0} | all-to-all | bytes 1048576 | tf_op jit(solution)/shard_map/all_to_all | solution.py:235
  40.5 0.4 middle.1
  40.9 2.1 %collective-permute-start.1 = (bf16[256,128]{1,0:T(8,128)(2,1)S(1)}, bf16[256,128]{1,0:T(8,128)(2,1)S(1)}, u32[]{:S(2)}, u32[]{:S(2)}) collective-permute-start(bf16[256,128]{1,0:T(8,128)(2,1)S(1)} %get-tuple-element.16.own_ref), channel_id=1, source_target_pairs={{0,8},{8,16},{16,24},{24,32},{32,40},{40,48},{48,56},{56,64},{64,7... | collective-permute-start | bytes 196616 | tf_op jit(solution)/shard_map/ppermute | solution.py:32
  43.0 16.4 %all_to_all.21.sums_ref = f32[32,1,128]{2,1,0:T(1,128)S(1)} all-to-all(f32[32,1,128]{2,1,0:T(1,128)S(1)} %get-tuple-element.15), channel_id=1, replica_groups=mesh['tm'=32,'chan'=8] {'tm'}, dimensions={0} | all-to-all | bytes 32768 | tf_op jit(solution)/shard_map/all_to_all | solution.py:277
  59.4 0.0 collective-permute-done.1.tail_ref
  59.4 0.0 copy-done.4
  59.4 1.8 %norm_conv.3 = bf16[8,256,128]{2,1,0:T(8,128)(2,1)S(1)} custom-call(f32[32,1,128]{2,1,0:T(1,128)S(1)} %all_to_all.21.sums_ref, bf16[256,128]{1,0:T(8,128)(2,1)S(1)} %get-tuple-element.16.own_ref, bf16[256,128]{1,0:T(8,128)(2,1)S(1)} %collective-permute-done.1.tail_ref, f32[8,128]{1,0:T(8,128)S(1)} %get-tuple-element.13.params_ref, ...), custom_call_target="tpu_custom_call" | custom-call | flops 905969664 | bytes 3145728 | tf_op jit(solution)/shard_map/norm_conv/pallas_call | solution.py:220
  61.2 11.6 %all_to_all.22.parts_ref = bf16[8,256,128]{2,1,0:T(8,128)(2,1)S(1)} all-to-all(bf16[8,256,128]{2,1,0:T(8,128)(2,1)S(1)} %norm_conv.3), channel_id=1, replica_groups=mesh['tm'=32,'chan'=8] {'chan'}, dimensions={0} | all-to-all | bytes 1048576 | tf_op jit(solution)/shard_map/all_to_all | solution.py:235
  72.7 0.8 %last.1 = f32[64,2,256]{2,1,0:T(2,128)} custom-call(bf16[8,256,128]{2,1,0:T(8,128)(2,1)S(1)} %all_to_all.22.parts_ref, f32[8,128]{1,0:T(8,128)S(1)} %get-tuple-element.13.params_ref, bf16[256,128]{1,0:T(8,128)(2,1)S(1)} %get-tuple-element.12.after_ref.own_ref.packed_ref), custom_call_target="tpu_custom_call" | custom-call | tf_op jit(solution)/shard_map/last/pallas_call | solution.py:280
  (2 shorter events, 0.0 us)
Async XLA Ops:
  0.0 0.8 %copy-start.2 = (bf16[64,2,256]{2,1,0:T(2,128)(2,1)S(1)}, bf16[64,2,256]{2,1,0:T(2,128)(2,1)}, u32[]{:S(2)}) copy-start(bf16[64,2,256]{2,1,0:T(2,128)(2,1)} %x_hbm.1) | copy-start | bytes 196612
  2.0 23.2 %collective-permute-start = (bf16[256,128]{1,0:T(8,128)(2,1)S(1)}, bf16[256,128]{1,0:T(8,128)(2,1)S(1)}, u32[]{:S(2)}, u32[]{:S(2)}) collective-permute-start(bf16[256,128]{1,0:T(8,128)(2,1)S(1)} %get-tuple-element.12.after_ref.own_ref.packed_ref), channel_id=1, source_target_pairs={{0,8},{8,16},{16,24},{24,32},{32,40},{40,48},{48,56},{56,64},{64,7... | collective-permute-start | bytes 196616 | tf_op jit(solution)/shard_map/ppermute | solution.py:32
  4.8 20.4 %all-to-all-start = ((f32[32,1,128]{2,1,0:T(1,128)}), f32[32,1,128]{2,1,0:T(1,128)S(1)}, u32[]{:S(2)}, u32[]{:S(2)}) async-start(f32[32,1,128]{2,1,0:T(1,128)} %get-tuple-element.11), calls=%async_computation | async-start | bytes 32768 | tf_op jit(solution)/shard_map/all_to_all | solution.py:256
  16.7 1.5 %copy-start = (bf16[64,27,512]{2,0,1:T(8,128)(2,1)S(1)}, bf16[64,27,512]{2,0,1:T(8,128)(2,1)}, u32[]{:S(2)}) copy-start(bf16[64,27,512]{2,0,1:T(8,128)(2,1)} %param.14) | copy-start | bytes 5308420
  18.2 0.7 copy-start.3
  18.8 6.4 %copy-start.1 = (bf16[64,27,512]{2,0,1:T(8,128)(2,1)S(1)}, bf16[64,27,512]{2,0,1:T(8,128)(2,1)}, u32[]{:S(2)}) copy-start(bf16[64,27,512]{2,0,1:T(8,128)(2,1)} %param.14) | copy-start | bytes 5308420
  25.2 34.2 %copy-start.4 = (bf16[64,27,512]{2,0,1:T(8,128)(2,1)S(1)}, bf16[64,27,512]{2,0,1:T(8,128)(2,1)}, u32[]{:S(2)}) copy-start(bf16[64,27,512]{2,0,1:T(8,128)(2,1)} %param.18) | copy-start | bytes 5308420
  40.9 18.5 %collective-permute-start.1 = (bf16[256,128]{1,0:T(8,128)(2,1)S(1)}, bf16[256,128]{1,0:T(8,128)(2,1)S(1)}, u32[]{:S(2)}, u32[]{:S(2)}) collective-permute-start(bf16[256,128]{1,0:T(8,128)(2,1)S(1)} %get-tuple-element.16.own_ref), channel_id=1, source_target_pairs={{0,8},{8,16},{16,24},{24,32},{32,40},{40,48},{48,56},{56,64},{64,7... | collective-permute-start | bytes 196616 | tf_op jit(solution)/shard_map/ppermute | solution.py:32

commit v4 on v3

--- a/solution.py
+++ b/solution.py
@@ -110,7 +110,7 @@
     device = lax.broadcasted_iota(jnp.int32, (count, 1, LANES), 0)
     half = (lax.broadcasted_iota(jnp.int32, (count, 1, LANES), 2) >= CHANS).astype(jnp.int32)
     frame_of = 2 * device + half
-    sums = sums_ref[...]
+    sums = sums_ref[:, 0:1, :]
     is_sum = holds_sum((1, LANES))
     stats = []
     for start, end in ((start_zero, end_zero), (start_one, end_one)):
@@ -241,7 +241,7 @@
     count = lax.axis_size("tm")
     first = (lax.axis_index("tm") * 2).astype(jnp.int32).reshape(1)
     packed_shape = shape_of((CELLS, LANES), jnp.bfloat16)
-    sums_shape = shape_of((count, 1, LANES), jnp.float32)
+    sums_shape = shape_of((count, 4, LANES), jnp.float32)
     flat_one = jnp.transpose(w_one, (1, 0, 2)).reshape(ROWS, C)
     flat_two = jnp.transpose(w_two, (1, 0, 2)).reshape(ROWS, C)
     packed, sums = pl.pallas_call(
@@ -253,8 +253,8 @@
         compiler_params=SMALL,
         name="pack",
     )(clip_input)
+    tail = ring_shift(packed, "tm", 1)
     everyone = lax.all_to_all(sums, "tm", 0, 0, tiled=True)
-    tail = ring_shift(packed, "tm", 1)
     affine = (gamma_one, beta_one, bias_one, gamma_two, beta_two, bias_two, gamma_two, beta_two)
     params, clips = pl.pallas_call(
         prepare_kernel,
@@ -274,8 +274,8 @@
         compiler_params=SMALL,
         name="middle",
     )(parts, params)
+    tail = ring_shift(y_one, "tm", 1)
     everyone = lax.all_to_all(sums, "tm", 0, 0, tiled=True)
-    tail = ring_shift(y_one, "tm", 1)
     parts = normed_conv(3, tail, y_one, everyone, params, clips, flat_two)
     return pl.pallas_call(
         last_kernel,

time: 73.9 us -> 74.1 us (level)
  blocking collectives: 41.4 us -> 25.1 us
  starting transfers between devices: 15.9 us -> 23.2 us
  waiting for transfers between devices: 5.77 us -> 12.9 us
  local copies, waits for them, and re-layouts: 3.77 us -> 5.23 us
    all_to_all x1 -> x0, blocking collectives: 16.4 us -> none  [on_device(): everyone = lax.all_to_all(sums, 'tm', 0, 0, tiled=True)]
    all_to_all x1 -> x2, starting transfers between devices: 11.1 us -> 19.8 us  [on_device(): everyone = lax.all_to_all(sums, 'tm', 0, 0, tiled=True)]
    all_to_all x1 -> x2, waiting for transfers between devices: 5.76 us -> 11.5 us  [on_device(): everyone = lax.all_to_all(sums, 'tm', 0, 0, tiled=True)]
    unnamed x10, local copies, waits for them, and re-layouts: 2.97 us -> 4.44 us
    ppermute x2, starting transfers between devices: 4.85 us -> 3.42 us  [ring_shift(): lax.ppermute(value, axis, [(source, (source + steps) % count) for source...]
    ppermute x2, waiting for transfers between devices: 0.01 us -> 1.33 us  [ring_shift(): lax.ppermute(value, axis, [(source, (source + steps) % count) for source...]
  transfers between devices with their start and end apart: 3 -> 4, of which waited for: 1 -> 3; matrix products, arithmetic and copies ran while one was open for 1% -> 1% of each run, Pallas kernels for 1% -> 1%
where the time goes in v4:
time: 74.1 us; the launch traced here: 73.7 us
  blocking collectives  25.1 us (34%)
  starting transfers between devices  23.2 us (31%)
  waiting for transfers between devices  12.9 us (17%)
  Pallas kernels  7.26 us (10%)
  local copies, waits for them, and re-layouts  5.23 us (7%)
    all_to_all x2, blocking collectives, normed_conv(): return lax.all_to_all(partial, 'chan', 0, 0, tiled=True)  25.1 us
    all_to_all x2, starting transfers between devices, on_device(): everyone = lax.all_to_all(sums, 'tm', 0, 0, tiled=True)  19.8 us
    all_to_all x2, waiting for transfers between devices, on_device(): everyone = lax.all_to_all(sums, 'tm', 0, 0, tiled=True)  11.5 us
    unnamed x10, local copies, waits for them, and re-layouts  4.44 us
    pallas_call x2, Pallas kernels, normed_conv(): pl.pallas_call(functools.partial(conv_kernel, at), out_shape=shape_of((pa...  3.57 us
    ppermute x2, starting transfers between devices, ring_shift(): lax.ppermute(value, axis, [(source, (source + steps) % count) for source...  3.42 us
  transfers between devices with their start and end apart: 4, of which 3 were waited for; matrix products, arithmetic and copies ran while one was open for 1% of the time, Pallas kernels for 1%

profile of v4, /device:TPU:1, one launch (start us, length us, event | category | flops | bytes accessed | tf_op | source)
XLA Modules:
  0.0 73.7 jit_solution(14922297804199775186)
XLA Ops:
  0.0 0.0 copy-start.2
  0.0 0.8 %copy-done.2 = bf16[64,2,256]{2,1,0:T(2,128)(2,1)S(1)} copy-done((bf16[64,2,256]{2,1,0:T(2,128)(2,1)S(1)}, bf16[64,2,256]{2,1,0:T(2,128)(2,1)}, u32[]{:S(2)}) %copy-start.2) | copy-done | bytes 65560
  0.8 1.2 %pack.1 = (bf16[256,128]{1,0:T(8,128)(2,1)S(1)}, f32[32,4,128]{2,1,0:T(4,128)}) custom-call(bf16[64,2,256]{2,1,0:T(2,128)(2,1)S(1)} %copy-done.2), custom_call_target="tpu_custom_call" | custom-call | tf_op jit(solution)/shard_map/pack/pallas_call | solution.py:247
  2.1 12.8 %all-to-all-start = ((f32[32,4,128]{2,1,0:T(4,128)}), f32[32,4,128]{2,1,0:T(4,128)S(1)}, u32[]{:S(2)}, u32[]{:S(2)}) async-start(f32[32,4,128]{2,1,0:T(4,128)} %get-tuple-element.11), calls=%async_computation | async-start | bytes 131072 | tf_op jit(solution)/shard_map/all_to_all | solution.py:257
  14.8 1.7 %collective-permute-start = (bf16[256,128]{1,0:T(8,128)(2,1)S(1)}, bf16[256,128]{1,0:T(8,128)(2,1)S(1)}, u32[]{:S(2)}, u32[]{:S(2)}) collective-permute-start(bf16[256,128]{1,0:T(8,128)(2,1)S(1)} %get-tuple-element.12.after_ref.own_ref.packed_ref), channel_id=1, source_target_pairs={{0,8},{8,16},{16,24},{24,32},{32,40},{40,48},{48,56},{56,64},{64,7... | collective-permute-start | bytes 196616 | tf_op jit(solution)/shard_map/ppermute | solution.py:32
  16.6 0.8 %stack.29.affine_ref = f32[8,64]{1,0:T(8,128)S(1)} concatenate(f32[1,64]{1,0:T(1,128)} %bitcast.20, f32[1,64]{1,0:T(1,128)} %bitcast.21, f32[1,64]{1,0:T(1,128)} %bitcast.22, f32[1,64]{1,0:T(1,128)} %bitcast.16, f32[1,64]{1,0:T(1,128)} %bitcast.18, f32[1,64]{1,0:T(1,128)} %bitcast.23, f32[1,64]{1,0:T(1,128)} %bitcast.17, f32[1,64]{1,0:T(1,128)} %bitcast.19), dimensions={0} | concatenate | bytes 4096 | tf_op jit(solution)/shard_map/stack | solution.py:267
  17.4 1.5 %copy-done = bf16[64,27,512]{2,0,1:T(8,128)(2,1)S(1)} copy-done((bf16[64,27,512]{2,0,1:T(8,128)(2,1)S(1)}, bf16[64,27,512]{2,0,1:T(8,128)(2,1)}, u32[]{:S(2)}) %copy-start) | copy-done | bytes 1769496
  18.8 0.0 copy-start.3
  18.8 0.7 copy-done.3
  19.5 0.6 prepare.1
  20.1 0.0 collective-permute-done.tail_ref
  20.1 4.7 %all-to-all-done.sums_ref = f32[32,4,128]{2,1,0:T(4,128)S(1)} async-done(((f32[32,4,128]{2,1,0:T(4,128)}), f32[32,4,128]{2,1,0:T(4,128)S(1)}, u32[]{:S(2)}, u32[]{:S(2)}) %all-to-all-start) | async-done | bytes 65568 | tf_op jit(solution)/shard_map/all_to_all | solution.py:257
  24.8 0.0 copy-done.1
  24.8 1.8 %norm_conv.2 = bf16[8,256,128]{2,1,0:T(8,128)(2,1)S(1)} custom-call(f32[32,4,128]{2,1,0:T(4,128)S(1)} %all-to-all-done.sums_ref, bf16[256,128]{1,0:T(8,128)(2,1)S(1)} %get-tuple-element.12.after_ref.own_ref.packed_ref, bf16[256,128]{1,0:T(8,128)(2,1)S(1)} %collective-permute-done.tail_ref, f32[8,128]{1,0:T(8,128)S(1)} %get-tuple-element.13.params_ref, ...), custom_call_target="tpu_custom_call" | custom-call | flops 905969664 | bytes 3145728 | tf_op jit(solution)/shard_map/norm_conv/pallas_call | solution.py:220
  26.6 13.4 %all_to_all.20.parts_ref = bf16[8,256,128]{2,1,0:T(8,128)(2,1)S(1)} all-to-all(bf16[8,256,128]{2,1,0:T(8,128)(2,1)S(1)} %norm_conv.2), channel_id=1, replica_groups=mesh['tm'=32,'chan'=8] {'chan'}, dimensions={0} | all-to-all | bytes 1048576 | tf_op jit(solution)/shard_map/all_to_all | solution.py:235
  40.0 1.0 %middle.1 = (bf16[256,128]{1,0:T(8,128)(2,1)S(1)}, f32[32,4,128]{2,1,0:T(4,128)}) custom-call(bf16[8,256,128]{2,1,0:T(8,128)(2,1)S(1)} %all_to_all.20.parts_ref, f32[8,128]{1,0:T(8,128)S(1)} %get-tuple-element.13.params_ref), custom_call_target="tpu_custom_call" | custom-call | tf_op jit(solution)/shard_map/middle/pallas_call | solution.py:269
  41.0 7.1 %all-to-all-start.2 = ((f32[32,4,128]{2,1,0:T(4,128)}), f32[32,4,128]{2,1,0:T(4,128)S(1)}, u32[]{:S(2)}, u32[]{:S(2)}) async-start(f32[32,4,128]{2,1,0:T(4,128)} %get-tuple-element.15), calls=%async_computation.2 | async-start | bytes 131072 | tf_op jit(solution)/shard_map/all_to_all | solution.py:278
  48.1 1.7 %collective-permute-start.1 = (bf16[256,128]{1,0:T(8,128)(2,1)S(1)}, bf16[256,128]{1,0:T(8,128)(2,1)S(1)}, u32[]{:S(2)}, u32[]{:S(2)}) collective-permute-start(bf16[256,128]{1,0:T(8,128)(2,1)S(1)} %get-tuple-element.16.own_ref), channel_id=1, source_target_pairs={{0,8},{8,16},{16,24},{24,32},{32,40},{40,48},{48,56},{56,64},{64,7... | collective-permute-start | bytes 196616 | tf_op jit(solution)/shard_map/ppermute | solution.py:32
  49.8 1.3 %collective-permute-done.1.tail_ref = bf16[256,128]{1,0:T(8,128)(2,1)S(1)} collective-permute-done((bf16[256,128]{1,0:T(8,128)(2,1)S(1)}, bf16[256,128]{1,0:T(8,128)(2,1)S(1)}, u32[]{:S(2)}, u32[]{:S(2)}) %collective-permute-start.1) | collective-permute-done | bytes 65568 | tf_op jit(solution)/shard_map/ppermute | solution.py:32
  51.1 6.8 %all-to-all-done.2.sums_ref = f32[32,4,128]{2,1,0:T(4,128)S(1)} async-done(((f32[32,4,128]{2,1,0:T(4,128)}), f32[32,4,128]{2,1,0:T(4,128)S(1)}, u32[]{:S(2)}, u32[]{:S(2)}) %all-to-all-start.2) | async-done | bytes 65568 | tf_op jit(solution)/shard_map/all_to_all | solution.py:278
  58.0 1.5 %copy-done.4 = bf16[64,27,512]{2,0,1:T(8,128)(2,1)S(1)} copy-done((bf16[64,27,512]{2,0,1:T(8,128)(2,1)S(1)}, bf16[64,27,512]{2,0,1:T(8,128)(2,1)}, u32[]{:S(2)}) %copy-start.4) | copy-done | bytes 1769496
  59.4 1.8 %norm_conv.3 = bf16[8,256,128]{2,1,0:T(8,128)(2,1)S(1)} custom-call(f32[32,4,128]{2,1,0:T(4,128)S(1)} %all-to-all-done.2.sums_ref, bf16[256,128]{1,0:T(8,128)(2,1)S(1)} %get-tuple-element.16.own_ref, bf16[256,128]{1,0:T(8,128)(2,1)S(1)} %collective-permute-done.1.tail_ref, f32[8,128]{1,0:T(8,128)S(1)} %get-tuple-element.13.params_ref, ...), custom_call_target="tpu_custom_call" | custom-call | flops 905969664 | bytes 3145728 | tf_op jit(solution)/shard_map/norm_conv/pallas_call | solution.py:220
  61.2 11.7 %all_to_all.21.parts_ref = bf16[8,256,128]{2,1,0:T(8,128)(2,1)S(1)} all-to-all(bf16[8,256,128]{2,1,0:T(8,128)(2,1)S(1)} %norm_conv.3), channel_id=1, replica_groups=mesh['tm'=32,'chan'=8] {'chan'}, dimensions={0} | all-to-all | bytes 1048576 | tf_op jit(solution)/shard_map/all_to_all | solution.py:235
  72.9 0.8 %last.1 = f32[64,2,256]{2,1,0:T(2,128)} custom-call(bf16[8,256,128]{2,1,0:T(8,128)(2,1)S(1)} %all_to_all.21.parts_ref, f32[8,128]{1,0:T(8,128)S(1)} %get-tuple-element.13.params_ref, bf16[256,128]{1,0:T(8,128)(2,1)S(1)} %get-tuple-element.12.after_ref.own_ref.packed_ref), custom_call_target="tpu_custom_call" | custom-call | tf_op jit(solution)/shard_map/last/pallas_call | solution.py:280
  (3 shorter events, 0.0 us)
Async XLA Ops:
  0.0 0.8 %copy-start.2 = (bf16[64,2,256]{2,1,0:T(2,128)(2,1)S(1)}, bf16[64,2,256]{2,1,0:T(2,128)(2,1)}, u32[]{:S(2)}) copy-start(bf16[64,2,256]{2,1,0:T(2,128)(2,1)} %x_hbm.1) | copy-start | bytes 196612
  2.1 22.7 %all-to-all-start = ((f32[32,4,128]{2,1,0:T(4,128)}), f32[32,4,128]{2,1,0:T(4,128)S(1)}, u32[]{:S(2)}, u32[]{:S(2)}) async-start(f32[32,4,128]{2,1,0:T(4,128)} %get-tuple-element.11), calls=%async_computation | async-start | bytes 131072 | tf_op jit(solution)/shard_map/all_to_all | solution.py:257
  14.8 5.2 %collective-permute-start = (bf16[256,128]{1,0:T(8,128)(2,1)S(1)}, bf16[256,128]{1,0:T(8,128)(2,1)S(1)}, u32[]{:S(2)}, u32[]{:S(2)}) collective-permute-start(bf16[256,128]{1,0:T(8,128)(2,1)S(1)} %get-tuple-element.12.after_ref.own_ref.packed_ref), channel_id=1, source_target_pairs={{0,8},{8,16},{16,24},{24,32},{32,40},{40,48},{48,56},{56,64},{64,7... | collective-permute-start | bytes 196616 | tf_op jit(solution)/shard_map/ppermute | solution.py:32
  17.3 1.5 %copy-start = (bf16[64,27,512]{2,0,1:T(8,128)(2,1)S(1)}, bf16[64,27,512]{2,0,1:T(8,128)(2,1)}, u32[]{:S(2)}) copy-start(bf16[64,27,512]{2,0,1:T(8,128)(2,1)} %param.14) | copy-start | bytes 5308420
  18.8 0.7 copy-start.3
  19.5 5.3 %copy-start.1 = (bf16[64,27,512]{2,0,1:T(8,128)(2,1)S(1)}, bf16[64,27,512]{2,0,1:T(8,128)(2,1)}, u32[]{:S(2)}) copy-start(bf16[64,27,512]{2,0,1:T(8,128)(2,1)} %param.14) | copy-start | bytes 5308420
  41.0 16.9 %all-to-all-start.2 = ((f32[32,4,128]{2,1,0:T(4,128)}), f32[32,4,128]{2,1,0:T(4,128)S(1)}, u32[]{:S(2)}, u32[]{:S(2)}) async-start(f32[32,4,128]{2,1,0:T(4,128)} %get-tuple-element.15), calls=%async_computation.2 | async-start | bytes 131072 | tf_op jit(solution)/shard_map/all_to_all | solution.py:278
  48.1 3.0 %collective-permute-start.1 = (bf16[256,128]{1,0:T(8,128)(2,1)S(1)}, bf16[256,128]{1,0:T(8,128)(2,1)S(1)}, u32[]{:S(2)}, u32[]{:S(2)}) collective-permute-start(bf16[256,128]{1,0:T(8,128)(2,1)S(1)} %get-tuple-element.16.own_ref), channel_id=1, source_target_pairs={{0,8},{8,16},{16,24},{24,32},{32,40},{40,48},{48,56},{56,64},{64,7... | collective-permute-start | bytes 196616 | tf_op jit(solution)/shard_map/ppermute | solution.py:32
  58.0 1.5 %copy-start.4 = (bf16[64,27,512]{2,0,1:T(8,128)(2,1)S(1)}, bf16[64,27,512]{2,0,1:T(8,128)(2,1)}, u32[]{:S(2)}) copy-start(bf16[64,27,512]{2,0,1:T(8,128)(2,1)} %param.18) | copy-start | bytes 5308420

commit v5 on v4

--- a/solution.py
+++ b/solution.py
@@ -1,5 +1,3 @@
-import functools
-
 import jax
 import jax.numpy as jnp
 from jax import lax
@@ -87,11 +85,13 @@
     return start, end
 
 
-def prepare_kernel(
-    lengths_ref, first_ref, after_ref, weight_ref, affine_ref, params_ref, clips_ref
-):
+def prepare_kernel(after_ref, weight_ref, affine_ref, params_ref):
     del after_ref, weight_ref
     params_ref[...] = both_halves(affine_ref[...])
+
+
+def clips_kernel(lengths_ref, first_ref, after_ref, clips_ref):
+    del after_ref
     frame = first_ref[0]
     start_zero, end_zero = clip_bounds(lengths_ref, frame)
     start_one, end_one = clip_bounds(lengths_ref, frame + 1)
@@ -100,7 +100,7 @@
 
 
 def conv_kernel(
-    at, sums_ref, own_ref, tail_ref, params_ref, clips_ref, w_ref, out_ref, slots_ref, cols_ref
+    sums_ref, own_ref, tail_ref, params_ref, clips_ref, w_ref, out_ref, slots_ref, cols_ref
 ):
     clips = clips_ref[...]
     start_zero, end_zero = clips[0:1, :], clips[1:2, :]
@@ -121,8 +121,8 @@
         mean = jnp.where(is_sum, row, pltpu.roll(row, GROUP_SIZE // 2, 1))
         second = jnp.where(is_sum, pltpu.roll(row, LANES - GROUP_SIZE // 2, 1), row)
         stats.append((mean, lax.rsqrt(second - mean * mean + EPS)))
-    gamma = params_ref[at : at + 1, :]
-    beta = params_ref[at + 1 : at + 2, :]
+    gamma = params_ref[0:1, :]
+    beta = params_ref[1:2, :]
     left_row = left_half((1, LANES))
     mean_tail, scale_tail = stats[0]
     mean_own = jnp.where(left_row, stats[0][0], stats[1][0])
@@ -205,7 +205,7 @@
 
 
 def last_kernel(parts_ref, params_ref, packed_ref, out_ref):
-    value = sum_partials(parts_ref, params_ref[5:6, :]) + packed_ref[...].astype(jnp.float32)
+    value = sum_partials(parts_ref, params_ref[2:3, :]) + packed_ref[...].astype(jnp.float32)
     rows = value.T
     out_ref[:, 0, :] = rows[:CHANS]
     out_ref[:, 1, :] = rows[CHANS:]
@@ -215,10 +215,22 @@
     return jax.ShapeDtypeStruct(shape, dtype)
 
 
-def normed_conv(at, tail, packed, sums, params, clips, weight):
+def prepare(after, weight, gamma, beta, bias):
+    return pl.pallas_call(
+        prepare_kernel,
+        out_shape=shape_of((4, LANES), jnp.float32),
+        in_specs=[VMEM, VMEM, VMEM],
+        out_specs=VMEM,
+        compiler_params=SMALL,
+        cost_estimate=pl.CostEstimate(flops=10000, bytes_accessed=2 << 20, transcendentals=0),
+        name="prepare",
+    )(after, weight, jnp.stack((gamma, beta, bias, bias)))
+
+
+def normed_conv(tail, packed, sums, params, clips, weight):
     parts = C // CHANS
     partial = pl.pallas_call(
-        functools.partial(conv_kernel, at),
+        conv_kernel,
         out_shape=shape_of((parts, CELLS, LANES), jnp.bfloat16),
         in_specs=[VMEM, VMEM, VMEM, VMEM, VMEM, VMEM],
         out_specs=VMEM,
@@ -255,17 +267,17 @@
     )(clip_input)
     tail = ring_shift(packed, "tm", 1)
     everyone = lax.all_to_all(sums, "tm", 0, 0, tiled=True)
-    affine = (gamma_one, beta_one, bias_one, gamma_two, beta_two, bias_two, gamma_two, beta_two)
-    params, clips = pl.pallas_call(
-        prepare_kernel,
-        out_shape=(shape_of((8, LANES), jnp.float32), shape_of((8, LANES), jnp.int32)),
-        in_specs=[SMEM, SMEM, VMEM, VMEM, VMEM],
-        out_specs=(VMEM, VMEM),
-        compiler_params=SMALL,
-        cost_estimate=pl.CostEstimate(flops=10000, bytes_accessed=2 << 20, transcendentals=0),
-        name="prepare",
-    )(lengths, first, packed, flat_one, jnp.stack(affine))
-    parts = normed_conv(0, tail, packed, everyone, params, clips, flat_one)
+    clips = pl.pallas_call(
+        clips_kernel,
+        out_shape=shape_of((8, LANES), jnp.int32),
+        in_specs=[SMEM, SMEM, VMEM],
+        out_specs=VMEM,
+        compiler_params=SMALL,
+        cost_estimate=pl.CostEstimate(flops=10000, bytes_accessed=1 << 20, transcendentals=0),
+        name="clips",
+    )(lengths, first, packed)
+    params = prepare(packed, flat_one, gamma_one, beta_one, bias_one)
+    parts = normed_conv(tail, packed, everyone, params, clips, flat_one)
     y_one, sums = pl.pallas_call(
         middle_kernel,
         out_shape=(packed_shape, sums_shape),
@@ -276,7 +288,8 @@
     )(parts, params)
     tail = ring_shift(y_one, "tm", 1)
     everyone = lax.all_to_all(sums, "tm", 0, 0, tiled=True)
-    parts = normed_conv(3, tail, y_one, everyone, params, clips, flat_two)
+    params = prepare(y_one, flat_two, gamma_two, beta_two, bias_two)
+    parts = normed_conv(tail, y_one, everyone, params, clips, flat_two)
     return pl.pallas_call(
         last_kernel,
         out_shape=shape_of(clip_input.shape, jnp.float32),

time: 74.1 us -> 74.5 us (level)
  Pallas kernels: 7.26 us -> 10.4 us
  local copies, waits for them, and re-layouts: 5.23 us -> 2.34 us
  other arithmetic: 0 us -> 1.41 us
  waiting for transfers between devices: 12.9 us -> 11.5 us
    pallas_call x3 -> x5, Pallas kernels: 4.18 us -> 6.48 us  [the longest x2 4.45 us: normed_conv(): pl.pallas_call(conv_kernel, out_shape=shape_of((parts, CELLS, LANES), jnp...]
    unnamed x10 -> x14, local copies, waits for them, and re-layouts: 4.44 us -> 2.34 us
    another operation x0 -> x2, other arithmetic: none -> 1.41 us  [prepare(): jnp.stack((gamma, beta, bias, bias))]
    pallas_call x1, Pallas kernels: 0.81 us -> 1.65 us  [on_device(): pl.pallas_call(last_kernel, out_shape=shape_of(clip_input.shape, jnp.floa...]
    another operation x1 -> x0, local copies, waits for them, and re-layouts: 0.79 us -> none  [on_device(): jnp.stack(affine)]
    ppermute x2, waiting for transfers between devices: 1.33 us -> 0.59 us  [ring_shift(): lax.ppermute(value, axis, [(source, (source + steps) % count) for source...]
  transfers between devices with their start and end apart: 4 -> 4, of which waited for: 3 -> 3; matrix products, arithmetic and copies ran while one was open for 1% -> 2% of each run, Pallas kernels for 1% -> 3%
where the time goes in v5:
time: 74.5 us; the launch traced here: 74 us
  blocking collectives  25 us (34%)
  starting transfers between devices  23.3 us (31%)
  waiting for transfers between devices  11.5 us (15%)
  Pallas kernels  10.4 us (14%)
  local copies, waits for them, and re-layouts  2.34 us (3%)
  other arithmetic  1.41 us (2%)
    all_to_all x2, blocking collectives, normed_conv(): return lax.all_to_all(partial, 'chan', 0, 0, tiled=True)  25 us
    all_to_all x2, starting transfers between devices, on_device(): everyone = lax.all_to_all(sums, 'tm', 0, 0, tiled=True)  19.9 us
    all_to_all x2, waiting for transfers between devices, on_device(): everyone = lax.all_to_all(sums, 'tm', 0, 0, tiled=True)  10.9 us
    pallas_call x2, Pallas kernels, normed_conv(): pl.pallas_call(conv_kernel, out_shape=shape_of((parts, CELLS, LANES), jnp...  4.45 us
    ppermute x2, starting transfers between devices, ring_shift(): lax.ppermute(value, axis, [(source, (source + steps) % count) for source...  3.42 us
    unnamed x14, local copies, waits for them, and re-layouts  2.34 us
    pallas_call x1, Pallas kernels, on_device(): pl.pallas_call(last_kernel, out_shape=shape_of(clip_input.shape, jnp.floa...  1.65 us
  transfers between devices with their start and end apart: 4, of which 3 were waited for; matrix products, arithmetic and copies ran while one was open for 2% of the time, Pallas kernels for 3%

profile of v5, /device:TPU:1, one launch (start us, length us, event | category | flops | bytes accessed | tf_op | source)
XLA Modules:
  0.0 74.0 jit_solution(6919378189853703341)
XLA Ops:
  0.0 0.8 %copy-done.3 = bf16[64,2,256]{2,1,0:T(2,128)(2,1)S(1)} copy-done((bf16[64,2,256]{2,1,0:T(2,128)(2,1)S(1)}, bf16[64,2,256]{2,1,0:T(2,128)(2,1)}, u32[]{:S(2)}) %copy-start.3) | copy-done | bytes 65560
  0.8 1.2 %pack.1 = (bf16[256,128]{1,0:T(8,128)(2,1)}, f32[32,4,128]{2,1,0:T(4,128)}) custom-call(bf16[64,2,256]{2,1,0:T(2,128)(2,1)S(1)} %copy-done.3), custom_call_target="tpu_custom_call" | custom-call | tf_op jit(solution)/shard_map/pack/pallas_call | solution.py:259
  2.1 12.8 %all-to-all-start = ((f32[32,4,128]{2,1,0:T(4,128)}), f32[32,4,128]{2,1,0:T(4,128)}, u32[]{:S(2)}, u32[]{:S(2)}) async-start(f32[32,4,128]{2,1,0:T(4,128)} %get-tuple-element.9), calls=%async_computation | async-start | bytes 131072 | tf_op jit(solution)/shard_map/all_to_all | solution.py:269
  14.9 1.7 %collective-permute-start = (bf16[256,128]{1,0:T(8,128)(2,1)}, bf16[256,128]{1,0:T(8,128)(2,1)}, u32[]{:S(2)}, u32[]{:S(2)}) collective-permute-start(bf16[256,128]{1,0:T(8,128)(2,1)} %get-tuple-element.10.after_ref.own_ref.packed_ref), channel_id=1, source_target_pairs={{0,8},{8,16},{16,24},{24,32},{32,40},{40,48},{48,56},{56,64},{64,7... | collective-permute-start | bytes 196616 | tf_op jit(solution)/shard_map/ppermute | solution.py:30
  16.6 0.7 %pad_maximum_fusion.affine_ref = f32[4,64]{1,0:T(4,128)S(1)} fusion(f32[1,64]{1,0:T(1,128)} %bitcast.17, f32[1,64]{1,0:T(1,128)} %bitcast.18, f32[1,64]{1,0:T(1,128)} %bitcast.19), kind=kLoop, calls=%fused_computation | loop fusion | flops 768 | bytes 1792 | tf_op jit(solution)/shard_map/stack | solution.py:227
  17.4 0.0 copy-start
  17.4 1.5 %copy-done = bf16[64,27,512]{2,0,1:T(8,128)(2,1)S(1)} copy-done((bf16[64,27,512]{2,0,1:T(8,128)(2,1)S(1)}, bf16[64,27,512]{2,0,1:T(8,128)(2,1)}, u32[]{:S(2)}) %copy-start) | copy-done | bytes 1769496
  18.8 1.0 %prepare.2.params_ref = f32[4,128]{1,0:T(4,128)S(1)} custom-call(bf16[256,128]{1,0:T(8,128)(2,1)} %get-tuple-element.10.after_ref.own_ref.packed_ref, bf16[1728,512]{1,0:T(8,128)(2,1)S(1)} %bitcast.13, f32[4,64]{1,0:T(4,128)S(1)} %pad_maximum_fusion.affine_ref), custom_call_target="tpu_custom_call" | custom-call | flops 10000 | bytes 2097152 | tf_op jit(solution)/shard_map/prepare/pallas_call | solution.py:219
  19.9 0.9 %clips.1.clips_ref = s32[8,128]{1,0:T(8,128)S(1)} custom-call(s32[16]{0:T(128)S(1)} %copy-done.4, s32[1]{0:T(128)} %bitcast.5.first_ref, bf16[256,128]{1,0:T(8,128)(2,1)} %get-tuple-element.10.after_ref.own_ref.packed_ref), custom_call_target="tpu_custom_call" | custom-call | flops 10000 | bytes 1048576 | tf_op jit(solution)/shard_map/clips/pallas_call | solution.py:270
  20.8 0.0 copy-start.5
  20.8 0.0 copy-start.6
  20.9 4.1 %all-to-all-done.sums_ref = f32[32,4,128]{2,1,0:T(4,128)} async-done(((f32[32,4,128]{2,1,0:T(4,128)}), f32[32,4,128]{2,1,0:T(4,128)}, u32[]{:S(2)}, u32[]{:S(2)}) %all-to-all-start) | async-done | bytes 65568 | tf_op jit(solution)/shard_map/all_to_all | solution.py:269
  24.9 2.7 %norm_conv.2 = bf16[8,256,128]{2,1,0:T(8,128)(2,1)S(1)} custom-call(f32[32,4,128]{2,1,0:T(4,128)} %all-to-all-done.sums_ref, bf16[256,128]{1,0:T(8,128)(2,1)} %get-tuple-element.10.after_ref.own_ref.packed_ref, bf16[256,128]{1,0:T(8,128)(2,1)} %collective-permute-done.tail_ref, f32[4,128]{1,0:T(4,128)S(1)} %prepare.2.params_ref, ...), custom_call_target="tpu_custom_call" | custom-call | flops 905969664 | bytes 3145728 | tf_op jit(solution)/shard_map/norm_conv/pallas_call | solution.py:232
  27.6 13.3 %all_to_all.20.parts_ref = bf16[8,256,128]{2,1,0:T(8,128)(2,1)S(1)} all-to-all(bf16[8,256,128]{2,1,0:T(8,128)(2,1)S(1)} %norm_conv.2), channel_id=1, replica_groups=mesh['tm'=32,'chan'=8] {'chan'}, dimensions={0} | all-to-all | bytes 1048576 | tf_op jit(solution)/shard_map/all_to_all | solution.py:247
  40.9 1.0 %middle.1 = (bf16[256,128]{1,0:T(8,128)(2,1)S(1)}, f32[32,4,128]{2,1,0:T(4,128)}) custom-call(bf16[8,256,128]{2,1,0:T(8,128)(2,1)S(1)} %all_to_all.20.parts_ref, f32[4,128]{1,0:T(4,128)S(1)} %prepare.2.params_ref), custom_call_target="tpu_custom_call" | custom-call | tf_op jit(solution)/shard_map/middle/pallas_call | solution.py:281
  42.0 7.1 %all-to-all-start.2 = ((f32[32,4,128]{2,1,0:T(4,128)}), f32[32,4,128]{2,1,0:T(4,128)S(1)}, u32[]{:S(2)}, u32[]{:S(2)}) async-start(f32[32,4,128]{2,1,0:T(4,128)} %get-tuple-element.11), calls=%async_computation.2 | async-start | bytes 131072 | tf_op jit(solution)/shard_map/all_to_all | solution.py:290
  49.0 1.7 %collective-permute-start.1 = (bf16[256,128]{1,0:T(8,128)(2,1)S(1)}, bf16[256,128]{1,0:T(8,128)(2,1)S(1)}, u32[]{:S(2)}, u32[]{:S(2)}) collective-permute-start(bf16[256,128]{1,0:T(8,128)(2,1)S(1)} %get-tuple-element.12.after_ref.own_ref), channel_id=1, source_target_pairs={{0,8},{8,16},{16,24},{24,32},{32,40},{40,48},{48,56},{56,64},{64,7... | collective-permute-start | bytes 196616 | tf_op jit(solution)/shard_map/ppermute | solution.py:30
  50.7 0.7 pad_maximum_fusion.1.affine_ref
  51.4 0.1 prepare.3.params_ref
  51.5 0.6 collective-permute-done.1.tail_ref
  52.1 6.8 %all-to-all-done.2.sums_ref = f32[32,4,128]{2,1,0:T(4,128)S(1)} async-done(((f32[32,4,128]{2,1,0:T(4,128)}), f32[32,4,128]{2,1,0:T(4,128)S(1)}, u32[]{:S(2)}, u32[]{:S(2)}) %all-to-all-start.2) | async-done | bytes 65568 | tf_op jit(solution)/shard_map/all_to_all | solution.py:290
  58.9 1.8 %norm_conv.3 = bf16[8,256,128]{2,1,0:T(8,128)(2,1)S(1)} custom-call(f32[32,4,128]{2,1,0:T(4,128)S(1)} %all-to-all-done.2.sums_ref, bf16[256,128]{1,0:T(8,128)(2,1)S(1)} %get-tuple-element.12.after_ref.own_ref, bf16[256,128]{1,0:T(8,128)(2,1)S(1)} %collective-permute-done.1.tail_ref, f32[4,128]{1,0:T(4,128)S(1)} %prepare.3.params_ref, ...), custom_call_target="tpu_custom_call" | custom-call | flops 905969664 | bytes 3145728 | tf_op jit(solution)/shard_map/norm_conv/pallas_call | solution.py:232
  60.7 11.7 %all_to_all.21.parts_ref = bf16[8,256,128]{2,1,0:T(8,128)(2,1)S(1)} all-to-all(bf16[8,256,128]{2,1,0:T(8,128)(2,1)S(1)} %norm_conv.3), channel_id=1, replica_groups=mesh['tm'=32,'chan'=8] {'chan'}, dimensions={0} | all-to-all | bytes 1048576 | tf_op jit(solution)/shard_map/all_to_all | solution.py:247
  72.4 1.7 %last.1 = f32[64,2,256]{2,1,0:T(2,128)} custom-call(bf16[8,256,128]{2,1,0:T(8,128)(2,1)S(1)} %all_to_all.21.parts_ref, f32[4,128]{1,0:T(4,128)S(1)} %prepare.3.params_ref, bf16[256,128]{1,0:T(8,128)(2,1)} %get-tuple-element.10.after_ref.own_ref.packed_ref), custom_call_target="tpu_custom_call" | custom-call | tf_op jit(solution)/shard_map/last/pallas_call | solution.py:293
  (10 shorter events, 0.0 us)
Async XLA Ops:
  0.0 0.8 %copy-start.3 = (bf16[64,2,256]{2,1,0:T(2,128)(2,1)S(1)}, bf16[64,2,256]{2,1,0:T(2,128)(2,1)}, u32[]{:S(2)}) copy-start(bf16[64,2,256]{2,1,0:T(2,128)(2,1)} %x_hbm.1) | copy-start | bytes 196612
  0.8 19.0 %copy-start.4 = (s32[16]{0:T(128)S(1)}, s32[16]{0:T(128)}, u32[]{:S(2)}) copy-start(s32[16]{0:T(128)} %lengths_ref.1) | copy-start | bytes 196
  2.1 22.8 %all-to-all-start = ((f32[32,4,128]{2,1,0:T(4,128)}), f32[32,4,128]{2,1,0:T(4,128)}, u32[]{:S(2)}, u32[]{:S(2)}) async-start(f32[32,4,128]{2,1,0:T(4,128)} %get-tuple-element.9), calls=%async_computation | async-start | bytes 131072 | tf_op jit(solution)/shard_map/all_to_all | solution.py:269
  14.9 5.9 %collective-permute-start = (bf16[256,128]{1,0:T(8,128)(2,1)}, bf16[256,128]{1,0:T(8,128)(2,1)}, u32[]{:S(2)}, u32[]{:S(2)}) collective-permute-start(bf16[256,128]{1,0:T(8,128)(2,1)} %get-tuple-element.10.after_ref.own_ref.packed_ref), channel_id=1, source_target_pairs={{0,8},{8,16},{16,24},{24,32},{32,40},{40,48},{48,56},{56,64},{64,7... | collective-permute-start | bytes 196616 | tf_op jit(solution)/shard_map/ppermute | solution.py:30
  17.4 1.5 %copy-start = (bf16[64,27,512]{2,0,1:T(8,128)(2,1)S(1)}, bf16[64,27,512]{2,0,1:T(8,128)(2,1)}, u32[]{:S(2)}) copy-start(bf16[64,27,512]{2,0,1:T(8,128)(2,1)} %param.14) | copy-start | bytes 5308420
  18.8 6.1 %copy-start.1 = (bf16[64,27,512]{2,0,1:T(8,128)(2,1)S(1)}, bf16[64,27,512]{2,0,1:T(8,128)(2,1)}, u32[]{:S(2)}) copy-start(bf16[64,27,512]{2,0,1:T(8,128)(2,1)} %param.14) | copy-start | bytes 5308420
  20.8 29.9 %copy-start.5 = (f32[64]{0:T(128)S(1)}, f32[64]{0:T(128)}, u32[]{:S(2)}) copy-start(f32[64]{0:T(128)} %param.19) | copy-start | bytes 772
  20.8 29.9 %copy-start.6 = (f32[64]{0:T(128)S(1)}, f32[64]{0:T(128)}, u32[]{:S(2)}) copy-start(f32[64]{0:T(128)} %param.17) | copy-start | bytes 772
  20.8 30.6 %copy-start.2 = (bf16[64,27,512]{2,0,1:T(8,128)(2,1)S(1)}, bf16[64,27,512]{2,0,1:T(8,128)(2,1)}, u32[]{:S(2)}) copy-start(bf16[64,27,512]{2,0,1:T(8,128)(2,1)} %param.18) | copy-start | bytes 5308420
  42.0 16.9 %all-to-all-start.2 = ((f32[32,4,128]{2,1,0:T(4,128)}), f32[32,4,128]{2,1,0:T(4,128)S(1)}, u32[]{:S(2)}, u32[]{:S(2)}) async-start(f32[32,4,128]{2,1,0:T(4,128)} %get-tuple-element.11), calls=%async_computation.2 | async-start | bytes 131072 | tf_op jit(solution)/shard_map/all_to_all | solution.py:290
  49.0 3.0 %collective-permute-start.1 = (bf16[256,128]{1,0:T(8,128)(2,1)S(1)}, bf16[256,128]{1,0:T(8,128)(2,1)S(1)}, u32[]{:S(2)}, u32[]{:S(2)}) collective-permute-start(bf16[256,128]{1,0:T(8,128)(2,1)S(1)} %get-tuple-element.12.after_ref.own_ref), channel_id=1, source_target_pairs={{0,8},{8,16},{16,24},{24,32},{32,40},{40,48},{48,56},{56,64},{64,7... | collective-permute-start | bytes 196616 | tf_op jit(solution)/shard_map/ppermute | solution.py:30

commit v6 on v4

--- a/solution.py
+++ b/solution.py
@@ -27,6 +27,10 @@
 SMALL = pltpu.CompilerParams(vmem_limit_bytes=4 << 20)
 
 
+def in_hbm(value):
+    return pltpu.with_memory_space_constraint(value, pltpu.HBM)
+
+
 def ring_shift(value, axis, steps):
     count = lax.axis_size(axis)
     return lax.ppermute(value, axis, [(source, (source + steps) % count) for source in range(count)])
@@ -88,11 +92,22 @@
 
 
 def prepare_kernel(
-    lengths_ref, first_ref, after_ref, weight_ref, affine_ref, params_ref, clips_ref
+    lengths_hbm, after_ref, gamma_one_hbm, beta_one_hbm, bias_one_hbm, gamma_two_hbm, beta_two_hbm,
+    bias_two_hbm, params_ref, clips_ref, lengths_ref, rows_ref, sems,
 ):
-    del after_ref, weight_ref
-    params_ref[...] = both_halves(affine_ref[...])
-    frame = first_ref[0]
+    del after_ref
+    affine = (gamma_one_hbm, beta_one_hbm, bias_one_hbm, gamma_two_hbm, beta_two_hbm, bias_two_hbm)
+    loads = [pltpu.make_async_copy(lengths_hbm, lengths_ref, sems.at[len(affine)])]
+    for k, ref in enumerate(affine):
+        loads.append(pltpu.make_async_copy(ref, rows_ref.at[k], sems.at[k]))
+    for load in loads:
+        load.start()
+    for load in loads:
+        load.wait()
+    for k in range(len(affine)):
+        params_ref[k : k + 1, :] = both_halves(rows_ref[k])
+    params_ref[len(affine) :, :] = jnp.zeros((8 - len(affine), LANES), jnp.float32)
+    frame = (2 * lax.axis_index("tm")).astype(jnp.int32)
     start_zero, end_zero = clip_bounds(lengths_ref, frame)
     start_one, end_one = clip_bounds(lengths_ref, frame + 1)
     for k, number in enumerate((start_zero, end_zero, start_one, end_one, frame, frame, frame, frame)):
@@ -100,8 +115,11 @@
 
 
 def conv_kernel(
-    at, sums_ref, own_ref, tail_ref, params_ref, clips_ref, w_ref, out_ref, slots_ref, cols_ref
+    at, sums_ref, own_ref, tail_ref, params_ref, clips_ref, w_hbm, out_ref, w_ref, slots_ref,
+    cols_ref, sem,
 ):
+    load = pltpu.make_async_copy(w_hbm, w_ref, sem)
+    load.start()
     clips = clips_ref[...]
     start_zero, end_zero = clips[0:1, :], clips[1:2, :]
     start_one, end_one = clips[2:3, :], clips[3:4, :]
@@ -176,6 +194,7 @@
             cols_ref[own * CELLS : (own + 1) * CELLS, pair * LANES : (pair + 1) * LANES] = jnp.where(
                 left, first, second
             )
+    load.wait()
     for block in range(2):
         width = C // 2
         partial = jnp.dot(
@@ -220,13 +239,15 @@
     partial = pl.pallas_call(
         functools.partial(conv_kernel, at),
         out_shape=shape_of((parts, CELLS, LANES), jnp.bfloat16),
-        in_specs=[VMEM, VMEM, VMEM, VMEM, VMEM, VMEM],
+        in_specs=[VMEM, VMEM, VMEM, VMEM, VMEM, HBM],
         out_specs=VMEM,
         scratch_shapes=[
+            pltpu.VMEM((ROWS, C), jnp.bfloat16),
             pltpu.VMEM((3, 6, SLOT, LANES), jnp.bfloat16),
             pltpu.VMEM((2 * CELLS, DEPTH), jnp.bfloat16),
+            pltpu.SemaphoreType.DMA,
         ],
-        compiler_params=pltpu.CompilerParams(vmem_limit_bytes=10 << 20),
+        compiler_params=pltpu.CompilerParams(vmem_limit_bytes=12 << 20),
         cost_estimate=pl.CostEstimate(
             flops=2 * ROWS * C * 2 * CELLS, bytes_accessed=3 << 20, transcendentals=4 * CELLS * CHANS
         ),
@@ -239,11 +260,10 @@
     clip_input, lengths, gamma_one, beta_one, w_one, bias_one, gamma_two, beta_two, w_two, bias_two
 ):
     count = lax.axis_size("tm")
-    first = (lax.axis_index("tm") * 2).astype(jnp.int32).reshape(1)
     packed_shape = shape_of((CELLS, LANES), jnp.bfloat16)
     sums_shape = shape_of((count, 4, LANES), jnp.float32)
-    flat_one = jnp.transpose(w_one, (1, 0, 2)).reshape(ROWS, C)
-    flat_two = jnp.transpose(w_two, (1, 0, 2)).reshape(ROWS, C)
+    flat_one = in_hbm(jnp.transpose(w_one, (1, 0, 2)).reshape(ROWS, C))
+    flat_two = in_hbm(jnp.transpose(w_two, (1, 0, 2)).reshape(ROWS, C))
     packed, sums = pl.pallas_call(
         pack_kernel,
         out_shape=(packed_shape, sums_shape),
@@ -252,19 +272,24 @@
         scratch_shapes=[pltpu.VMEM((CHANS, 2, CELLS), jnp.bfloat16), pltpu.SemaphoreType.DMA],
         compiler_params=SMALL,
         name="pack",
-    )(clip_input)
+    )(in_hbm(clip_input))
     tail = ring_shift(packed, "tm", 1)
     everyone = lax.all_to_all(sums, "tm", 0, 0, tiled=True)
-    affine = (gamma_one, beta_one, bias_one, gamma_two, beta_two, bias_two, gamma_two, beta_two)
+    affine = (gamma_one, beta_one, bias_one, gamma_two, beta_two, bias_two)
     params, clips = pl.pallas_call(
         prepare_kernel,
         out_shape=(shape_of((8, LANES), jnp.float32), shape_of((8, LANES), jnp.int32)),
-        in_specs=[SMEM, SMEM, VMEM, VMEM, VMEM],
+        in_specs=[HBM, VMEM] + [HBM] * len(affine),
         out_specs=(VMEM, VMEM),
+        scratch_shapes=[
+            pltpu.SMEM(lengths.shape, jnp.int32),
+            pltpu.VMEM((len(affine), 1, CHANS), jnp.float32),
+            pltpu.SemaphoreType.DMA((len(affine) + 1,)),
+        ],
         compiler_params=SMALL,
-        cost_estimate=pl.CostEstimate(flops=10000, bytes_accessed=2 << 20, transcendentals=0),
+        cost_estimate=pl.CostEstimate(flops=10000, bytes_accessed=1 << 20, transcendentals=0),
         name="prepare",
-    )(lengths, first, packed, flat_one, jnp.stack(affine))
+    )(in_hbm(lengths), packed, *[in_hbm(row.reshape(1, CHANS)) for row in affine])
     parts = normed_conv(0, tail, packed, everyone, params, clips, flat_one)
     y_one, sums = pl.pallas_call(
         middle_kernel,

time: 74.1 us -> 73.9 us (level)
  local copies, waits for them, and re-layouts: 5.23 us -> 0 us
  Pallas kernels: 7.26 us -> 10.8 us
  waiting for transfers between devices: 12.9 us -> 15.5 us
  starting transfers between devices: 23.2 us -> 22.1 us
    unnamed x10 -> x0, local copies, waits for them, and re-layouts: 4.44 us -> none
    pallas_call x2, Pallas kernels: 3.57 us -> 6.01 us  [normed_conv(): pl.pallas_call(functools.partial(conv_kernel, at), out_shape=shape_of((pa...]
    all_to_all x2, waiting for transfers between devices: 11.5 us -> 13.7 us  [on_device(): everyone = lax.all_to_all(sums, 'tm', 0, 0, tiled=True)]
    all_to_all x2, starting transfers between devices: 19.8 us -> 18.7 us  [on_device(): everyone = lax.all_to_all(sums, 'tm', 0, 0, tiled=True)]
    another operation x1 -> x0, local copies, waits for them, and re-layouts: 0.79 us -> none  [on_device(): jnp.stack(affine)]
    pallas_call x1, Pallas kernels: 1.22 us -> 2.01 us  [on_device(): pl.pallas_call(pack_kernel, out_shape=(packed_shape, sums_shape), in_spec...]
  transfers between devices with their start and end apart: 4 -> 4, of which waited for: 3 -> 4; matrix products, arithmetic and copies ran while one was open for 1% -> 0% of each run, Pallas kernels for 1% -> 1%
where the time goes in v6:
time: 73.9 us; the launch traced here: 73.5 us
  blocking collectives  25.1 us (34%)
  starting transfers between devices  22.1 us (30%)
  waiting for transfers between devices  15.5 us (21%)
  Pallas kernels  10.8 us (15%)
    all_to_all x2, blocking collectives, normed_conv(): return lax.all_to_all(partial, 'chan', 0, 0, tiled=True)  25.1 us
    all_to_all x2, starting transfers between devices, on_device(): everyone = lax.all_to_all(sums, 'tm', 0, 0, tiled=True)  18.7 us
    all_to_all x2, waiting for transfers between devices, on_device(): everyone = lax.all_to_all(sums, 'tm', 0, 0, tiled=True)  13.7 us
    pallas_call x2, Pallas kernels, normed_conv(): pl.pallas_call(functools.partial(conv_kernel, at), out_shape=shape_of((pa...  6.01 us
    ppermute x2, starting transfers between devices, ring_shift(): lax.ppermute(value, axis, [(source, (source + steps) % count) for source...  3.42 us
    pallas_call x1, Pallas kernels, on_device(): pl.pallas_call(pack_kernel, out_shape=(packed_shape, sums_shape), in_spec...  2.01 us
    ppermute x2, waiting for transfers between devices, ring_shift(): lax.ppermute(value, axis, [(source, (source + steps) % count) for source...  1.78 us
  transfers between devices with their start and end apart: 4, of which 4 were waited for; matrix products, arithmetic and copies ran while one was open for 0% of the time, Pallas kernels for 1%

profile of v6, /device:TPU:1, one launch (start us, length us, event | category | flops | bytes accessed | tf_op | source)
XLA Modules:
  0.0 73.5 jit_solution(5486732329935950571)
XLA Ops:
  0.0 2.0 %pack.1 = (bf16[256,128]{1,0:T(8,128)(2,1)S(1)}, f32[32,4,128]{2,1,0:T(4,128)}) custom-call(bf16[64,2,256]{2,1,0:T(2,128)(2,1)} %x_hbm.1), custom_call_target="tpu_custom_call" | custom-call | tf_op jit(solution)/shard_map/pack/pallas_call | solution.py:267
  2.0 12.8 %all-to-all-start = ((f32[32,4,128]{2,1,0:T(4,128)}), f32[32,4,128]{2,1,0:T(4,128)S(1)}, u32[]{:S(2)}, u32[]{:S(2)}) async-start(f32[32,4,128]{2,1,0:T(4,128)} %get-tuple-element.11), calls=%async_computation | async-start | bytes 131072 | tf_op jit(solution)/shard_map/all_to_all | solution.py:277
  14.8 1.7 %collective-permute-start = (bf16[256,128]{1,0:T(8,128)(2,1)S(1)}, bf16[256,128]{1,0:T(8,128)(2,1)S(1)}, u32[]{:S(2)}, u32[]{:S(2)}) collective-permute-start(bf16[256,128]{1,0:T(8,128)(2,1)S(1)} %get-tuple-element.12.after_ref.own_ref.packed_ref), channel_id=1, source_target_pairs={{0,8},{8,16},{16,24},{24,32},{32,40},{40,48},{48,56},{56,64},{64,7... | collective-permute-start | bytes 196616 | tf_op jit(solution)/shard_map/ppermute | solution.py:36
  16.5 0.9 %prepare.1 = (f32[8,128]{1,0:T(8,128)S(1)}, s32[8,128]{1,0:T(8,128)S(1)}) custom-call(s32[16]{0:T(128)} %lengths_hbm.1, bf16[256,128]{1,0:T(8,128)(2,1)S(1)} %get-tuple-element.12.after_ref.own_ref.packed_ref, f32[1,64]{1,0:T(1,128)} %bitcast.12, f32[1,64]{1,0:T(1,128)} %bitcast.13, f32[1,64]{1,0:T(1,128)} %bitcast.14, f32[1,64]{1,0:T(1,128)} %bitcast.15, ...), custom_call_target="tpu_custom_call" | custom-call | flops 10000 | bytes 1048576 | tf_op jit(solution)/shard_map/prepare/pallas_call | solution.py:279
  17.4 0.5 collective-permute-done.tail_ref
  17.8 6.9 %all-to-all-done.sums_ref = f32[32,4,128]{2,1,0:T(4,128)S(1)} async-done(((f32[32,4,128]{2,1,0:T(4,128)}), f32[32,4,128]{2,1,0:T(4,128)S(1)}, u32[]{:S(2)}, u32[]{:S(2)}) %all-to-all-start) | async-done | bytes 65568 | tf_op jit(solution)/shard_map/all_to_all | solution.py:277
  24.7 3.0 %norm_conv.2 = bf16[8,256,128]{2,1,0:T(8,128)(2,1)S(1)} custom-call(f32[32,4,128]{2,1,0:T(4,128)S(1)} %all-to-all-done.sums_ref, bf16[256,128]{1,0:T(8,128)(2,1)S(1)} %get-tuple-element.12.after_ref.own_ref.packed_ref, bf16[256,128]{1,0:T(8,128)(2,1)S(1)} %collective-permute-done.tail_ref, f32[8,128]{1,0:T(8,128)S(1)} %get-tuple-element.13.params_ref, ...), custom_call_target="tpu_custom_call" | custom-call | flops 905969664 | bytes 3145728 | tf_op jit(solution)/shard_map/norm_conv/pallas_call | solution.py:239
  27.8 13.4 %all_to_all.20.parts_ref = bf16[8,256,128]{2,1,0:T(8,128)(2,1)S(1)} all-to-all(bf16[8,256,128]{2,1,0:T(8,128)(2,1)S(1)} %norm_conv.2), channel_id=1, replica_groups=mesh['tm'=32,'chan'=8] {'chan'}, dimensions={0} | all-to-all | bytes 1048576 | tf_op jit(solution)/shard_map/all_to_all | solution.py:256
  41.1 1.0 %middle.1 = (bf16[256,128]{1,0:T(8,128)(2,1)S(1)}, f32[32,4,128]{2,1,0:T(4,128)}) custom-call(bf16[8,256,128]{2,1,0:T(8,128)(2,1)S(1)} %all_to_all.20.parts_ref, f32[8,128]{1,0:T(8,128)S(1)} %get-tuple-element.13.params_ref), custom_call_target="tpu_custom_call" | custom-call | tf_op jit(solution)/shard_map/middle/pallas_call | solution.py:294
  42.2 6.0 %all-to-all-start.2 = ((f32[32,4,128]{2,1,0:T(4,128)}), f32[32,4,128]{2,1,0:T(4,128)S(1)}, u32[]{:S(2)}, u32[]{:S(2)}) async-start(f32[32,4,128]{2,1,0:T(4,128)} %get-tuple-element.15), calls=%async_computation.2 | async-start | bytes 131072 | tf_op jit(solution)/shard_map/all_to_all | solution.py:303
  48.2 1.7 %collective-permute-start.1 = (bf16[256,128]{1,0:T(8,128)(2,1)S(1)}, bf16[256,128]{1,0:T(8,128)(2,1)S(1)}, u32[]{:S(2)}, u32[]{:S(2)}) collective-permute-start(bf16[256,128]{1,0:T(8,128)(2,1)S(1)} %get-tuple-element.16.own_ref), channel_id=1, source_target_pairs={{0,8},{8,16},{16,24},{24,32},{32,40},{40,48},{48,56},{56,64},{64,7... | collective-permute-start | bytes 196616 | tf_op jit(solution)/shard_map/ppermute | solution.py:36
  49.9 1.3 %collective-permute-done.1.tail_ref = bf16[256,128]{1,0:T(8,128)(2,1)S(1)} collective-permute-done((bf16[256,128]{1,0:T(8,128)(2,1)S(1)}, bf16[256,128]{1,0:T(8,128)(2,1)S(1)}, u32[]{:S(2)}, u32[]{:S(2)}) %collective-permute-start.1) | collective-permute-done | bytes 65568 | tf_op jit(solution)/shard_map/ppermute | solution.py:36
  51.2 6.8 %all-to-all-done.2.sums_ref = f32[32,4,128]{2,1,0:T(4,128)S(1)} async-done(((f32[32,4,128]{2,1,0:T(4,128)}), f32[32,4,128]{2,1,0:T(4,128)S(1)}, u32[]{:S(2)}, u32[]{:S(2)}) %all-to-all-start.2) | async-done | bytes 65568 | tf_op jit(solution)/shard_map/all_to_all | solution.py:303
  58.0 3.0 %norm_conv.3 = bf16[8,256,128]{2,1,0:T(8,128)(2,1)S(1)} custom-call(f32[32,4,128]{2,1,0:T(4,128)S(1)} %all-to-all-done.2.sums_ref, bf16[256,128]{1,0:T(8,128)(2,1)S(1)} %get-tuple-element.16.own_ref, bf16[256,128]{1,0:T(8,128)(2,1)S(1)} %collective-permute-done.1.tail_ref, f32[8,128]{1,0:T(8,128)S(1)} %get-tuple-element.13.params_ref, ...), custom_call_target="tpu_custom_call" | custom-call | flops 905969664 | bytes 3145728 | tf_op jit(solution)/shard_map/norm_conv/pallas_call | solution.py:239
  61.1 11.7 %all_to_all.21.parts_ref = bf16[8,256,128]{2,1,0:T(8,128)(2,1)S(1)} all-to-all(bf16[8,256,128]{2,1,0:T(8,128)(2,1)S(1)} %norm_conv.3), channel_id=1, replica_groups=mesh['tm'=32,'chan'=8] {'chan'}, dimensions={0} | all-to-all | bytes 1048576 | tf_op jit(solution)/shard_map/all_to_all | solution.py:256
  72.7 0.8 %last.1 = f32[64,2,256]{2,1,0:T(2,128)} custom-call(bf16[8,256,128]{2,1,0:T(8,128)(2,1)S(1)} %all_to_all.21.parts_ref, f32[8,128]{1,0:T(8,128)S(1)} %get-tuple-element.13.params_ref, bf16[256,128]{1,0:T(8,128)(2,1)S(1)} %get-tuple-element.12.after_ref.own_ref.packed_ref), custom_call_target="tpu_custom_call" | custom-call | tf_op jit(solution)/shard_map/last/pallas_call | solution.py:305
Async XLA Ops:
  2.0 22.7 %all-to-all-start = ((f32[32,4,128]{2,1,0:T(4,128)}), f32[32,4,128]{2,1,0:T(4,128)S(1)}, u32[]{:S(2)}, u32[]{:S(2)}) async-start(f32[32,4,128]{2,1,0:T(4,128)} %get-tuple-element.11), calls=%async_computation | async-start | bytes 131072 | tf_op jit(solution)/shard_map/all_to_all | solution.py:277
  14.8 3.0 %collective-permute-start = (bf16[256,128]{1,0:T(8,128)(2,1)S(1)}, bf16[256,128]{1,0:T(8,128)(2,1)S(1)}, u32[]{:S(2)}, u32[]{:S(2)}) collective-permute-start(bf16[256,128]{1,0:T(8,128)(2,1)S(1)} %get-tuple-element.12.after_ref.own_ref.packed_ref), channel_id=1, source_target_pairs={{0,8},{8,16},{16,24},{24,32},{32,40},{40,48},{48,56},{56,64},{64,7... | collective-permute-start | bytes 196616 | tf_op jit(solution)/shard_map/ppermute | solution.py:36
  42.2 15.9 %all-to-all-start.2 = ((f32[32,4,128]{2,1,0:T(4,128)}), f32[32,4,128]{2,1,0:T(4,128)S(1)}, u32[]{:S(2)}, u32[]{:S(2)}) async-start(f32[32,4,128]{2,1,0:T(4,128)} %get-tuple-element.15), calls=%async_computation.2 | async-start | bytes 131072 | tf_op jit(solution)/shard_map/all_to_all | solution.py:303
  48.2 3.0 %collective-permute-start.1 = (bf16[256,128]{1,0:T(8,128)(2,1)S(1)}, bf16[256,128]{1,0:T(8,128)(2,1)S(1)}, u32[]{:S(2)}, u32[]{:S(2)}) collective-permute-start(bf16[256,128]{1,0:T(8,128)(2,1)S(1)} %get-tuple-element.16.own_ref), channel_id=1, source_target_pairs={{0,8},{8,16},{16,24},{24,32},{32,40},{40,48},{48,56},{56,64},{64,7... | collective-permute-start | bytes 196616 | tf_op jit(solution)/shard_map/ppermute | solution.py:36

commit v7 on v6

--- a/solution.py
+++ b/solution.py
@@ -92,10 +92,10 @@
 
 
 def prepare_kernel(
-    lengths_hbm, after_ref, gamma_one_hbm, beta_one_hbm, bias_one_hbm, gamma_two_hbm, beta_two_hbm,
+    lengths_hbm, after_ref, weight_ref, gamma_one_hbm, beta_one_hbm, bias_one_hbm, gamma_two_hbm, beta_two_hbm,
     bias_two_hbm, params_ref, clips_ref, lengths_ref, rows_ref, sems,
 ):
-    del after_ref
+    del after_ref, weight_ref
     affine = (gamma_one_hbm, beta_one_hbm, bias_one_hbm, gamma_two_hbm, beta_two_hbm, bias_two_hbm)
     loads = [pltpu.make_async_copy(lengths_hbm, lengths_ref, sems.at[len(affine)])]
     for k, ref in enumerate(affine):
@@ -114,12 +114,16 @@
         clips_ref[k : k + 1, :] = jnp.full((1, LANES), number, jnp.int32)
 
 
+def fetch_kernel(weight_hbm, after_ref, weight_ref, sem):
+    del after_ref
+    load = pltpu.make_async_copy(weight_hbm, weight_ref, sem)
+    load.start()
+    load.wait()
+
+
 def conv_kernel(
-    at, sums_ref, own_ref, tail_ref, params_ref, clips_ref, w_hbm, out_ref, w_ref, slots_ref,
-    cols_ref, sem,
+    at, sums_ref, own_ref, tail_ref, params_ref, clips_ref, w_ref, out_ref, slots_ref, cols_ref
 ):
-    load = pltpu.make_async_copy(w_hbm, w_ref, sem)
-    load.start()
     clips = clips_ref[...]
     start_zero, end_zero = clips[0:1, :], clips[1:2, :]
     start_one, end_one = clips[2:3, :], clips[3:4, :]
@@ -194,7 +198,6 @@
             cols_ref[own * CELLS : (own + 1) * CELLS, pair * LANES : (pair + 1) * LANES] = jnp.where(
                 left, first, second
             )
-    load.wait()
     for block in range(2):
         width = C // 2
         partial = jnp.dot(
@@ -239,15 +242,13 @@
     partial = pl.pallas_call(
         functools.partial(conv_kernel, at),
         out_shape=shape_of((parts, CELLS, LANES), jnp.bfloat16),
-        in_specs=[VMEM, VMEM, VMEM, VMEM, VMEM, HBM],
+        in_specs=[VMEM, VMEM, VMEM, VMEM, VMEM, VMEM],
         out_specs=VMEM,
         scratch_shapes=[
-            pltpu.VMEM((ROWS, C), jnp.bfloat16),
             pltpu.VMEM((3, 6, SLOT, LANES), jnp.bfloat16),
             pltpu.VMEM((2 * CELLS, DEPTH), jnp.bfloat16),
-            pltpu.SemaphoreType.DMA,
         ],
-        compiler_params=pltpu.CompilerParams(vmem_limit_bytes=12 << 20),
+        compiler_params=pltpu.CompilerParams(vmem_limit_bytes=10 << 20),
         cost_estimate=pl.CostEstimate(
             flops=2 * ROWS * C * 2 * CELLS, bytes_accessed=3 << 20, transcendentals=4 * CELLS * CHANS
         ),
@@ -262,7 +263,7 @@
     count = lax.axis_size("tm")
     packed_shape = shape_of((CELLS, LANES), jnp.bfloat16)
     sums_shape = shape_of((count, 4, LANES), jnp.float32)
-    flat_one = in_hbm(jnp.transpose(w_one, (1, 0, 2)).reshape(ROWS, C))
+    flat_one = jnp.transpose(w_one, (1, 0, 2)).reshape(ROWS, C)
     flat_two = in_hbm(jnp.transpose(w_two, (1, 0, 2)).reshape(ROWS, C))
     packed, sums = pl.pallas_call(
         pack_kernel,
@@ -279,7 +280,7 @@
     params, clips = pl.pallas_call(
         prepare_kernel,
         out_shape=(shape_of((8, LANES), jnp.float32), shape_of((8, LANES), jnp.int32)),
-        in_specs=[HBM, VMEM] + [HBM] * len(affine),
+        in_specs=[HBM, VMEM, VMEM] + [HBM] * len(affine),
         out_specs=(VMEM, VMEM),
         scratch_shapes=[
             pltpu.SMEM(lengths.shape, jnp.int32),
@@ -289,7 +290,7 @@
         compiler_params=SMALL,
         cost_estimate=pl.CostEstimate(flops=10000, bytes_accessed=1 << 20, transcendentals=0),
         name="prepare",
-    )(in_hbm(lengths), packed, *[in_hbm(row.reshape(1, CHANS)) for row in affine])
+    )(in_hbm(lengths), packed, flat_one, *[in_hbm(row.reshape(1, CHANS)) for row in affine])
     parts = normed_conv(0, tail, packed, everyone, params, clips, flat_one)
     y_one, sums = pl.pallas_call(
         middle_kernel,
@@ -301,7 +302,17 @@
     )(parts, params)
     tail = ring_shift(y_one, "tm", 1)
     everyone = lax.all_to_all(sums, "tm", 0, 0, tiled=True)
-    parts = normed_conv(3, tail, y_one, everyone, params, clips, flat_two)
+    held = pl.pallas_call(
+        fetch_kernel,
+        out_shape=shape_of((ROWS, C), jnp.bfloat16),
+        in_specs=[HBM, VMEM],
+        out_specs=VMEM,
+        scratch_shapes=[pltpu.SemaphoreType.DMA],
+        compiler_params=SMALL,
+        cost_estimate=pl.CostEstimate(flops=10000, bytes_accessed=2 << 20, transcendentals=0),
+        name="fetch",
+    )(flat_two, y_one)
+    parts = normed_conv(3, tail, y_one, everyone, params, clips, held)
     return pl.pallas_call(
         last_kernel,
         out_shape=shape_of(clip_input.shape, jnp.float32),

time: 73.9 us -> 71.5 us (0.968)
  waiting for transfers between devices: 15.5 us -> 12.4 us
  local copies, waits for them, and re-layouts: 0 us -> 1.48 us
  Pallas kernels: 10.8 us -> 9.93 us
    pallas_call x2, Pallas kernels: 6.01 us -> 3.57 us  [normed_conv(): pl.pallas_call(functools.partial(conv_kernel, at), out_shape=shape_of((pa...]
    ppermute x2, waiting for transfers between devices: 1.78 us -> 0.01 us  [ring_shift(): lax.ppermute(value, axis, [(source, (source + steps) % count) for source...]
    pallas_call x0 -> x1, Pallas kernels: none -> 1.48 us  [on_device(): pl.pallas_call(fetch_kernel, out_shape=shape_of((ROWS, C), jnp.bfloat16),...]
    unnamed x0 -> x4, local copies, waits for them, and re-layouts: none -> 1.48 us
    all_to_all x2, waiting for transfers between devices: 13.7 us -> 12.4 us  [on_device(): everyone = lax.all_to_all(sums, 'tm', 0, 0, tiled=True)]
  transfers between devices with their start and end apart: 4 -> 4, of which waited for: 4 -> 2; matrix products, arithmetic and copies ran while one was open for 0% -> 0% of each run, Pallas kernels for 1% -> 3%
where the time goes in v7:
time: 71.5 us; the launch traced here: 71.1 us
  blocking collectives  25.1 us (35%)
  starting transfers between devices  22.1 us (31%)
  waiting for transfers between devices  12.4 us (17%)
  Pallas kernels  9.93 us (14%)
  local copies, waits for them, and re-layouts  1.48 us (2%)
    all_to_all x2, blocking collectives, normed_conv(): return lax.all_to_all(partial, 'chan', 0, 0, tiled=True)  25.1 us
    all_to_all x2, starting transfers between devices, on_device(): everyone = lax.all_to_all(sums, 'tm', 0, 0, tiled=True)  18.7 us
    all_to_all x2, waiting for transfers between devices, on_device(): everyone = lax.all_to_all(sums, 'tm', 0, 0, tiled=True)  12.4 us
    pallas_call x2, Pallas kernels, normed_conv(): pl.pallas_call(functools.partial(conv_kernel, at), out_shape=shape_of((pa...  3.57 us
    ppermute x2, starting transfers between devices, ring_shift(): lax.ppermute(value, axis, [(source, (source + steps) % count) for source...  3.42 us
    pallas_call x1, Pallas kernels, on_device(): pl.pallas_call(pack_kernel, out_shape=(packed_shape, sums_shape), in_spec...  2.01 us
    pallas_call x1, Pallas kernels, on_device(): pl.pallas_call(fetch_kernel, out_shape=shape_of((ROWS, C), jnp.bfloat16),...  1.48 us
    unnamed x4, local copies, waits for them, and re-layouts  1.48 us
  transfers between devices with their start and end apart: 4, of which 2 were waited for; matrix products, arithmetic and copies ran while one was open for 0% of the time, Pallas kernels for 3%

profile of v7, /device:TPU:1, one launch (start us, length us, event | category | flops | bytes accessed | tf_op | source)
XLA Modules:
  0.0 71.1 jit_solution(9297634918729137593)
XLA Ops:
  0.0 2.0 %pack.1 = (bf16[256,128]{1,0:T(8,128)(2,1)S(1)}, f32[32,4,128]{2,1,0:T(4,128)}) custom-call(bf16[64,2,256]{2,1,0:T(2,128)(2,1)} %x_hbm.1), custom_call_target="tpu_custom_call" | custom-call | tf_op jit(solution)/shard_map/pack/pallas_call | solution.py:268
  2.0 12.8 %all-to-all-start = ((f32[32,4,128]{2,1,0:T(4,128)}), f32[32,4,128]{2,1,0:T(4,128)S(1)}, u32[]{:S(2)}, u32[]{:S(2)}) async-start(f32[32,4,128]{2,1,0:T(4,128)} %get-tuple-element.11), calls=%async_computation | async-start | bytes 131072 | tf_op jit(solution)/shard_map/all_to_all | solution.py:278
  14.8 1.7 %collective-permute-start = (bf16[256,128]{1,0:T(8,128)(2,1)S(1)}, bf16[256,128]{1,0:T(8,128)(2,1)S(1)}, u32[]{:S(2)}, u32[]{:S(2)}) collective-permute-start(bf16[256,128]{1,0:T(8,128)(2,1)S(1)} %get-tuple-element.12.after_ref.own_ref.packed_ref), channel_id=1, source_target_pairs={{0,8},{8,16},{16,24},{24,32},{32,40},{40,48},{48,56},{56,64},{64,7... | collective-permute-start | bytes 196616 | tf_op jit(solution)/shard_map/ppermute | solution.py:36
  16.5 0.0 copy-start
  16.5 1.5 %copy-done = bf16[64,27,512]{2,0,1:T(8,128)(2,1)S(1)} copy-done((bf16[64,27,512]{2,0,1:T(8,128)(2,1)S(1)}, bf16[64,27,512]{2,0,1:T(8,128)(2,1)}, u32[]{:S(2)}) %copy-start) | copy-done | bytes 1769496
  18.0 0.0 copy-start.1
  18.0 1.0 %prepare.1 = (f32[8,128]{1,0:T(8,128)S(1)}, s32[8,128]{1,0:T(8,128)S(1)}) custom-call(s32[16]{0:T(128)} %lengths_hbm.1, bf16[256,128]{1,0:T(8,128)(2,1)S(1)} %get-tuple-element.12.after_ref.own_ref.packed_ref, bf16[1728,512]{1,0:T(8,128)(2,1)S(1)} %bitcast.12, f32[1,64]{1,0:T(1,128)} %bitcast.15, f32[1,64]{1,0:T(1,128)} %bitcast.16, f32[1,64]{1,0:T(1,128)} %bitcast.17, ...), custom_call_target="tpu_custom_call" | custom-call | flops 10000 | bytes 1048576 | tf_op jit(solution)/shard_map/prepare/pallas_call | solution.py:280
  19.0 0.0 collective-permute-done.tail_ref
  19.0 5.7 %all-to-all-done.sums_ref = f32[32,4,128]{2,1,0:T(4,128)S(1)} async-done(((f32[32,4,128]{2,1,0:T(4,128)}), f32[32,4,128]{2,1,0:T(4,128)S(1)}, u32[]{:S(2)}, u32[]{:S(2)}) %all-to-all-start) | async-done | bytes 65568 | tf_op jit(solution)/shard_map/all_to_all | solution.py:278
  24.7 0.0 copy-done.1
  24.7 1.8 %norm_conv.2 = bf16[8,256,128]{2,1,0:T(8,128)(2,1)S(1)} custom-call(f32[32,4,128]{2,1,0:T(4,128)S(1)} %all-to-all-done.sums_ref, bf16[256,128]{1,0:T(8,128)(2,1)S(1)} %get-tuple-element.12.after_ref.own_ref.packed_ref, bf16[256,128]{1,0:T(8,128)(2,1)S(1)} %collective-permute-done.tail_ref, f32[8,128]{1,0:T(8,128)S(1)} %get-tuple-element.13.params_ref, ...), custom_call_target="tpu_custom_call" | custom-call | flops 905969664 | bytes 3145728 | tf_op jit(solution)/shard_map/norm_conv/pallas_call | solution.py:242
  26.5 13.4 %all_to_all.20.parts_ref = bf16[8,256,128]{2,1,0:T(8,128)(2,1)S(1)} all-to-all(bf16[8,256,128]{2,1,0:T(8,128)(2,1)S(1)} %norm_conv.2), channel_id=1, replica_groups=mesh['tm'=32,'chan'=8] {'chan'}, dimensions={0} | all-to-all | bytes 1048576 | tf_op jit(solution)/shard_map/all_to_all | solution.py:257
  39.9 1.0 %middle.1 = (bf16[256,128]{1,0:T(8,128)(2,1)S(1)}, f32[32,4,128]{2,1,0:T(4,128)}) custom-call(bf16[8,256,128]{2,1,0:T(8,128)(2,1)S(1)} %all_to_all.20.parts_ref, f32[8,128]{1,0:T(8,128)S(1)} %get-tuple-element.13.params_ref), custom_call_target="tpu_custom_call" | custom-call | tf_op jit(solution)/shard_map/middle/pallas_call | solution.py:295
  41.0 6.0 %all-to-all-start.2 = ((f32[32,4,128]{2,1,0:T(4,128)}), f32[32,4,128]{2,1,0:T(4,128)S(1)}, u32[]{:S(2)}, u32[]{:S(2)}) async-start(f32[32,4,128]{2,1,0:T(4,128)} %get-tuple-element.15), calls=%async_computation.2 | async-start | bytes 131072 | tf_op jit(solution)/shard_map/all_to_all | solution.py:304
  46.9 1.7 %collective-permute-start.1 = (bf16[256,128]{1,0:T(8,128)(2,1)S(1)}, bf16[256,128]{1,0:T(8,128)(2,1)S(1)}, u32[]{:S(2)}, u32[]{:S(2)}) collective-permute-start(bf16[256,128]{1,0:T(8,128)(2,1)S(1)} %get-tuple-element.16.after_ref.own_ref), channel_id=1, source_target_pairs={{0,8},{8,16},{16,24},{24,32},{32,40},{40,48},{48,56},{56,64},{64,7... | collective-permute-start | bytes 196616 | tf_op jit(solution)/shard_map/ppermute | solution.py:36
  48.7 1.5 %fetch.1.w_ref = bf16[1728,512]{1,0:T(8,128)(2,1)S(1)} custom-call(bf16[1728,512]{1,0:T(8,128)(2,1)} %bitcast.14, bf16[256,128]{1,0:T(8,128)(2,1)S(1)} %get-tuple-element.16.after_ref.own_ref), custom_call_target="tpu_custom_call" | custom-call | flops 10000 | bytes 2097152 | tf_op jit(solution)/shard_map/fetch/pallas_call | solution.py:305
  50.1 0.0 collective-permute-done.1.tail_ref
  50.2 6.7 %all-to-all-done.2.sums_ref = f32[32,4,128]{2,1,0:T(4,128)S(1)} async-done(((f32[32,4,128]{2,1,0:T(4,128)}), f32[32,4,128]{2,1,0:T(4,128)S(1)}, u32[]{:S(2)}, u32[]{:S(2)}) %all-to-all-start.2) | async-done | bytes 65568 | tf_op jit(solution)/shard_map/all_to_all | solution.py:304
  56.8 1.8 %norm_conv.3 = bf16[8,256,128]{2,1,0:T(8,128)(2,1)S(1)} custom-call(f32[32,4,128]{2,1,0:T(4,128)S(1)} %all-to-all-done.2.sums_ref, bf16[256,128]{1,0:T(8,128)(2,1)S(1)} %get-tuple-element.16.after_ref.own_ref, bf16[256,128]{1,0:T(8,128)(2,1)S(1)} %collective-permute-done.1.tail_ref, f32[8,128]{1,0:T(8,128)S(1)} %get-tuple-element.13.params_ref, ...), custom_call_target="tpu_custom_call" | custom-call | flops 905969664 | bytes 3145728 | tf_op jit(solution)/shard_map/norm_conv/pallas_call | solution.py:242
  58.6 11.7 %all_to_all.21.parts_ref = bf16[8,256,128]{2,1,0:T(8,128)(2,1)S(1)} all-to-all(bf16[8,256,128]{2,1,0:T(8,128)(2,1)S(1)} %norm_conv.3), channel_id=1, replica_groups=mesh['tm'=32,'chan'=8] {'chan'}, dimensions={0} | all-to-all | bytes 1048576 | tf_op jit(solution)/shard_map/all_to_all | solution.py:257
  70.3 0.8 %last.1 = f32[64,2,256]{2,1,0:T(2,128)} custom-call(bf16[8,256,128]{2,1,0:T(8,128)(2,1)S(1)} %all_to_all.21.parts_ref, f32[8,128]{1,0:T(8,128)S(1)} %get-tuple-element.13.params_ref, bf16[256,128]{1,0:T(8,128)(2,1)S(1)} %get-tuple-element.12.after_ref.own_ref.packed_ref), custom_call_target="tpu_custom_call" | custom-call | tf_op jit(solution)/shard_map/last/pallas_call | solution.py:316
Async XLA Ops:
  2.0 22.7 %all-to-all-start = ((f32[32,4,128]{2,1,0:T(4,128)}), f32[32,4,128]{2,1,0:T(4,128)S(1)}, u32[]{:S(2)}, u32[]{:S(2)}) async-start(f32[32,4,128]{2,1,0:T(4,128)} %get-tuple-element.11), calls=%async_computation | async-start | bytes 131072 | tf_op jit(solution)/shard_map/all_to_all | solution.py:278
  14.8 4.2 %collective-permute-start = (bf16[256,128]{1,0:T(8,128)(2,1)S(1)}, bf16[256,128]{1,0:T(8,128)(2,1)S(1)}, u32[]{:S(2)}, u32[]{:S(2)}) collective-permute-start(bf16[256,128]{1,0:T(8,128)(2,1)S(1)} %get-tuple-element.12.after_ref.own_ref.packed_ref), channel_id=1, source_target_pairs={{0,8},{8,16},{16,24},{24,32},{32,40},{40,48},{48,56},{56,64},{64,7... | collective-permute-start | bytes 196616 | tf_op jit(solution)/shard_map/ppermute | solution.py:36
  16.5 1.5 %copy-start = (bf16[64,27,512]{2,0,1:T(8,128)(2,1)S(1)}, bf16[64,27,512]{2,0,1:T(8,128)(2,1)}, u32[]{:S(2)}) copy-start(bf16[64,27,512]{2,0,1:T(8,128)(2,1)} %param.14) | copy-start | bytes 5308420
  18.0 6.8 %copy-start.1 = (bf16[64,27,512]{2,0,1:T(8,128)(2,1)S(1)}, bf16[64,27,512]{2,0,1:T(8,128)(2,1)}, u32[]{:S(2)}) copy-start(bf16[64,27,512]{2,0,1:T(8,128)(2,1)} %param.14) | copy-start | bytes 5308420
  41.0 15.8 %all-to-all-start.2 = ((f32[32,4,128]{2,1,0:T(4,128)}), f32[32,4,128]{2,1,0:T(4,128)S(1)}, u32[]{:S(2)}, u32[]{:S(2)}) async-start(f32[32,4,128]{2,1,0:T(4,128)} %get-tuple-element.15), calls=%async_computation.2 | async-start | bytes 131072 | tf_op jit(solution)/shard_map/all_to_all | solution.py:304
  46.9 3.2 %collective-permute-start.1 = (bf16[256,128]{1,0:T(8,128)(2,1)S(1)}, bf16[256,128]{1,0:T(8,128)(2,1)S(1)}, u32[]{:S(2)}, u32[]{:S(2)}) collective-permute-start(bf16[256,128]{1,0:T(8,128)(2,1)S(1)} %get-tuple-element.16.after_ref.own_ref), channel_id=1, source_target_pairs={{0,8},{8,16},{16,24},{24,32},{32,40},{40,48},{48,56},{56,64},{64,7... | collective-permute-start | bytes 196616 | tf_op jit(solution)/shard_map/ppermute | solution.py:36

commit v8 on v6

--- a/solution.py
+++ b/solution.py
@@ -114,12 +114,16 @@
         clips_ref[k : k + 1, :] = jnp.full((1, LANES), number, jnp.int32)
 
 
+def fetch_kernel(weight_hbm, after_ref, weight_ref, sem):
+    del after_ref
+    load = pltpu.make_async_copy(weight_hbm, weight_ref, sem)
+    load.start()
+    load.wait()
+
+
 def conv_kernel(
-    at, sums_ref, own_ref, tail_ref, params_ref, clips_ref, w_hbm, out_ref, w_ref, slots_ref,
-    cols_ref, sem,
+    at, sums_ref, own_ref, tail_ref, params_ref, clips_ref, w_ref, out_ref, slots_ref, cols_ref
 ):
-    load = pltpu.make_async_copy(w_hbm, w_ref, sem)
-    load.start()
     clips = clips_ref[...]
     start_zero, end_zero = clips[0:1, :], clips[1:2, :]
     start_one, end_one = clips[2:3, :], clips[3:4, :]
@@ -194,7 +198,6 @@
             cols_ref[own * CELLS : (own + 1) * CELLS, pair * LANES : (pair + 1) * LANES] = jnp.where(
                 left, first, second
             )
-    load.wait()
     for block in range(2):
         width = C // 2
         partial = jnp.dot(
@@ -234,20 +237,31 @@
     return jax.ShapeDtypeStruct(shape, dtype)
 
 
+def fetch(weight, after):
+    return pl.pallas_call(
+        fetch_kernel,
+        out_shape=shape_of((ROWS, C), jnp.bfloat16),
+        in_specs=[HBM, VMEM],
+        out_specs=VMEM,
+        scratch_shapes=[pltpu.SemaphoreType.DMA],
+        compiler_params=SMALL,
+        cost_estimate=pl.CostEstimate(flops=10000, bytes_accessed=2 << 20, transcendentals=0),
+        name="fetch",
+    )(weight, after)
+
+
 def normed_conv(at, tail, packed, sums, params, clips, weight):
     parts = C // CHANS
     partial = pl.pallas_call(
         functools.partial(conv_kernel, at),
         out_shape=shape_of((parts, CELLS, LANES), jnp.bfloat16),
-        in_specs=[VMEM, VMEM, VMEM, VMEM, VMEM, HBM],
+        in_specs=[VMEM, VMEM, VMEM, VMEM, VMEM, VMEM],
         out_specs=VMEM,
         scratch_shapes=[
-            pltpu.VMEM((ROWS, C), jnp.bfloat16),
             pltpu.VMEM((3, 6, SLOT, LANES), jnp.bfloat16),
             pltpu.VMEM((2 * CELLS, DEPTH), jnp.bfloat16),
-            pltpu.SemaphoreType.DMA,
         ],
-        compiler_params=pltpu.CompilerParams(vmem_limit_bytes=12 << 20),
+        compiler_params=pltpu.CompilerParams(vmem_limit_bytes=10 << 20),
         cost_estimate=pl.CostEstimate(
             flops=2 * ROWS * C * 2 * CELLS, bytes_accessed=3 << 20, transcendentals=4 * CELLS * CHANS
         ),
@@ -290,7 +304,7 @@
         cost_estimate=pl.CostEstimate(flops=10000, bytes_accessed=1 << 20, transcendentals=0),
         name="prepare",
     )(in_hbm(lengths), packed, *[in_hbm(row.reshape(1, CHANS)) for row in affine])
-    parts = normed_conv(0, tail, packed, everyone, params, clips, flat_one)
+    parts = normed_conv(0, tail, packed, everyone, params, clips, fetch(flat_one, packed))
     y_one, sums = pl.pallas_call(
         middle_kernel,
         out_shape=(packed_shape, sums_shape),
@@ -301,7 +315,8 @@
     )(parts, params)
     tail = ring_shift(y_one, "tm", 1)
     everyone = lax.all_to_all(sums, "tm", 0, 0, tiled=True)
-    parts = normed_conv(3, tail, y_one, everyone, params, clips, flat_two)
+    held = fetch(flat_two, y_one)
+    parts = normed_conv(3, tail, y_one, everyone, params, clips, held)
     return pl.pallas_call(
         last_kernel,
         out_shape=shape_of(clip_input.shape, jnp.float32),

time: 73.9 us -> 71.5 us (0.968)
  waiting for transfers between devices: 15.5 us -> 12.5 us
    pallas_call x0 -> x2, Pallas kernels: none -> 2.97 us  [fetch(): pl.pallas_call(fetch_kernel, out_shape=shape_of((ROWS, C), jnp.bfloat16),...]
    pallas_call x2, Pallas kernels: 6.01 us -> 3.58 us  [normed_conv(): pl.pallas_call(functools.partial(conv_kernel, at), out_shape=shape_of((pa...]
    ppermute x2, waiting for transfers between devices: 1.78 us -> 0.01 us  [ring_shift(): lax.ppermute(value, axis, [(source, (source + steps) % count) for source...]
    all_to_all x2, waiting for transfers between devices: 13.7 us -> 12.5 us  [on_device(): everyone = lax.all_to_all(sums, 'tm', 0, 0, tiled=True)]
  transfers between devices with their start and end apart: 4 -> 4, of which waited for: 4 -> 2; matrix products, arithmetic and copies ran while one was open for 0% -> 0% of each run, Pallas kernels for 1% -> 5%
where the time goes in v8:
time: 71.5 us; the launch traced here: 71.1 us
  blocking collectives  25.1 us (35%)
  starting transfers between devices  22.2 us (31%)
  waiting for transfers between devices  12.5 us (17%)
  Pallas kernels  11.3 us (16%)
    all_to_all x2, blocking collectives, normed_conv(): return lax.all_to_all(partial, 'chan', 0, 0, tiled=True)  25.1 us
    all_to_all x2, starting transfers between devices, on_device(): everyone = lax.all_to_all(sums, 'tm', 0, 0, tiled=True)  18.7 us
    all_to_all x2, waiting for transfers between devices, on_device(): everyone = lax.all_to_all(sums, 'tm', 0, 0, tiled=True)  12.5 us
    pallas_call x2, Pallas kernels, normed_conv(): pl.pallas_call(functools.partial(conv_kernel, at), out_shape=shape_of((pa...  3.58 us
    ppermute x2, starting transfers between devices, ring_shift(): lax.ppermute(value, axis, [(source, (source + steps) % count) for source...  3.42 us
    pallas_call x2, Pallas kernels, fetch(): pl.pallas_call(fetch_kernel, out_shape=shape_of((ROWS, C), jnp.bfloat16),...  2.97 us
    pallas_call x1, Pallas kernels, on_device(): pl.pallas_call(pack_kernel, out_shape=(packed_shape, sums_shape), in_spec...  2.01 us
  transfers between devices with their start and end apart: 4, of which 2 were waited for; matrix products, arithmetic and copies ran while one was open for 0% of the time, Pallas kernels for 5%

profile of v8, /device:TPU:1, one launch (start us, length us, event | category | flops | bytes accessed | tf_op | source)
XLA Modules:
  0.0 71.1 jit_solution(15617424656215908151)
XLA Ops:
  0.0 2.0 %pack.1 = (bf16[256,128]{1,0:T(8,128)(2,1)S(1)}, f32[32,4,128]{2,1,0:T(4,128)}) custom-call(bf16[64,2,256]{2,1,0:T(2,128)(2,1)} %x_hbm.1), custom_call_target="tpu_custom_call" | custom-call | tf_op jit(solution)/shard_map/pack/pallas_call | solution.py:281
  2.0 12.8 %all-to-all-start = ((f32[32,4,128]{2,1,0:T(4,128)}), f32[32,4,128]{2,1,0:T(4,128)S(1)}, u32[]{:S(2)}, u32[]{:S(2)}) async-start(f32[32,4,128]{2,1,0:T(4,128)} %get-tuple-element.11), calls=%async_computation | async-start | bytes 131072 | tf_op jit(solution)/shard_map/all_to_all | solution.py:291
  14.8 1.7 %collective-permute-start = (bf16[256,128]{1,0:T(8,128)(2,1)S(1)}, bf16[256,128]{1,0:T(8,128)(2,1)S(1)}, u32[]{:S(2)}, u32[]{:S(2)}) collective-permute-start(bf16[256,128]{1,0:T(8,128)(2,1)S(1)} %get-tuple-element.12.after_ref.own_ref.packed_ref), channel_id=1, source_target_pairs={{0,8},{8,16},{16,24},{24,32},{32,40},{40,48},{48,56},{56,64},{64,7... | collective-permute-start | bytes 196616 | tf_op jit(solution)/shard_map/ppermute | solution.py:36
  16.5 1.5 %fetch.2.w_ref = bf16[1728,512]{1,0:T(8,128)(2,1)S(1)} custom-call(bf16[1728,512]{1,0:T(8,128)(2,1)} %bitcast.12, bf16[256,128]{1,0:T(8,128)(2,1)S(1)} %get-tuple-element.12.after_ref.own_ref.packed_ref), custom_call_target="tpu_custom_call" | custom-call | flops 10000 | bytes 2097152 | tf_op jit(solution)/shard_map/fetch/pallas_call | solution.py:241
  18.0 0.9 %prepare.1 = (f32[8,128]{1,0:T(8,128)S(1)}, s32[8,128]{1,0:T(8,128)S(1)}) custom-call(s32[16]{0:T(128)} %lengths_hbm.1, bf16[256,128]{1,0:T(8,128)(2,1)S(1)} %get-tuple-element.12.after_ref.own_ref.packed_ref, f32[1,64]{1,0:T(1,128)} %bitcast.14, f32[1,64]{1,0:T(1,128)} %bitcast.15, f32[1,64]{1,0:T(1,128)} %bitcast.16, f32[1,64]{1,0:T(1,128)} %bitcast.17, ...), custom_call_target="tpu_custom_call" | custom-call | flops 10000 | bytes 1048576 | tf_op jit(solution)/shard_map/prepare/pallas_call | solution.py:293
  18.9 0.0 collective-permute-done.tail_ref
  18.9 5.9 %all-to-all-done.sums_ref = f32[32,4,128]{2,1,0:T(4,128)S(1)} async-done(((f32[32,4,128]{2,1,0:T(4,128)}), f32[32,4,128]{2,1,0:T(4,128)S(1)}, u32[]{:S(2)}, u32[]{:S(2)}) %all-to-all-start) | async-done | bytes 65568 | tf_op jit(solution)/shard_map/all_to_all | solution.py:291
  24.7 1.8 %norm_conv.2 = bf16[8,256,128]{2,1,0:T(8,128)(2,1)S(1)} custom-call(f32[32,4,128]{2,1,0:T(4,128)S(1)} %all-to-all-done.sums_ref, bf16[256,128]{1,0:T(8,128)(2,1)S(1)} %get-tuple-element.12.after_ref.own_ref.packed_ref, bf16[256,128]{1,0:T(8,128)(2,1)S(1)} %collective-permute-done.tail_ref, f32[8,128]{1,0:T(8,128)S(1)} %get-tuple-element.13.params_ref, ...), custom_call_target="tpu_custom_call" | custom-call | flops 905969664 | bytes 3145728 | tf_op jit(solution)/shard_map/norm_conv/pallas_call | solution.py:255
  26.5 13.4 %all_to_all.20.parts_ref = bf16[8,256,128]{2,1,0:T(8,128)(2,1)S(1)} all-to-all(bf16[8,256,128]{2,1,0:T(8,128)(2,1)S(1)} %norm_conv.2), channel_id=1, replica_groups=mesh['tm'=32,'chan'=8] {'chan'}, dimensions={0} | all-to-all | bytes 1048576 | tf_op jit(solution)/shard_map/all_to_all | solution.py:270
  39.9 1.0 %middle.1 = (bf16[256,128]{1,0:T(8,128)(2,1)S(1)}, f32[32,4,128]{2,1,0:T(4,128)}) custom-call(bf16[8,256,128]{2,1,0:T(8,128)(2,1)S(1)} %all_to_all.20.parts_ref, f32[8,128]{1,0:T(8,128)S(1)} %get-tuple-element.13.params_ref), custom_call_target="tpu_custom_call" | custom-call | tf_op jit(solution)/shard_map/middle/pallas_call | solution.py:308
  41.0 6.0 %all-to-all-start.2 = ((f32[32,4,128]{2,1,0:T(4,128)}), f32[32,4,128]{2,1,0:T(4,128)S(1)}, u32[]{:S(2)}, u32[]{:S(2)}) async-start(f32[32,4,128]{2,1,0:T(4,128)} %get-tuple-element.15), calls=%async_computation.2 | async-start | bytes 131072 | tf_op jit(solution)/shard_map/all_to_all | solution.py:317
  46.9 1.7 %collective-permute-start.1 = (bf16[256,128]{1,0:T(8,128)(2,1)S(1)}, bf16[256,128]{1,0:T(8,128)(2,1)S(1)}, u32[]{:S(2)}, u32[]{:S(2)}) collective-permute-start(bf16[256,128]{1,0:T(8,128)(2,1)S(1)} %get-tuple-element.16.after_ref.own_ref), channel_id=1, source_target_pairs={{0,8},{8,16},{16,24},{24,32},{32,40},{40,48},{48,56},{56,64},{64,7... | collective-permute-start | bytes 196616 | tf_op jit(solution)/shard_map/ppermute | solution.py:36
  48.7 1.5 %fetch.3.w_ref = bf16[1728,512]{1,0:T(8,128)(2,1)S(1)} custom-call(bf16[1728,512]{1,0:T(8,128)(2,1)} %bitcast.13, bf16[256,128]{1,0:T(8,128)(2,1)S(1)} %get-tuple-element.16.after_ref.own_ref), custom_call_target="tpu_custom_call" | custom-call | flops 10000 | bytes 2097152 | tf_op jit(solution)/shard_map/fetch/pallas_call | solution.py:241
  50.1 0.0 collective-permute-done.1.tail_ref
  50.2 6.7 %all-to-all-done.2.sums_ref = f32[32,4,128]{2,1,0:T(4,128)S(1)} async-done(((f32[32,4,128]{2,1,0:T(4,128)}), f32[32,4,128]{2,1,0:T(4,128)S(1)}, u32[]{:S(2)}, u32[]{:S(2)}) %all-to-all-start.2) | async-done | bytes 65568 | tf_op jit(solution)/shard_map/all_to_all | solution.py:317
  56.8 1.8 %norm_conv.3 = bf16[8,256,128]{2,1,0:T(8,128)(2,1)S(1)} custom-call(f32[32,4,128]{2,1,0:T(4,128)S(1)} %all-to-all-done.2.sums_ref, bf16[256,128]{1,0:T(8,128)(2,1)S(1)} %get-tuple-element.16.after_ref.own_ref, bf16[256,128]{1,0:T(8,128)(2,1)S(1)} %collective-permute-done.1.tail_ref, f32[8,128]{1,0:T(8,128)S(1)} %get-tuple-element.13.params_ref, ...), custom_call_target="tpu_custom_call" | custom-call | flops 905969664 | bytes 3145728 | tf_op jit(solution)/shard_map/norm_conv/pallas_call | solution.py:255
  58.6 11.7 %all_to_all.21.parts_ref = bf16[8,256,128]{2,1,0:T(8,128)(2,1)S(1)} all-to-all(bf16[8,256,128]{2,1,0:T(8,128)(2,1)S(1)} %norm_conv.3), channel_id=1, replica_groups=mesh['tm'=32,'chan'=8] {'chan'}, dimensions={0} | all-to-all | bytes 1048576 | tf_op jit(solution)/shard_map/all_to_all | solution.py:270
  70.3 0.8 %last.1 = f32[64,2,256]{2,1,0:T(2,128)} custom-call(bf16[8,256,128]{2,1,0:T(8,128)(2,1)S(1)} %all_to_all.21.parts_ref, f32[8,128]{1,0:T(8,128)S(1)} %get-tuple-element.13.params_ref, bf16[256,128]{1,0:T(8,128)(2,1)S(1)} %get-tuple-element.12.after_ref.own_ref.packed_ref), custom_call_target="tpu_custom_call" | custom-call | tf_op jit(solution)/shard_map/last/pallas_call | solution.py:320
Async XLA Ops:
  2.0 22.7 %all-to-all-start = ((f32[32,4,128]{2,1,0:T(4,128)}), f32[32,4,128]{2,1,0:T(4,128)S(1)}, u32[]{:S(2)}, u32[]{:S(2)}) async-start(f32[32,4,128]{2,1,0:T(4,128)} %get-tuple-element.11), calls=%async_computation | async-start | bytes 131072 | tf_op jit(solution)/shard_map/all_to_all | solution.py:291
  14.8 4.1 %collective-permute-start = (bf16[256,128]{1,0:T(8,128)(2,1)S(1)}, bf16[256,128]{1,0:T(8,128)(2,1)S(1)}, u32[]{:S(2)}, u32[]{:S(2)}) collective-permute-start(bf16[256,128]{1,0:T(8,128)(2,1)S(1)} %get-tuple-element.12.after_ref.own_ref.packed_ref), channel_id=1, source_target_pairs={{0,8},{8,16},{16,24},{24,32},{32,40},{40,48},{48,56},{56,64},{64,7... | collective-permute-start | bytes 196616 | tf_op jit(solution)/shard_map/ppermute | solution.py:36
  41.0 15.9 %all-to-all-start.2 = ((f32[32,4,128]{2,1,0:T(4,128)}), f32[32,4,128]{2,1,0:T(4,128)S(1)}, u32[]{:S(2)}, u32[]{:S(2)}) async-start(f32[32,4,128]{2,1,0:T(4,128)} %get-tuple-element.15), calls=%async_computation.2 | async-start | bytes 131072 | tf_op jit(solution)/shard_map/all_to_all | solution.py:317
  46.9 3.2 %collective-permute-start.1 = (bf16[256,128]{1,0:T(8,128)(2,1)S(1)}, bf16[256,128]{1,0:T(8,128)(2,1)S(1)}, u32[]{:S(2)}, u32[]{:S(2)}) collective-permute-start(bf16[256,128]{1,0:T(8,128)(2,1)S(1)} %get-tuple-element.16.after_ref.own_ref), channel_id=1, source_target_pairs={{0,8},{8,16},{16,24},{24,32},{32,40},{40,48},{48,56},{56,64},{64,7... | collective-permute-start | bytes 196616 | tf_op jit(solution)/shard_map/ppermute | solution.py:36

commit v9 on v8

--- a/solution.py
+++ b/solution.py
@@ -68,16 +68,6 @@
     return jnp.concatenate([row, row], axis=1)
 
 
-def pack_kernel(x_hbm, packed_ref, sums_ref, x_ref, sem):
-    load = pltpu.make_async_copy(x_hbm, x_ref, sem)
-    load.start()
-    load.wait()
-    rows = jnp.concatenate([x_ref[:, 0, :], x_ref[:, 1, :]], axis=0).astype(jnp.float32)
-    values = rows.T
-    packed_ref[...] = values.astype(jnp.bfloat16)
-    write_sums(values, sums_ref)
-
-
 def clip_bounds(lengths_ref, frame):
     total = jnp.int32(0)
     start = jnp.int32(0)
@@ -91,15 +81,16 @@
     return start, end
 
 
-def prepare_kernel(
-    lengths_hbm, after_ref, gamma_one_hbm, beta_one_hbm, bias_one_hbm, gamma_two_hbm, beta_two_hbm,
-    bias_two_hbm, params_ref, clips_ref, lengths_ref, rows_ref, sems,
+def pack_kernel(
+    x_hbm, lengths_hbm, gamma_one_hbm, beta_one_hbm, bias_one_hbm, gamma_two_hbm, beta_two_hbm,
+    bias_two_hbm, packed_ref, sums_ref, params_ref, clips_ref, x_ref, lengths_ref, rows_ref, sems,
 ):
-    del after_ref
     affine = (gamma_one_hbm, beta_one_hbm, bias_one_hbm, gamma_two_hbm, beta_two_hbm, bias_two_hbm)
+    large = pltpu.make_async_copy(x_hbm, x_ref, sems.at[len(affine) + 1])
     loads = [pltpu.make_async_copy(lengths_hbm, lengths_ref, sems.at[len(affine)])]
     for k, ref in enumerate(affine):
         loads.append(pltpu.make_async_copy(ref, rows_ref.at[k], sems.at[k]))
+    large.start()
     for load in loads:
         load.start()
     for load in loads:
@@ -112,6 +103,11 @@
     start_one, end_one = clip_bounds(lengths_ref, frame + 1)
     for k, number in enumerate((start_zero, end_zero, start_one, end_one, frame, frame, frame, frame)):
         clips_ref[k : k + 1, :] = jnp.full((1, LANES), number, jnp.int32)
+    large.wait()
+    x = x_ref[...].astype(jnp.float32)
+    values = jnp.concatenate([x[:, 0, :], x[:, 1, :]], axis=0).T
+    packed_ref[...] = values.astype(jnp.bfloat16)
+    write_sums(values, sums_ref)
 
 
 def fetch_kernel(weight_hbm, after_ref, weight_ref, sem):
@@ -278,32 +274,28 @@
     sums_shape = shape_of((count, 4, LANES), jnp.float32)
     flat_one = in_hbm(jnp.transpose(w_one, (1, 0, 2)).reshape(ROWS, C))
     flat_two = in_hbm(jnp.transpose(w_two, (1, 0, 2)).reshape(ROWS, C))
-    packed, sums = pl.pallas_call(
+    affine = (gamma_one, beta_one, bias_one, gamma_two, beta_two, bias_two)
+    packed, sums, params, clips = pl.pallas_call(
         pack_kernel,
-        out_shape=(packed_shape, sums_shape),
-        in_specs=[HBM],
-        out_specs=(VMEM, VMEM),
-        scratch_shapes=[pltpu.VMEM((CHANS, 2, CELLS), jnp.bfloat16), pltpu.SemaphoreType.DMA],
+        out_shape=(
+            packed_shape,
+            sums_shape,
+            shape_of((8, LANES), jnp.float32),
+            shape_of((8, LANES), jnp.int32),
+        ),
+        in_specs=[HBM] * (2 + len(affine)),
+        out_specs=(VMEM, VMEM, VMEM, VMEM),
+        scratch_shapes=[
+            pltpu.VMEM((CHANS, 2, CELLS), jnp.bfloat16),
+            pltpu.SMEM(lengths.shape, jnp.int32),
+            pltpu.VMEM((len(affine), 1, CHANS), jnp.float32),
+            pltpu.SemaphoreType.DMA((len(affine) + 2,)),
+        ],
         compiler_params=SMALL,
         name="pack",
-    )(in_hbm(clip_input))
+    )(in_hbm(clip_input), in_hbm(lengths), *[in_hbm(row.reshape(1, CHANS)) for row in affine])
     tail = ring_shift(packed, "tm", 1)
     everyone = lax.all_to_all(sums, "tm", 0, 0, tiled=True)
-    affine = (gamma_one, beta_one, bias_one, gamma_two, beta_two, bias_two)
-    params, clips = pl.pallas_call(
-        prepare_kernel,
-        out_shape=(shape_of((8, LANES), jnp.float32), shape_of((8, LANES), jnp.int32)),
-        in_specs=[HBM, VMEM] + [HBM] * len(affine),
-        out_specs=(VMEM, VMEM),
-        scratch_shapes=[
-            pltpu.SMEM(lengths.shape, jnp.int32),
-            pltpu.VMEM((len(affine), 1, CHANS), jnp.float32),
-            pltpu.SemaphoreType.DMA((len(affine) + 1,)),
-        ],
-        compiler_params=SMALL,
-        cost_estimate=pl.CostEstimate(flops=10000, bytes_accessed=1 << 20, transcendentals=0),
-        name="prepare",
-    )(in_hbm(lengths), packed, *[in_hbm(row.reshape(1, CHANS)) for row in affine])
     parts = normed_conv(0, tail, packed, everyone, params, clips, fetch(flat_one, packed))
     y_one, sums = pl.pallas_call(
         middle_kernel,

time: 71.5 us -> 71.5 us (level)
  Pallas kernels: 11.3 us -> 10.4 us
  waiting for transfers between devices: 12.5 us -> 13.4 us
    all_to_all x2, waiting for transfers between devices: 12.5 us -> 13.4 us  [on_device(): everyone = lax.all_to_all(sums, 'tm', 0, 0, tiled=True)]
    pallas_call x2 -> x1, Pallas kernels: 2.89 us -> 2.03 us  [on_device(): pl.pallas_call(pack_kernel, out_shape=(packed_shape, sums_shape, shape_of...]
  transfers between devices with their start and end apart: 4 -> 4, of which waited for: 2 -> 2; matrix products, arithmetic and copies ran while one was open for 0% -> 0% of each run, Pallas kernels for 5% -> 4%
where the time goes in v9:
time: 71.5 us; the launch traced here: 71.1 us
  blocking collectives  25.1 us (35%)
  starting transfers between devices  22.1 us (31%)
  waiting for transfers between devices  13.4 us (19%)
  Pallas kernels  10.4 us (15%)
    all_to_all x2, blocking collectives, normed_conv(): return lax.all_to_all(partial, 'chan', 0, 0, tiled=True)  25.1 us
    all_to_all x2, starting transfers between devices, on_device(): everyone = lax.all_to_all(sums, 'tm', 0, 0, tiled=True)  18.7 us
    all_to_all x2, waiting for transfers between devices, on_device(): everyone = lax.all_to_all(sums, 'tm', 0, 0, tiled=True)  13.4 us
    pallas_call x2, Pallas kernels, normed_conv(): pl.pallas_call(functools.partial(conv_kernel, at), out_shape=shape_of((pa...  3.57 us
    ppermute x2, starting transfers between devices, ring_shift(): lax.ppermute(value, axis, [(source, (source + steps) % count) for source...  3.42 us
    pallas_call x2, Pallas kernels, fetch(): pl.pallas_call(fetch_kernel, out_shape=shape_of((ROWS, C), jnp.bfloat16),...  2.97 us
    pallas_call x1, Pallas kernels, on_device(): pl.pallas_call(pack_kernel, out_shape=(packed_shape, sums_shape, shape_of...  2.03 us
  transfers between devices with their start and end apart: 4, of which 2 were waited for; matrix products, arithmetic and copies ran while one was open for 0% of the time, Pallas kernels for 4%

profile of v9, /device:TPU:1, one launch (start us, length us, event | category | flops | bytes accessed | tf_op | source)
XLA Modules:
  0.0 71.1 jit_solution(10448572404638832412)
XLA Ops:
  0.0 2.0 %pack.1 = (bf16[256,128]{1,0:T(8,128)(2,1)S(1)}, f32[32,4,128]{2,1,0:T(4,128)}, f32[8,128]{1,0:T(8,128)S(1)}, s32[8,128]{1,0:T(8,128)S(1)}) custom-call(bf16[64,2,256]{2,1,0:T(2,128)(2,1)} %x_hbm.1, s32[16]{0:T(128)} %lengths_hbm.1, f32[1,64]{1,0:T(1,128)} %bitcast.14, f32[1,64]{1,0:T(1,128)} %bitcast.15, f32[1,64]{1,0:T(1,128)} %bitcast.16, ...), custom_call_target="tpu_custom_call" | custom-call | tf_op jit(solution)/shard_map/pack/pallas_call | solution.py:278
  2.0 12.8 %all-to-all-start = ((f32[32,4,128]{2,1,0:T(4,128)}), f32[32,4,128]{2,1,0:T(4,128)S(1)}, u32[]{:S(2)}, u32[]{:S(2)}) async-start(f32[32,4,128]{2,1,0:T(4,128)} %get-tuple-element.11), calls=%async_computation | async-start | bytes 131072 | tf_op jit(solution)/shard_map/all_to_all | solution.py:298
  14.8 1.7 %collective-permute-start = (bf16[256,128]{1,0:T(8,128)(2,1)S(1)}, bf16[256,128]{1,0:T(8,128)(2,1)S(1)}, u32[]{:S(2)}, u32[]{:S(2)}) collective-permute-start(bf16[256,128]{1,0:T(8,128)(2,1)S(1)} %get-tuple-element.12.after_ref.own_ref.packed_ref), channel_id=1, source_target_pairs={{0,8},{8,16},{16,24},{24,32},{32,40},{40,48},{48,56},{56,64},{64,7... | collective-permute-start | bytes 196616 | tf_op jit(solution)/shard_map/ppermute | solution.py:36
  16.5 1.5 %fetch.2.w_ref = bf16[1728,512]{1,0:T(8,128)(2,1)S(1)} custom-call(bf16[1728,512]{1,0:T(8,128)(2,1)} %bitcast.12, bf16[256,128]{1,0:T(8,128)(2,1)S(1)} %get-tuple-element.12.after_ref.own_ref.packed_ref), custom_call_target="tpu_custom_call" | custom-call | flops 10000 | bytes 2097152 | tf_op jit(solution)/shard_map/fetch/pallas_call | solution.py:237
  18.0 0.0 collective-permute-done.tail_ref
  18.0 6.7 %all-to-all-done.sums_ref = f32[32,4,128]{2,1,0:T(4,128)S(1)} async-done(((f32[32,4,128]{2,1,0:T(4,128)}), f32[32,4,128]{2,1,0:T(4,128)S(1)}, u32[]{:S(2)}, u32[]{:S(2)}) %all-to-all-start) | async-done | bytes 65568 | tf_op jit(solution)/shard_map/all_to_all | solution.py:298
  24.8 1.8 %norm_conv.2 = bf16[8,256,128]{2,1,0:T(8,128)(2,1)S(1)} custom-call(f32[32,4,128]{2,1,0:T(4,128)S(1)} %all-to-all-done.sums_ref, bf16[256,128]{1,0:T(8,128)(2,1)S(1)} %get-tuple-element.12.after_ref.own_ref.packed_ref, bf16[256,128]{1,0:T(8,128)(2,1)S(1)} %collective-permute-done.tail_ref, f32[8,128]{1,0:T(8,128)S(1)} %get-tuple-element.13.params_ref, ...), custom_call_target="tpu_custom_call" | custom-call | flops 905969664 | bytes 3145728 | tf_op jit(solution)/shard_map/norm_conv/pallas_call | solution.py:251
  26.5 13.4 %all_to_all.20.parts_ref = bf16[8,256,128]{2,1,0:T(8,128)(2,1)S(1)} all-to-all(bf16[8,256,128]{2,1,0:T(8,128)(2,1)S(1)} %norm_conv.2), channel_id=1, replica_groups=mesh['tm'=32,'chan'=8] {'chan'}, dimensions={0} | all-to-all | bytes 1048576 | tf_op jit(solution)/shard_map/all_to_all | solution.py:266
  39.9 1.0 %middle.1 = (bf16[256,128]{1,0:T(8,128)(2,1)S(1)}, f32[32,4,128]{2,1,0:T(4,128)}) custom-call(bf16[8,256,128]{2,1,0:T(8,128)(2,1)S(1)} %all_to_all.20.parts_ref, f32[8,128]{1,0:T(8,128)S(1)} %get-tuple-element.13.params_ref), custom_call_target="tpu_custom_call" | custom-call | tf_op jit(solution)/shard_map/middle/pallas_call | solution.py:300
  41.0 6.0 %all-to-all-start.2 = ((f32[32,4,128]{2,1,0:T(4,128)}), f32[32,4,128]{2,1,0:T(4,128)S(1)}, u32[]{:S(2)}, u32[]{:S(2)}) async-start(f32[32,4,128]{2,1,0:T(4,128)} %get-tuple-element.15), calls=%async_computation.2 | async-start | bytes 131072 | tf_op jit(solution)/shard_map/all_to_all | solution.py:309
  47.0 1.7 %collective-permute-start.1 = (bf16[256,128]{1,0:T(8,128)(2,1)S(1)}, bf16[256,128]{1,0:T(8,128)(2,1)S(1)}, u32[]{:S(2)}, u32[]{:S(2)}) collective-permute-start(bf16[256,128]{1,0:T(8,128)(2,1)S(1)} %get-tuple-element.16.after_ref.own_ref), channel_id=1, source_target_pairs={{0,8},{8,16},{16,24},{24,32},{32,40},{40,48},{48,56},{56,64},{64,7... | collective-permute-start | bytes 196616 | tf_op jit(solution)/shard_map/ppermute | solution.py:36
  48.7 1.5 %fetch.3.w_ref = bf16[1728,512]{1,0:T(8,128)(2,1)S(1)} custom-call(bf16[1728,512]{1,0:T(8,128)(2,1)} %bitcast.13, bf16[256,128]{1,0:T(8,128)(2,1)S(1)} %get-tuple-element.16.after_ref.own_ref), custom_call_target="tpu_custom_call" | custom-call | flops 10000 | bytes 2097152 | tf_op jit(solution)/shard_map/fetch/pallas_call | solution.py:237
  50.2 0.0 collective-permute-done.1.tail_ref
  50.2 6.7 %all-to-all-done.2.sums_ref = f32[32,4,128]{2,1,0:T(4,128)S(1)} async-done(((f32[32,4,128]{2,1,0:T(4,128)}), f32[32,4,128]{2,1,0:T(4,128)S(1)}, u32[]{:S(2)}, u32[]{:S(2)}) %all-to-all-start.2) | async-done | bytes 65568 | tf_op jit(solution)/shard_map/all_to_all | solution.py:309
  56.8 1.8 %norm_conv.3 = bf16[8,256,128]{2,1,0:T(8,128)(2,1)S(1)} custom-call(f32[32,4,128]{2,1,0:T(4,128)S(1)} %all-to-all-done.2.sums_ref, bf16[256,128]{1,0:T(8,128)(2,1)S(1)} %get-tuple-element.16.after_ref.own_ref, bf16[256,128]{1,0:T(8,128)(2,1)S(1)} %collective-permute-done.1.tail_ref, f32[8,128]{1,0:T(8,128)S(1)} %get-tuple-element.13.params_ref, ...), custom_call_target="tpu_custom_call" | custom-call | flops 905969664 | bytes 3145728 | tf_op jit(solution)/shard_map/norm_conv/pallas_call | solution.py:251
  58.6 11.7 %all_to_all.21.parts_ref = bf16[8,256,128]{2,1,0:T(8,128)(2,1)S(1)} all-to-all(bf16[8,256,128]{2,1,0:T(8,128)(2,1)S(1)} %norm_conv.3), channel_id=1, replica_groups=mesh['tm'=32,'chan'=8] {'chan'}, dimensions={0} | all-to-all | bytes 1048576 | tf_op jit(solution)/shard_map/all_to_all | solution.py:266
  70.3 0.8 %last.1 = f32[64,2,256]{2,1,0:T(2,128)} custom-call(bf16[8,256,128]{2,1,0:T(8,128)(2,1)S(1)} %all_to_all.21.parts_ref, f32[8,128]{1,0:T(8,128)S(1)} %get-tuple-element.13.params_ref, bf16[256,128]{1,0:T(8,128)(2,1)S(1)} %get-tuple-element.12.after_ref.own_ref.packed_ref), custom_call_target="tpu_custom_call" | custom-call | tf_op jit(solution)/shard_map/last/pallas_call | solution.py:312
Async XLA Ops:
  2.0 22.7 %all-to-all-start = ((f32[32,4,128]{2,1,0:T(4,128)}), f32[32,4,128]{2,1,0:T(4,128)S(1)}, u32[]{:S(2)}, u32[]{:S(2)}) async-start(f32[32,4,128]{2,1,0:T(4,128)} %get-tuple-element.11), calls=%async_computation | async-start | bytes 131072 | tf_op jit(solution)/shard_map/all_to_all | solution.py:298
  14.8 3.2 %collective-permute-start = (bf16[256,128]{1,0:T(8,128)(2,1)S(1)}, bf16[256,128]{1,0:T(8,128)(2,1)S(1)}, u32[]{:S(2)}, u32[]{:S(2)}) collective-permute-start(bf16[256,128]{1,0:T(8,128)(2,1)S(1)} %get-tuple-element.12.after_ref.own_ref.packed_ref), channel_id=1, source_target_pairs={{0,8},{8,16},{16,24},{24,32},{32,40},{40,48},{48,56},{56,64},{64,7... | collective-permute-start | bytes 196616 | tf_op jit(solution)/shard_map/ppermute | solution.py:36
  41.0 15.8 %all-to-all-start.2 = ((f32[32,4,128]{2,1,0:T(4,128)}), f32[32,4,128]{2,1,0:T(4,128)S(1)}, u32[]{:S(2)}, u32[]{:S(2)}) async-start(f32[32,4,128]{2,1,0:T(4,128)} %get-tuple-element.15), calls=%async_computation.2 | async-start | bytes 131072 | tf_op jit(solution)/shard_map/all_to_all | solution.py:309
  47.0 3.2 %collective-permute-start.1 = (bf16[256,128]{1,0:T(8,128)(2,1)S(1)}, bf16[256,128]{1,0:T(8,128)(2,1)S(1)}, u32[]{:S(2)}, u32[]{:S(2)}) collective-permute-start(bf16[256,128]{1,0:T(8,128)(2,1)S(1)} %get-tuple-element.16.after_ref.own_ref), channel_id=1, source_target_pairs={{0,8},{8,16},{16,24},{24,32},{32,40},{40,48},{48,56},{56,64},{64,7... | collective-permute-start | bytes 196616 | tf_op jit(solution)/shard_map/ppermute | solution.py:36

commit v10 on v8

--- a/solution.py
+++ b/solution.py
@@ -33,7 +33,7 @@
 
 def ring_shift(value, axis, steps):
     count = lax.axis_size(axis)
-    return lax.ppermute(value, axis, [(source, (source + steps) % count) for source in range(count)])
+    return lax.ppermute(value, axis, [(source, source + steps) for source in range(count - steps)])
 
 
 def left_half(shape):

time: 71.5 us -> 73.4 us (1.027)
  starting transfers between devices: 22.2 us -> 27.6 us
  waiting for transfers between devices: 12.5 us -> 8.84 us
    all_to_all x2, waiting for transfers between devices: 12.5 us -> 8.84 us  [on_device(): everyone = lax.all_to_all(sums, 'tm', 0, 0, tiled=True)]
    ppermute x2, starting transfers between devices: 3.42 us -> 7.08 us  [ring_shift(): lax.ppermute(value, axis, [(source, source + steps) for source in range(c...]
    all_to_all x2, starting transfers between devices: 18.7 us -> 20.5 us  [on_device(): everyone = lax.all_to_all(sums, 'tm', 0, 0, tiled=True)]
where the time goes in v10:
time: 73.4 us; the launch traced here: 73 us
  starting transfers between devices  27.6 us (38%)
  blocking collectives  25.1 us (34%)
  Pallas kernels  11.3 us (15%)
  waiting for transfers between devices  8.84 us (12%)
    all_to_all x2, blocking collectives, normed_conv(): return lax.all_to_all(partial, 'chan', 0, 0, tiled=True)  25.1 us
    all_to_all x2, starting transfers between devices, on_device(): everyone = lax.all_to_all(sums, 'tm', 0, 0, tiled=True)  20.5 us
    all_to_all x2, waiting for transfers between devices, on_device(): everyone = lax.all_to_all(sums, 'tm', 0, 0, tiled=True)  8.84 us
    ppermute x2, starting transfers between devices, ring_shift(): lax.ppermute(value, axis, [(source, source + steps) for source in range(c...  7.08 us
    pallas_call x2, Pallas kernels, normed_conv(): pl.pallas_call(functools.partial(conv_kernel, at), out_shape=shape_of((pa...  3.57 us
    pallas_call x2, Pallas kernels, fetch(): pl.pallas_call(fetch_kernel, out_shape=shape_of((ROWS, C), jnp.bfloat16),...  2.98 us
    pallas_call x1, Pallas kernels, on_device(): pl.pallas_call(pack_kernel, out_shape=(packed_shape, sums_shape), in_spec...  2.01 us
  transfers between devices with their start and end apart: 4, of which 2 were waited for; matrix products, arithmetic and copies ran while one was open for 0% of the time, Pallas kernels for 5%

profile of v10, /device:TPU:1, one launch (start us, length us, event | category | flops | bytes accessed | tf_op | source)
XLA Modules:
  0.0 73.0 jit_solution(9202278164338898106)
XLA Ops:
  0.0 2.0 %pack.1 = (bf16[256,128]{1,0:T(8,128)(2,1)S(1)}, f32[32,4,128]{2,1,0:T(4,128)}) custom-call(bf16[64,2,256]{2,1,0:T(2,128)(2,1)} %x_hbm.1), custom_call_target="tpu_custom_call" | custom-call | tf_op jit(solution)/shard_map/pack/pallas_call | solution.py:281
  2.0 12.8 %all-to-all-start = ((f32[32,4,128]{2,1,0:T(4,128)}), f32[32,4,128]{2,1,0:T(4,128)S(1)}, u32[]{:S(2)}, u32[]{:S(2)}) async-start(f32[32,4,128]{2,1,0:T(4,128)} %get-tuple-element.11), calls=%async_computation | async-start | bytes 131072 | tf_op jit(solution)/shard_map/all_to_all | solution.py:291
  14.8 3.5 %collective-permute-start = (bf16[256,128]{1,0:T(8,128)(2,1)S(1)}, bf16[256,128]{1,0:T(8,128)(2,1)S(1)}, u32[]{:S(2)}, u32[]{:S(2)}) collective-permute-start(bf16[256,128]{1,0:T(8,128)(2,1)S(1)} %get-tuple-element.12.after_ref.own_ref.packed_ref), channel_id=1, source_target_pairs={{0,8},{8,16},{16,24},{24,32},{32,40},{40,48},{48,56},{56,64},{64,7... | collective-permute-start | bytes 196616 | tf_op jit(solution)/shard_map/ppermute | solution.py:36
  18.3 1.5 %fetch.2.w_ref = bf16[1728,512]{1,0:T(8,128)(2,1)S(1)} custom-call(bf16[1728,512]{1,0:T(8,128)(2,1)} %bitcast.12, bf16[256,128]{1,0:T(8,128)(2,1)S(1)} %get-tuple-element.12.after_ref.own_ref.packed_ref), custom_call_target="tpu_custom_call" | custom-call | flops 10000 | bytes 2097152 | tf_op jit(solution)/shard_map/fetch/pallas_call | solution.py:241
  19.8 0.9 %prepare.1 = (f32[8,128]{1,0:T(8,128)S(1)}, s32[8,128]{1,0:T(8,128)S(1)}) custom-call(s32[16]{0:T(128)} %lengths_hbm.1, bf16[256,128]{1,0:T(8,128)(2,1)S(1)} %get-tuple-element.12.after_ref.own_ref.packed_ref, f32[1,64]{1,0:T(1,128)} %bitcast.14, f32[1,64]{1,0:T(1,128)} %bitcast.15, f32[1,64]{1,0:T(1,128)} %bitcast.16, f32[1,64]{1,0:T(1,128)} %bitcast.17, ...), custom_call_target="tpu_custom_call" | custom-call | flops 10000 | bytes 1048576 | tf_op jit(solution)/shard_map/prepare/pallas_call | solution.py:293
  20.7 0.0 collective-permute-done.tail_ref
  20.7 4.0 %all-to-all-done.sums_ref = f32[32,4,128]{2,1,0:T(4,128)S(1)} async-done(((f32[32,4,128]{2,1,0:T(4,128)}), f32[32,4,128]{2,1,0:T(4,128)S(1)}, u32[]{:S(2)}, u32[]{:S(2)}) %all-to-all-start) | async-done | bytes 65568 | tf_op jit(solution)/shard_map/all_to_all | solution.py:291
  24.7 1.8 %norm_conv.2 = bf16[8,256,128]{2,1,0:T(8,128)(2,1)S(1)} custom-call(f32[32,4,128]{2,1,0:T(4,128)S(1)} %all-to-all-done.sums_ref, bf16[256,128]{1,0:T(8,128)(2,1)S(1)} %get-tuple-element.12.after_ref.own_ref.packed_ref, bf16[256,128]{1,0:T(8,128)(2,1)S(1)} %collective-permute-done.tail_ref, f32[8,128]{1,0:T(8,128)S(1)} %get-tuple-element.13.params_ref, ...), custom_call_target="tpu_custom_call" | custom-call | flops 905969664 | bytes 3145728 | tf_op jit(solution)/shard_map/norm_conv/pallas_call | solution.py:255
  26.5 13.4 %all_to_all.20.parts_ref = bf16[8,256,128]{2,1,0:T(8,128)(2,1)S(1)} all-to-all(bf16[8,256,128]{2,1,0:T(8,128)(2,1)S(1)} %norm_conv.2), channel_id=1, replica_groups=mesh['tm'=32,'chan'=8] {'chan'}, dimensions={0} | all-to-all | bytes 1048576 | tf_op jit(solution)/shard_map/all_to_all | solution.py:270
  39.9 1.0 %middle.1 = (bf16[256,128]{1,0:T(8,128)(2,1)S(1)}, f32[32,4,128]{2,1,0:T(4,128)}) custom-call(bf16[8,256,128]{2,1,0:T(8,128)(2,1)S(1)} %all_to_all.20.parts_ref, f32[8,128]{1,0:T(8,128)S(1)} %get-tuple-element.13.params_ref), custom_call_target="tpu_custom_call" | custom-call | tf_op jit(solution)/shard_map/middle/pallas_call | solution.py:308
  41.0 7.8 %all-to-all-start.2 = ((f32[32,4,128]{2,1,0:T(4,128)}), f32[32,4,128]{2,1,0:T(4,128)S(1)}, u32[]{:S(2)}, u32[]{:S(2)}) async-start(f32[32,4,128]{2,1,0:T(4,128)} %get-tuple-element.15), calls=%async_computation.2 | async-start | bytes 131072 | tf_op jit(solution)/shard_map/all_to_all | solution.py:317
  48.7 3.5 %collective-permute-start.1 = (bf16[256,128]{1,0:T(8,128)(2,1)S(1)}, bf16[256,128]{1,0:T(8,128)(2,1)S(1)}, u32[]{:S(2)}, u32[]{:S(2)}) collective-permute-start(bf16[256,128]{1,0:T(8,128)(2,1)S(1)} %get-tuple-element.16.after_ref.own_ref), channel_id=1, source_target_pairs={{0,8},{8,16},{16,24},{24,32},{32,40},{40,48},{48,56},{56,64},{64,7... | collective-permute-start | bytes 196616 | tf_op jit(solution)/shard_map/ppermute | solution.py:36
  52.3 1.5 %fetch.3.w_ref = bf16[1728,512]{1,0:T(8,128)(2,1)S(1)} custom-call(bf16[1728,512]{1,0:T(8,128)(2,1)} %bitcast.13, bf16[256,128]{1,0:T(8,128)(2,1)S(1)} %get-tuple-element.16.after_ref.own_ref), custom_call_target="tpu_custom_call" | custom-call | flops 10000 | bytes 2097152 | tf_op jit(solution)/shard_map/fetch/pallas_call | solution.py:241
  53.8 0.0 collective-permute-done.1.tail_ref
  53.8 4.8 %all-to-all-done.2.sums_ref = f32[32,4,128]{2,1,0:T(4,128)S(1)} async-done(((f32[32,4,128]{2,1,0:T(4,128)}), f32[32,4,128]{2,1,0:T(4,128)S(1)}, u32[]{:S(2)}, u32[]{:S(2)}) %all-to-all-start.2) | async-done | bytes 65568 | tf_op jit(solution)/shard_map/all_to_all | solution.py:317
  58.6 1.8 %norm_conv.3 = bf16[8,256,128]{2,1,0:T(8,128)(2,1)S(1)} custom-call(f32[32,4,128]{2,1,0:T(4,128)S(1)} %all-to-all-done.2.sums_ref, bf16[256,128]{1,0:T(8,128)(2,1)S(1)} %get-tuple-element.16.after_ref.own_ref, bf16[256,128]{1,0:T(8,128)(2,1)S(1)} %collective-permute-done.1.tail_ref, f32[8,128]{1,0:T(8,128)S(1)} %get-tuple-element.13.params_ref, ...), custom_call_target="tpu_custom_call" | custom-call | flops 905969664 | bytes 3145728 | tf_op jit(solution)/shard_map/norm_conv/pallas_call | solution.py:255
  60.4 11.7 %all_to_all.21.parts_ref = bf16[8,256,128]{2,1,0:T(8,128)(2,1)S(1)} all-to-all(bf16[8,256,128]{2,1,0:T(8,128)(2,1)S(1)} %norm_conv.3), channel_id=1, replica_groups=mesh['tm'=32,'chan'=8] {'chan'}, dimensions={0} | all-to-all | bytes 1048576 | tf_op jit(solution)/shard_map/all_to_all | solution.py:270
  72.2 0.8 %last.1 = f32[64,2,256]{2,1,0:T(2,128)} custom-call(bf16[8,256,128]{2,1,0:T(8,128)(2,1)S(1)} %all_to_all.21.parts_ref, f32[8,128]{1,0:T(8,128)S(1)} %get-tuple-element.13.params_ref, bf16[256,128]{1,0:T(8,128)(2,1)S(1)} %get-tuple-element.12.after_ref.own_ref.packed_ref), custom_call_target="tpu_custom_call" | custom-call | tf_op jit(solution)/shard_map/last/pallas_call | solution.py:320
Async XLA Ops:
  2.0 22.7 %all-to-all-start = ((f32[32,4,128]{2,1,0:T(4,128)}), f32[32,4,128]{2,1,0:T(4,128)S(1)}, u32[]{:S(2)}, u32[]{:S(2)}) async-start(f32[32,4,128]{2,1,0:T(4,128)} %get-tuple-element.11), calls=%async_computation | async-start | bytes 131072 | tf_op jit(solution)/shard_map/all_to_all | solution.py:291
  14.8 5.9 %collective-permute-start = (bf16[256,128]{1,0:T(8,128)(2,1)S(1)}, bf16[256,128]{1,0:T(8,128)(2,1)S(1)}, u32[]{:S(2)}, u32[]{:S(2)}) collective-permute-start(bf16[256,128]{1,0:T(8,128)(2,1)S(1)} %get-tuple-element.12.after_ref.own_ref.packed_ref), channel_id=1, source_target_pairs={{0,8},{8,16},{16,24},{24,32},{32,40},{40,48},{48,56},{56,64},{64,7... | collective-permute-start | bytes 196616 | tf_op jit(solution)/shard_map/ppermute | solution.py:36
  41.0 17.7 %all-to-all-start.2 = ((f32[32,4,128]{2,1,0:T(4,128)}), f32[32,4,128]{2,1,0:T(4,128)S(1)}, u32[]{:S(2)}, u32[]{:S(2)}) async-start(f32[32,4,128]{2,1,0:T(4,128)} %get-tuple-element.15), calls=%async_computation.2 | async-start | bytes 131072 | tf_op jit(solution)/shard_map/all_to_all | solution.py:317
  48.7 5.0 %collective-permute-start.1 = (bf16[256,128]{1,0:T(8,128)(2,1)S(1)}, bf16[256,128]{1,0:T(8,128)(2,1)S(1)}, u32[]{:S(2)}, u32[]{:S(2)}) collective-permute-start(bf16[256,128]{1,0:T(8,128)(2,1)S(1)} %get-tuple-element.16.after_ref.own_ref), channel_id=1, source_target_pairs={{0,8},{8,16},{16,24},{24,32},{32,40},{40,48},{48,56},{56,64},{64,7... | collective-permute-start | bytes 196616 | tf_op jit(solution)/shard_map/ppermute | solution.py:36
